TPU v7x, 32 devices: a whole 2x2x4 slice. The times are simulated.
32 devices in a mesh: row: 8 (over z, core), col: 4 (over y, x).
Axes of the slice: x: 2, y: 2, z: 4, core: 2. Of those that a mesh axis runs over, the one named last changes fastest.
Arguments:
- start_block: bfloat16 [16, 4096], P(None, 'col'), may hold values from -33 to 33
- block_values: bfloat16 [8, 4, 12, 128, 128], P('row', 'col'), may hold values from -0.109375 to 0.109375
- block_columns: int32 [8, 4, 12], P('row', 'col'), may hold values from 0 to 7
- block_counts: int32 [8, 4, 4], P('row', 'col'), may hold values from 1 to 6, 12 in all within a row
Outputs:
- applied_once: bfloat16 [16, 4096], P(None, 'row')
- applied_twice: bfloat16 [16, 4096], P(None, 'row')
- basis_gram: float32 [32, 32], replicated
- projected_gram: float32 [32, 32], replicated
All inputs are finite; a program needn't handle non-finite values.
Results may differ from a plain program's by a relative error of at most 0.0039.
Values may be sent and summed in bfloat16 or wider, within the bound.
No kernel may reach another device: no remote copies, remote signals or barrier semaphores. Data moves between devices by JAX's collectives and lax.ppermute only.
A program may use at most 64 MiB of HBM per device.

v0:
```python
import jax
import jax.numpy as jnp
from jax import lax
from jax.sharding import PartitionSpec as P

highest = lax.Precision.HIGHEST


def broadcast(block, axis, owner):
    block = jnp.where(lax.axis_index(axis) == owner, block, jnp.zeros_like(block))
    return lax.psum(block, axis)


def block_rows_of(counts, block_total):
    row_ends = jnp.cumsum(counts)
    positions = jnp.arange(block_total, dtype=jnp.int32)
    return jnp.sum((row_ends[None, :] <= positions[:, None]).astype(jnp.int32), axis=1)


def forward_tile(values, columns, block_row, source, row_blocks):
    vector_count = source.shape[0]
    block_size = values.shape[1]
    pieces = source.reshape(vector_count, -1, block_size)[:, columns, :]
    products = jnp.einsum("bij,kbj->kbi", values, pieces, preferred_element_type=jnp.float32)
    row_hot = (block_row[:, None] == jnp.arange(row_blocks, dtype=jnp.int32)[None, :]).astype(
        jnp.float32
    )
    summed = jnp.einsum("kbi,br->kri", products, row_hot, precision=highest)
    return summed.reshape(vector_count, row_blocks * block_size)


def transpose_tile(values, columns, block_row, source, col_blocks):
    vector_count = source.shape[0]
    block_size = values.shape[1]
    pieces = source.reshape(vector_count, -1, block_size)[:, block_row, :]
    products = jnp.einsum("bji,kbj->kbi", values, pieces, preferred_element_type=jnp.float32)
    col_hot = (columns[:, None] == jnp.arange(col_blocks, dtype=jnp.int32)[None, :]).astype(
        jnp.float32
    )
    summed = jnp.einsum("kbi,bc->kci", products, col_hot, precision=highest)
    return summed.reshape(vector_count, col_blocks * block_size)


def inner_products(left_block, right_block):
    return jnp.dot(left_block, right_block.T, precision=highest)


def local(start_block, block_values, block_columns, block_counts):
    values = block_values[0, 0]
    columns = block_columns[0, 0]
    counts = block_counts[0, 0]
    block_size = values.shape[1]
    row_blocks = counts.shape[0]
    row_width = row_blocks * block_size
    col_width = start_block.shape[1]
    col_blocks = col_width // block_size
    block_row = block_rows_of(counts, values.shape[0])
    row_slot = lax.axis_index("row")
    col_slot = lax.axis_index("col")
    slab_ratio = lax.axis_size("row") // lax.axis_size("col")
    owner_col = row_slot // slab_ratio
    offset = row_slot % slab_ratio * row_width
    on_owner = col_slot == owner_col
    piece_len = row_width // lax.axis_size("col")
    norm_scale = 1.0 / (row_width * lax.axis_size("row"))

    def piece_of(vectors):
        return lax.dynamic_slice_in_dim(vectors, col_slot * piece_len, piece_len, 1)

    def apply_operator(col_part, row_part):
        forward = forward_tile(values, columns, block_row, col_part, row_blocks)
        backward = transpose_tile(values, columns, block_row, row_part, col_blocks)
        column_total = lax.psum(backward, "row")
        owner_share = lax.dynamic_slice_in_dim(column_total, offset, row_width, 1)
        row_term = forward + jnp.where(on_owner, owner_share, 0.0)
        whole_slab = lax.psum(row_term, "col").astype(jnp.bfloat16)
        own_piece = piece_of(whole_slab)
        return (whole_slab, own_piece.astype(jnp.float32))

    root_slab = broadcast(start_block, "col", owner_col)
    start_rows = lax.dynamic_slice_in_dim(root_slab, offset, row_width, 1)
    applied_once, once_piece = apply_operator(start_block, start_rows)
    start_piece = piece_of(start_rows).astype(jnp.float32)
    slab_parts = []
    for turn_index in range(slab_ratio):
        slab_parts.append(broadcast(applied_once, "row", col_slot * slab_ratio + turn_index))
    once_columns = jnp.concatenate(slab_parts, axis=1)
    applied_twice, twice_piece = apply_operator(once_columns, applied_once)
    gram_xx, gram_xy, gram_yy, gram_yz = lax.psum(
        (
            inner_products(start_piece, start_piece),
            inner_products(start_piece, once_piece),
            inner_products(once_piece, once_piece),
            inner_products(once_piece, twice_piece),
        ),
        ("row", "col"),
    )
    basis_gram = (
        jnp.concatenate(
            [jnp.concatenate([gram_xx, gram_xy], 1), jnp.concatenate([gram_xy.T, gram_yy], 1)], 0
        )
        * norm_scale
    )
    projected_gram = (
        jnp.concatenate(
            [jnp.concatenate([gram_xy, gram_yy], 1), jnp.concatenate([gram_yy, gram_yz], 1)], 0
        )
        * norm_scale
    )
    return (applied_once, applied_twice, basis_gram, projected_gram)


def solution(mesh):
    return jax.shard_map(
        local,
        mesh=mesh,
        in_specs=(
            P(None, "col"),
            P("row", "col", None, None, None),
            P("row", "col", None),
            P("row", "col", None),
        ),
        out_specs=(P(None, "row"), P(None, "row"), P(), P()),
        check_vma=False,
    )
```

profile of v0, /device:TPU:0, one launch (start us, length us, event | category | flops | bytes accessed | tf_op | source)
XLA Modules:
  0.0 240.9 jit_solution(7945162154595536846)
XLA Ops:
  7.2 0.8 reduce-window.8
  8.2 17.8 %psum.77 = bf16[16,1024]{1,0:T(8,128)(2,1)S(1)} all-reduce(bf16[16,1024]{1,0:T(8,128)(2,1)S(1)} %broadcast_select_fusion), channel_id=1, replica_groups=mesh['row'=8,'col'=4] {'col'}, use_global_device_ids=true, to_apply=%region_2.3 | all-reduce | flops 16384 | bytes 65536 | tf_op jit(solution)/shard_map/psum | solution.py:11
  26.0 0.6 gather_fusion.1
  26.6 0.2 convolution_bitcast_fusion.2
  26.8 0.7 copy-done.4
  27.6 0.6 copy.57
  28.4 0.6 gather_fusion
  29.0 0.3 convolution_bitcast_fusion.3
  29.3 0.2 fusion.10
  29.7 51.8 %all-reduce.5.cloned.1.call-done = f32[16,1024]{1,0:T(8,128)} async-done(((f32[16,1024]{1,0:T(8,128)}), f32[16,1024]{1,0:T(8,128)}) %all-reduce.5.cloned.1.call-update) | async-done | bytes 65552 | tf_op jit(solution)/shard_map/psum | solution.py:73
  81.4 0.8 bitcast_add_fusion.1
  82.2 16.2 %psum.79 = bf16[16,512]{1,0:T(8,128)(2,1)S(1)} all-reduce(f32[16,512]{1,0:T(8,128)S(1)} %bitcast_add_fusion.1), channel_id=1, replica_groups=mesh['row'=8,'col'=4] {'col'}, use_global_device_ids=true, to_apply=%region_4.5 | all-reduce | flops 8192 | bytes 49152 | tf_op jit(solution)/shard_map/psum | solution.py:76
  98.6 26.0 %all-reduce.1 = (bf16[16,512]{1,0:T(8,128)(2,1)S(1)}, bf16[16,512]{1,0:T(8,128)(2,1)S(1)}) all-reduce(bf16[16,512]{1,0:T(8,128)(2,1)S(1)} %get-tuple-element.11, bf16[16,512]{1,0:T(8,128)(2,1)S(1)} %get-tuple-element.10), channel_id=1, replica_groups=mesh['row'=8,'col'=4] {'row'}, use_global_device_ids=true, to_apply=%region_6.7 | all-reduce | flops 16384 | bytes 65536 | tf_op jit(solution)/shard_map/psum | solution.py:11
  124.6 0.6 gather_fusion.2
  125.2 0.3 convolution_bitcast_fusion.1
  125.7 0.6 gather_fusion.3
  126.2 0.2 convolution_bitcast_fusion
  126.6 0.6 copy.56
  127.3 0.2 fusion.21
  127.5 49.9 %all-reduce.7.cloned.1.call-done = f32[16,1024]{1,0:T(8,128)} async-done(((f32[16,1024]{1,0:T(8,128)}), f32[16,1024]{1,0:T(8,128)}) %all-reduce.7.cloned.1.call-update) | async-done | bytes 65552 | tf_op jit(solution)/shard_map/psum | solution.py:73
  177.4 0.8 bitcast_add_fusion
  178.2 16.2 %psum.83 = bf16[16,512]{1,0:T(8,128)(2,1)S(1)} all-reduce(f32[16,512]{1,0:T(8,128)S(1)} %bitcast_add_fusion), channel_id=1, replica_groups=mesh['row'=8,'col'=4] {'col'}, use_global_device_ids=true, to_apply=%region_8.9 | all-reduce | flops 8192 | bytes 49152 | tf_op jit(solution)/shard_map/psum | solution.py:76
  194.5 38.7 %all-reduce = (f32[16,16]{1,0:T(8,128)S(1)}, f32[16,16]{1,0:T(8,128)S(1)}, f32[16,16]{1,0:T(8,128)S(1)}, f32[16,16]{1,0:T(8,128)S(1)}) all-reduce(f32[16,16]{1,0:T(8,128)S(1)} %fusion.26, f32[16,16]{1,0:T(8,128)S(1)} %fusion.21, f32[16,16]{1,0:T(8,128)S(1)} %fusion.23, ...), channel_id=1, replica_groups=mesh['row'=8,'col'=4] {'row','col'}, use_global_device_ids=true, to_apply=%region_11.12 | all-reduce | flops 1024 | bytes 8192 | tf_op jit(solution)/shard_map/psum | solution.py:89
  233.4 0.7 maximum_multiply_fusion.1
  (33 shorter events, 1.4 us)
Async XLA Ops:
  7.2 19.4 %copy-start = (bf16[1,1,12,128,128]{4,3,2,1,0:T(8,128)(2,1)S(1)}, bf16[1,1,12,128,128]{4,3,2,1,0:T(8,128)(2,1)}, u32[]{:S(2)}) copy-start(bf16[1,1,12,128,128]{4,3,2,1,0:T(8,128)(2,1)} %param.5) | copy-start | bytes 1179652
  7.2 1.0 copy-start.2
  7.2 74.3 %all-reduce.5.cloned.1.call-start = ((), (), s32[]{:S(2)}) async-start(), calls=%async_computation | async-start | bytes 131072 | tf_op jit(solution)/shard_map/psum | solution.py:73
  26.8 0.7 copy-start.4
  28.3 149.1 %all-reduce.7.cloned.1.call-start = ((), (), s32[]{:S(2)}) async-start(), calls=%async_computation.1 | async-start | bytes 131072 | tf_op jit(solution)/shard_map/psum | solution.py:73
  98.4 95.9 %copy-start.1 = (bf16[16,512]{1,0:T(8,128)(2,1)}, bf16[16,512]{1,0:T(8,128)(2,1)S(1)}, u32[]{:S(2)}) copy-start(bf16[16,512]{1,0:T(8,128)(2,1)S(1)} %psum.79) | copy-start | bytes 49156
  194.4 38.8 %copy-start.3 = (bf16[16,512]{1,0:T(8,128)(2,1)}, bf16[16,512]{1,0:T(8,128)(2,1)S(1)}, u32[]{:S(2)}) copy-start(bf16[16,512]{1,0:T(8,128)(2,1)S(1)} %psum.83) | copy-start | bytes 49156
Sparse Core Ops, SparseCore 0:
  28.4 52.9 all-reduce.4
  127.4 49.9 all-reduce.6
where the time goes:
time: 241 us
  blocking collectives  115 us (48%)
  waiting for transfers between devices  102 us (42%)
  between operations  14.3 us (6%)
  local copies, waits for them, and re-layouts  4.37 us (2%)
  other arithmetic  3.19 us (1%)
  matrix products  2.45 us (1%)
    psum x2, waiting for transfers between devices, apply_operator(): column_total = lax.psum(backward, 'row')  102 us
    psum x2, blocking collectives, broadcast(): return lax.psum(block, axis)  43.7 us
    psum x1, blocking collectives, local(): lax.psum((inner_products(start_piece, start_piece), inner_products(start_...  38.7 us
    psum x2, blocking collectives, apply_operator(): whole_slab = lax.psum(row_term, 'col').astype(jnp.bfloat16)  32.5 us
  transfers between devices with their start and end apart: 2, of which 2 were waited for; matrix products, arithmetic and copies ran while one was open for 1% of the time, Pallas kernels for 0%

commit v1 on v0

v1 whole, which is shorter than its diff:
```python
import jax
import jax.numpy as jnp
from jax import lax
from jax.sharding import PartitionSpec as P

highest = lax.Precision.HIGHEST
both = ("row", "col")


def block_rows_of(counts, block_total):
    positions = jnp.arange(block_total, dtype=jnp.int32)
    row_blocks = counts.shape[0]
    row_ends = [counts[0]]
    for index in range(1, row_blocks):
        row_ends.append(row_ends[-1] + counts[index])
    return sum((end <= positions).astype(jnp.int32) for end in row_ends)


def forward_tile(values, columns, block_row, source, row_blocks):
    vector_count = source.shape[0]
    block_size = values.shape[1]
    pieces = source.reshape(vector_count, -1, block_size)[:, columns, :]
    products = jnp.einsum("bij,kbj->kbi", values, pieces, preferred_element_type=jnp.float32)
    row_hot = (block_row[:, None] == jnp.arange(row_blocks, dtype=jnp.int32)[None, :]).astype(
        jnp.float32
    )
    summed = jnp.einsum("kbi,br->kri", products, row_hot, precision=highest)
    return summed.reshape(vector_count, row_blocks * block_size)


def transpose_tile(values, columns, block_row, source, col_blocks):
    vector_count = source.shape[0]
    block_size = values.shape[1]
    pieces = source.reshape(vector_count, -1, block_size)[:, block_row, :]
    products = jnp.einsum("bji,kbj->kbi", values, pieces, preferred_element_type=jnp.float32)
    col_hot = (columns[:, None] == jnp.arange(col_blocks, dtype=jnp.int32)[None, :]).astype(
        jnp.float32
    )
    summed = jnp.einsum("kbi,bc->kci", products, col_hot, precision=highest)
    return summed.reshape(vector_count, col_blocks * block_size)


def inner_products(left_block, right_block):
    return lax.dot_general(
        left_block,
        right_block,
        (((1,), (1,)), ((), ())),
        precision=highest,
        preferred_element_type=jnp.float32,
    )


def to_plane_of(col_count, ratio):
    pairs = []
    for column in range(col_count):
        planes = sorted(range(col_count), key=lambda a: -abs(a - column))
        places = sorted(range(col_count), key=lambda c: bin(c ^ column).count("1"))
        for plane, place in zip(planes, places):
            for turn in range(ratio):
                source = (plane * ratio + turn) * col_count + column
                target = (column * ratio + turn) * col_count + place
                pairs.append((source, target))
    return pairs


def xor_sum(value, others):
    level = [value, *others]
    while len(level) > 1:
        level = [level[i] + level[i + 1] for i in range(0, len(level), 2)]
    return level[0]


def local(start_block, block_values, block_columns, block_counts):
    row_count, col_count = lax.axis_size("row"), lax.axis_size("col")
    ratio = row_count // col_count
    values = block_values[0, 0]
    columns = block_columns[0, 0]
    counts = block_counts[0, 0]
    block_size = values.shape[1]
    row_blocks = counts.shape[0]
    row_width = row_blocks * block_size
    col_blocks = start_block.shape[1] // block_size
    block_row = block_rows_of(counts, values.shape[0])
    turn = lax.axis_index("row") % ratio
    norm_scale = 1.0 / (row_width * row_count)
    gather_pairs = to_plane_of(col_count, ratio)
    spread_pairs = [(target, source) for source, target in gather_pairs]
    few = col_count <= 8

    def own_part(vectors, which):
        return lax.dynamic_slice_in_dim(vectors, which * row_width, row_width, 1)

    def row_swap(value, step):
        return lax.ppermute(value, "row", [(i, i ^ step) for i in range(row_count)])

    def chip_sum(backward):
        total = own_part(backward, turn)
        for step in range(1, ratio):
            total = total + row_swap(own_part(backward, turn ^ step), step)
        return total

    def col_sum(value):
        if not few:
            return lax.psum(value, "col")
        return xor_sum(
            value,
            [
                lax.ppermute(value, "col", [(i, i ^ step) for i in range(col_count)])
                for step in range(1, col_count)
            ],
        )

    def plane_sum(value):
        if not few:
            return lax.psum(value, "row") * (1.0 / ratio)
        return xor_sum(
            value,
            [
                lax.ppermute(value, "row", [(i, i ^ (ratio * step)) for i in range(row_count)])
                for step in range(1, col_count)
            ],
        )

    start_part = own_part(start_block, turn)
    start_rows = lax.ppermute(start_part, both, gather_pairs)
    forward = forward_tile(values, columns, block_row, start_block, row_blocks)
    backward = chip_sum(transpose_tile(values, columns, block_row, start_rows, col_blocks))
    term = forward + lax.ppermute(backward, both, gather_pairs)
    applied_once = col_sum(term).astype(jnp.bfloat16)

    once_part = lax.ppermute(applied_once, both, spread_pairs)
    backward = chip_sum(transpose_tile(values, columns, block_row, applied_once, col_blocks))
    backward_term = lax.ppermute(backward, both, gather_pairs)
    grams = jnp.concatenate(
        [
            inner_products(start_part, start_part),
            inner_products(start_part, once_part),
            inner_products(once_part, once_part),
            inner_products(backward, once_part.astype(jnp.float32)),
        ],
        axis=1,
    )
    parts = [once_part] + [row_swap(once_part, step) for step in range(1, ratio)]
    for step in range(1, ratio):
        grams = grams + row_swap(grams, step)
    once_columns = jnp.concatenate(
        [
            lax.switch(turn ^ place, [lambda part=part: part for part in parts])
            if ratio > 2
            else (parts[0] if ratio == 1 else jnp.where(turn == place, parts[0], parts[1]))
            for place in range(ratio)
        ],
        axis=1,
    )
    vector_count = start_block.shape[0]
    cross = plane_sum(grams[:, 3 * vector_count :])
    grams = jnp.concatenate([grams[:, : 3 * vector_count], cross], axis=1)
    forward = forward_tile(values, columns, block_row, once_columns, row_blocks)
    message = jnp.concatenate([forward + backward_term, grams], axis=1)
    message = col_sum(message)
    applied_twice = message[:, :row_width].astype(jnp.bfloat16)
    gram_xx, gram_xy, gram_yy, cross = jnp.split(message[:, row_width:], 4, axis=1)
    gram_yz = cross + cross.T
    basis_gram = (
        jnp.concatenate(
            [jnp.concatenate([gram_xx, gram_xy], 1), jnp.concatenate([gram_xy.T, gram_yy], 1)], 0
        )
        * norm_scale
    )
    projected_gram = (
        jnp.concatenate(
            [jnp.concatenate([gram_xy, gram_yy], 1), jnp.concatenate([gram_yy, gram_yz], 1)], 0
        )
        * norm_scale
    )
    return (applied_once, applied_twice, basis_gram, projected_gram)


def solution(mesh):
    return jax.shard_map(
        local,
        mesh=mesh,
        in_specs=(
            P(None, "col"),
            P("row", "col", None, None, None),
            P("row", "col", None),
            P("row", "col", None),
        ),
        out_specs=(P(None, "row"), P(None, "row"), P(), P()),
        check_vma=False,
    )
```

time: 241 us -> 52.9 us (0.22)
  blocking collectives: 115 us -> 0 us
  waiting for transfers between devices: 102 us -> 15.7 us
  starting transfers between devices: 0.08 us -> 22.8 us
  between operations: 14.3 us -> 3.47 us
    psum x5 -> x0, blocking collectives: 115 us -> none  [the longest x2 43.7 us: broadcast(): return lax.psum(block, axis)]
    psum x2 -> x0, waiting for transfers between devices: 102 us -> none  [apply_operator(): column_total = lax.psum(backward, 'row')]
    ppermute x0 -> x17, starting transfers between devices: none -> 22.8 us  [the longest x6 6.98 us: col_sum(): lax.ppermute(value, 'col', [(i, i ^ step) for i in range(col_count)])]
    ppermute x0 -> x17, waiting for transfers between devices: none -> 15.7 us  [the longest x6 6.7 us: col_sum(): lax.ppermute(value, 'col', [(i, i ^ step) for i in range(col_count)])]
  transfers between devices with their start and end apart: 2 -> 17, of which waited for: 2 -> 13; matrix products, arithmetic and copies ran while one was open for 1% -> 10% of each run, Pallas kernels for 0% -> 0%
where the time goes in v1:
time: 52.9 us; the launch traced here: 52.7 us
  starting transfers between devices  22.8 us (43%)
  waiting for transfers between devices  15.7 us (30%)
  local copies, waits for them, and re-layouts  5.93 us (11%)
  between operations  3.47 us (7%)
  other arithmetic  2.49 us (5%)
  matrix products  2.24 us (4%)
    ppermute x6, starting transfers between devices, col_sum(): lax.ppermute(value, 'col', [(i, i ^ step) for i in range(col_count)])  6.98 us
    ppermute x6, waiting for transfers between devices, col_sum(): lax.ppermute(value, 'col', [(i, i ^ step) for i in range(col_count)])  6.7 us
    ppermute x1, starting transfers between devices, local(): start_rows = lax.ppermute(start_part, both, gather_pairs)  3.89 us
    ppermute x1, starting transfers between devices, local(): term = forward + lax.ppermute(backward, both, gather_pairs)  3.6 us
    ppermute x3, starting transfers between devices, plane_sum(): lax.ppermute(value, 'row', [(i, i ^ ratio * step) for i in range(row_coun...  3.49 us
    ppermute x1, starting transfers between devices, local(): backward_term = lax.ppermute(backward, both, gather_pairs)  2.74 us
    ppermute x4, waiting for transfers between devices, row_swap(): return lax.ppermute(value, 'row', [(i, i ^ step) for i in range(row_count)])  2.31 us
    ppermute x1, waiting for transfers between devices, local(): backward_term = lax.ppermute(backward, both, gather_pairs)  2.19 us
  transfers between devices with their start and end apart: 17, of which 13 were waited for; matrix products, arithmetic and copies ran while one was open for 10% of the time, Pallas kernels for 0%

profile of v1, /device:TPU:0, one launch (start us, length us, event | category | flops | bytes accessed | tf_op | source)
XLA Modules:
  0.0 52.7 jit_solution(1883293944987046294)
XLA Ops:
  0.7 0.8 %copy-done.1 = bf16[16,1024]{1,0:T(8,128)(2,1)S(1)} copy-done((bf16[16,1024]{1,0:T(8,128)(2,1)S(1)}, bf16[16,1024]{1,0:T(8,128)(2,1)}, u32[]{:S(2)}) %copy-start.1) | copy-done | bytes 32792
  1.5 3.9 %collective-permute-start = (bf16[16,512]{1,0:T(8,128)(2,1)S(1)}, bf16[16,512]{1,0:T(8,128)(2,1)S(1)}, u32[]{:S(2)}, u32[]{:S(2)}) collective-permute-start(bf16[16,512]{1,0:T(8,128)(2,1)S(1)} %constant_dynamic-slice_fusion.2), channel_id=1, source_target_pairs={{24,0},{28,4},{16,1},{20,5},{8,2},{12,6},{0,3},{4,7},{25,9},{29,13... | collective-permute-start | bytes 49160 | tf_op jit(solution)/shard_map/ppermute | solution.py:125
  9.2 0.7 %fusion.33 = s32[12]{0:T(128)S(1)} fusion(s32[]{:T(128)S(6)} %add.138, s32[]{:T(128)S(6)} %add.136, s32[]{:T(128)S(6)} %add.134, s32[]{:T(128)} %bitcast), kind=kLoop, calls=%fused_computation.77 | loop fusion | flops 168 | bytes 64 | tf_op jit(solution)/shard_map/select_n | solution.py:34
  11.9 0.7 %fusion.28 = s32[12]{0:T(128)S(1)} fusion(s32[]{:T(128)S(6)} %add.138, s32[]{:T(128)S(6)} %add.136, s32[]{:T(128)S(6)} %add.134, s32[]{:T(128)} %bitcast), kind=kLoop, calls=%fused_computation.72 | loop fusion | flops 132 | bytes 64 | tf_op jit(solution)/shard_map/add | solution.py:16
  13.1 3.6 %collective-permute-start.2 = (f32[16,512]{1,0:T(8,128)S(1)}, f32[16,512]{1,0:T(8,128)S(1)}, u32[]{:S(2)}, u32[]{:S(2)}) collective-permute-start(f32[16,512]{1,0:T(8,128)S(1)} %dynamic-slice_add_fusion.1), channel_id=1, source_target_pairs={{24,0},{28,4},{16,1},{20,5},{8,2},{12,6},{0,3},{4,7},{25,9},{29,13... | collective-permute-start | bytes 98312 | tf_op jit(solution)/shard_map/ppermute | solution.py:128
  16.9 1.9 %collective-permute-done.2 = f32[16,512]{1,0:T(8,128)S(1)} collective-permute-done((f32[16,512]{1,0:T(8,128)S(1)}, f32[16,512]{1,0:T(8,128)S(1)}, u32[]{:S(2)}, u32[]{:S(2)}) %collective-permute-start.2) | collective-permute-done | bytes 32800 | tf_op jit(solution)/shard_map/ppermute | solution.py:128
  18.9 1.6 %collective-permute-start.4 = (f32[16,512]{1,0:T(8,128)S(1)}, f32[16,512]{1,0:T(8,128)S(1)}, u32[]{:S(2)}, u32[]{:S(2)}) collective-permute-start(f32[16,512]{1,0:T(8,128)S(1)} %bitcast_add_fusion.1), channel_id=1, source_target_pairs={{0,2},{1,3},{2,0},{3,1},{4,6},{5,7},{6,4},{7,5},{8,10},{9,11},{10,... | collective-permute-start | bytes 98312 | tf_op jit(solution)/shard_map/ppermute | solution.py:108
  20.5 1.1 %collective-permute-start.5 = (f32[16,512]{1,0:T(8,128)S(1)}, f32[16,512]{1,0:T(8,128)S(1)}, u32[]{:S(2)}, u32[]{:S(2)}) collective-permute-start(f32[16,512]{1,0:T(8,128)S(1)} %bitcast_add_fusion.1), channel_id=1, source_target_pairs={{0,3},{1,2},{2,1},{3,0},{4,7},{5,6},{6,5},{7,4},{8,11},{9,10},{10,... | collective-permute-start | bytes 98312 | tf_op jit(solution)/shard_map/ppermute | solution.py:108
  21.6 0.7 %collective-permute-start.3 = (f32[16,512]{1,0:T(8,128)S(1)}, f32[16,512]{1,0:T(8,128)S(1)}, u32[]{:S(2)}, u32[]{:S(2)}) collective-permute-start(f32[16,512]{1,0:T(8,128)S(1)} %bitcast_add_fusion.1), channel_id=1, source_target_pairs={{0,1},{1,0},{2,3},{3,2},{4,5},{5,4},{6,7},{7,6},{8,9},{9,8},{10,11... | collective-permute-start | bytes 98312 | tf_op jit(solution)/shard_map/ppermute | solution.py:108
  22.8 2.5 %collective-permute-done.5 = f32[16,512]{1,0:T(8,128)S(1)} collective-permute-done((f32[16,512]{1,0:T(8,128)S(1)}, f32[16,512]{1,0:T(8,128)S(1)}, u32[]{:S(2)}, u32[]{:S(2)}) %collective-permute-start.5) | collective-permute-done | bytes 32800 | tf_op jit(solution)/shard_map/ppermute | solution.py:108
  26.2 1.8 %collective-permute-start.6 = (bf16[16,512]{1,0:T(8,128)(2,1)S(1)}, bf16[16,512]{1,0:T(8,128)(2,1)S(1)}, u32[]{:S(2)}, u32[]{:S(2)}) collective-permute-start(bf16[16,512]{1,0:T(8,128)(2,1)S(1)} %add_convert_fusion), channel_id=1, source_target_pairs={{0,24},{4,28},{1,16},{5,20},{2,8},{6,12},{3,0},{7,4},{9,25},{13,29... | collective-permute-start | bytes 49160 | tf_op jit(solution)/shard_map/ppermute | solution.py:131
  29.1 1.7 %collective-permute-done.6 = bf16[16,512]{1,0:T(8,128)(2,1)S(1)} collective-permute-done((bf16[16,512]{1,0:T(8,128)(2,1)S(1)}, bf16[16,512]{1,0:T(8,128)(2,1)S(1)}, u32[]{:S(2)}, u32[]{:S(2)}) %collective-permute-start.6) | collective-permute-done | bytes 16416 | tf_op jit(solution)/shard_map/ppermute | solution.py:131
  31.0 1.1 %collective-permute-done.7 = bf16[16,512]{1,0:T(8,128)(2,1)S(1)} collective-permute-done((bf16[16,512]{1,0:T(8,128)(2,1)S(1)}, bf16[16,512]{1,0:T(8,128)(2,1)S(1)}, u32[]{:S(2)}, u32[]{:S(2)}) %collective-permute-start.7) | collective-permute-done | bytes 16416 | tf_op jit(solution)/shard_map/ppermute | solution.py:94
  33.4 0.7 %collective-permute-done.10 = f32[16,64]{1,0:T(8,128)S(1)} collective-permute-done((f32[16,64]{1,0:T(8,128)S(1)}, f32[16,64]{1,0:T(8,128)S(1)}, u32[]{:S(2)}, u32[]{:S(2)}) %collective-permute-start.10) | collective-permute-done | bytes 4128 | tf_op jit(solution)/shard_map/ppermute | solution.py:94
  34.2 1.7 %collective-permute-start.12 = (f32[16,16]{1,0:T(8,128)S(1)}, f32[16,16]{1,0:T(8,128)S(1)}, u32[]{:S(2)}, u32[]{:S(2)}) collective-permute-start(f32[16,16]{1,0:T(8,128)S(1)} %slice.49), channel_id=1, source_target_pairs={{0,16},{4,20},{8,24},{12,28},{16,0},{20,4},{24,8},{28,12},{1,17},{... | collective-permute-start | bytes 3080 | tf_op jit(solution)/shard_map/ppermute | solution.py:119
  36.0 1.1 %collective-permute-start.13 = (f32[16,16]{1,0:T(8,128)S(1)}, f32[16,16]{1,0:T(8,128)S(1)}, u32[]{:S(2)}, u32[]{:S(2)}) collective-permute-start(f32[16,16]{1,0:T(8,128)S(1)} %slice.49), channel_id=1, source_target_pairs={{0,24},{4,28},{8,16},{12,20},{16,8},{20,12},{24,0},{28,4},{1,25},{... | collective-permute-start | bytes 3080 | tf_op jit(solution)/shard_map/ppermute | solution.py:119
  37.9 2.7 %collective-permute-start.9 = (f32[16,512]{1,0:T(8,128)S(1)}, f32[16,512]{1,0:T(8,128)S(1)}, u32[]{:S(2)}, u32[]{:S(2)}) collective-permute-start(f32[16,512]{1,0:T(8,128)S(1)} %dynamic-slice_add_fusion), channel_id=1, source_target_pairs={{24,0},{28,4},{16,1},{20,5},{8,2},{12,6},{0,3},{4,7},{25,9},{29,13... | collective-permute-start | bytes 98312 | tf_op jit(solution)/shard_map/ppermute | solution.py:133
  40.6 0.9 %collective-permute-done.13 = f32[16,16]{1,0:T(8,128)S(1)} collective-permute-done((f32[16,16]{1,0:T(8,128)S(1)}, f32[16,16]{1,0:T(8,128)S(1)}, u32[]{:S(2)}, u32[]{:S(2)}) %collective-permute-start.13) | collective-permute-done | bytes 1056 | tf_op jit(solution)/shard_map/ppermute | solution.py:119
  41.6 2.2 %collective-permute-done.9 = f32[16,512]{1,0:T(8,128)S(1)} collective-permute-done((f32[16,512]{1,0:T(8,128)S(1)}, f32[16,512]{1,0:T(8,128)S(1)}, u32[]{:S(2)}, u32[]{:S(2)}) %collective-permute-start.9) | collective-permute-done | bytes 32800 | tf_op jit(solution)/shard_map/ppermute | solution.py:133
  43.9 1.0 %collective-permute-start.15 = (f32[16,576]{1,0:T(8,128)S(1)}, f32[16,576]{1,0:T(8,128)S(1)}, u32[]{:S(2)}, u32[]{:S(2)}) collective-permute-start(f32[16,576]{1,0:T(8,128)S(1)} %pad_maximum_fusion), channel_id=1, source_target_pairs={{0,2},{1,3},{2,0},{3,1},{4,6},{5,7},{6,4},{7,5},{8,10},{9,11},{10,... | collective-permute-start | bytes 110600 | tf_op jit(solution)/shard_map/ppermute | solution.py:108
  44.8 2.2 %collective-permute-start.16 = (f32[16,576]{1,0:T(8,128)S(1)}, f32[16,576]{1,0:T(8,128)S(1)}, u32[]{:S(2)}, u32[]{:S(2)}) collective-permute-start(f32[16,576]{1,0:T(8,128)S(1)} %pad_maximum_fusion), channel_id=1, source_target_pairs={{0,3},{1,2},{2,1},{3,0},{4,7},{5,6},{6,5},{7,4},{8,11},{9,10},{10,... | collective-permute-start | bytes 110600 | tf_op jit(solution)/shard_map/ppermute | solution.py:108
  47.9 1.9 %collective-permute-done.16 = f32[16,576]{1,0:T(8,128)S(1)} collective-permute-done((f32[16,576]{1,0:T(8,128)S(1)}, f32[16,576]{1,0:T(8,128)S(1)}, u32[]{:S(2)}, u32[]{:S(2)}) %collective-permute-start.16) | collective-permute-done | bytes 36896 | tf_op jit(solution)/shard_map/ppermute | solution.py:108
  49.7 1.3 %collective-permute-done.14 = f32[16,576]{1,0:T(8,128)S(1)} collective-permute-done((f32[16,576]{1,0:T(8,128)S(1)}, f32[16,576]{1,0:T(8,128)S(1)}, u32[]{:S(2)}, u32[]{:S(2)}) %collective-permute-start.14) | collective-permute-done | bytes 36896 | tf_op jit(solution)/shard_map/ppermute | solution.py:108
  52.0 0.7 %maximum_multiply_fusion.1 = (f32[32,32]{1,0:T(8,128)}, f32[32,32]{1,0:T(8,128)}) fusion(f32[16,16]{1,0:T(8,128)S(1)} %get-tuple-element.6, f32[16,16]{1,0:T(8,128)S(1)} %get-tuple-element.7, f32[16,32]{1,0:T(8,128)S(1)} %get-tuple-element.4, f32[16,16]{1,0:T(8,128)S(1)} %copy.20, f32[16,32]{1,0:T(8,128)S(1)} %get-tuple-element.5), kind=kLoop, calls=%fused_computation.40 | loop fusion | flops 6144 | bytes 15360 | tf_op jit(solution)/shard_map/mul | solution.py:171
  (70 shorter events, 10.8 us)
Async XLA Ops:
  0.6 9.9 %copy-start = (bf16[1,1,12,128,128]{4,3,2,1,0:T(8,128)(2,1)S(1)}, bf16[1,1,12,128,128]{4,3,2,1,0:T(8,128)(2,1)}, u32[]{:S(2)}) copy-start(bf16[1,1,12,128,128]{4,3,2,1,0:T(8,128)(2,1)} %param.5) | copy-start | bytes 1179652
  0.6 0.8 %copy-start.1 = (bf16[16,1024]{1,0:T(8,128)(2,1)S(1)}, bf16[16,1024]{1,0:T(8,128)(2,1)}, u32[]{:S(2)}) copy-start(bf16[16,1024]{1,0:T(8,128)(2,1)} %param.4) | copy-start | bytes 98308
  1.5 9.4 %collective-permute-start = (bf16[16,512]{1,0:T(8,128)(2,1)S(1)}, bf16[16,512]{1,0:T(8,128)(2,1)S(1)}, u32[]{:S(2)}, u32[]{:S(2)}) collective-permute-start(bf16[16,512]{1,0:T(8,128)(2,1)S(1)} %constant_dynamic-slice_fusion.2), channel_id=1, source_target_pairs={{24,0},{28,4},{16,1},{20,5},{8,2},{12,6},{0,3},{4,7},{25,9},{29,13... | collective-permute-start | bytes 49160 | tf_op jit(solution)/shard_map/ppermute | solution.py:125
  5.4 0.7 %copy-start.3 = (s32[1,1,4]{2,1,0:T(1,128)S(1)}, s32[1,1,4]{2,1,0:T(1,128)}, u32[]{:S(2)}) copy-start(s32[1,1,4]{2,1,0:T(1,128)} %param.7) | copy-start | bytes 52
  9.2 0.7 %copy-start.4 = (s32[1,1,12]{2,1,0:T(1,128)S(1)}, s32[1,1,12]{2,1,0:T(1,128)}, u32[]{:S(2)}) copy-start(s32[1,1,12]{2,1,0:T(1,128)} %param.6) | copy-start | bytes 148
  11.9 1.3 %collective-permute-start.1 = (f32[16,512]{1,0:T(8,128)S(1)}, f32[16,512]{1,0:T(8,128)S(1)}, u32[]{:S(2)}, u32[]{:S(2)}) collective-permute-start(f32[16,512]{1,0:T(8,128)S(1)} %constant_dynamic-slice_fusion.1), channel_id=1, source_target_pairs={{0,4},{4,0},{8,12},{12,8},{16,20},{20,16},{24,28},{28,24},{1,5},{5... | collective-permute-start | bytes 98312 | tf_op jit(solution)/shard_map/ppermute | solution.py:94
  13.1 5.7 %collective-permute-start.2 = (f32[16,512]{1,0:T(8,128)S(1)}, f32[16,512]{1,0:T(8,128)S(1)}, u32[]{:S(2)}, u32[]{:S(2)}) collective-permute-start(f32[16,512]{1,0:T(8,128)S(1)} %dynamic-slice_add_fusion.1), channel_id=1, source_target_pairs={{24,0},{28,4},{16,1},{20,5},{8,2},{12,6},{0,3},{4,7},{25,9},{29,13... | collective-permute-start | bytes 98312 | tf_op jit(solution)/shard_map/ppermute | solution.py:128
  18.9 3.9 %collective-permute-start.4 = (f32[16,512]{1,0:T(8,128)S(1)}, f32[16,512]{1,0:T(8,128)S(1)}, u32[]{:S(2)}, u32[]{:S(2)}) collective-permute-start(f32[16,512]{1,0:T(8,128)S(1)} %bitcast_add_fusion.1), channel_id=1, source_target_pairs={{0,2},{1,3},{2,0},{3,1},{4,6},{5,7},{6,4},{7,5},{8,10},{9,11},{10,... | collective-permute-start | bytes 98312 | tf_op jit(solution)/shard_map/ppermute | solution.py:108
  20.5 4.8 %collective-permute-start.5 = (f32[16,512]{1,0:T(8,128)S(1)}, f32[16,512]{1,0:T(8,128)S(1)}, u32[]{:S(2)}, u32[]{:S(2)}) collective-permute-start(f32[16,512]{1,0:T(8,128)S(1)} %bitcast_add_fusion.1), channel_id=1, source_target_pairs={{0,3},{1,2},{2,1},{3,0},{4,7},{5,6},{6,5},{7,4},{8,11},{9,10},{10,... | collective-permute-start | bytes 98312 | tf_op jit(solution)/shard_map/ppermute | solution.py:108
  21.6 3.9 %collective-permute-start.3 = (f32[16,512]{1,0:T(8,128)S(1)}, f32[16,512]{1,0:T(8,128)S(1)}, u32[]{:S(2)}, u32[]{:S(2)}) collective-permute-start(f32[16,512]{1,0:T(8,128)S(1)} %bitcast_add_fusion.1), channel_id=1, source_target_pairs={{0,1},{1,0},{2,3},{3,2},{4,5},{5,4},{6,7},{7,6},{8,9},{9,8},{10,11... | collective-permute-start | bytes 98312 | tf_op jit(solution)/shard_map/ppermute | solution.py:108
  25.6 0.6 %copy-start.2 = (bf16[16,512]{1,0:T(8,128)(2,1)}, bf16[16,512]{1,0:T(8,128)(2,1)S(1)}, u32[]{:S(2)}) copy-start(bf16[16,512]{1,0:T(8,128)(2,1)S(1)} %add_convert_fusion) | copy-start | bytes 49156
  26.2 4.6 %collective-permute-start.6 = (bf16[16,512]{1,0:T(8,128)(2,1)S(1)}, bf16[16,512]{1,0:T(8,128)(2,1)S(1)}, u32[]{:S(2)}, u32[]{:S(2)}) collective-permute-start(bf16[16,512]{1,0:T(8,128)(2,1)S(1)} %add_convert_fusion), channel_id=1, source_target_pairs={{0,24},{4,28},{1,16},{5,20},{2,8},{6,12},{3,0},{7,4},{9,25},{13,29... | collective-permute-start | bytes 49160 | tf_op jit(solution)/shard_map/ppermute | solution.py:131
  29.0 3.7 %collective-permute-start.8 = (f32[16,512]{1,0:T(8,128)S(1)}, f32[16,512]{1,0:T(8,128)S(1)}, u32[]{:S(2)}, u32[]{:S(2)}) collective-permute-start(f32[16,512]{1,0:T(8,128)S(1)} %constant_dynamic-slice_fusion), channel_id=1, source_target_pairs={{0,4},{4,0},{8,12},{12,8},{16,20},{20,16},{24,28},{28,24},{1,5},{5... | collective-permute-start | bytes 98312 | tf_op jit(solution)/shard_map/ppermute | solution.py:94
  30.9 1.2 %collective-permute-start.7 = (bf16[16,512]{1,0:T(8,128)(2,1)S(1)}, bf16[16,512]{1,0:T(8,128)(2,1)S(1)}, u32[]{:S(2)}, u32[]{:S(2)}) collective-permute-start(bf16[16,512]{1,0:T(8,128)(2,1)S(1)} %collective-permute-done.6), channel_id=1, source_target_pairs={{0,4},{4,0},{8,12},{12,8},{16,20},{20,16},{24,28},{28,24},{1,5},{5... | collective-permute-start | bytes 49160 | tf_op jit(solution)/shard_map/ppermute | solution.py:94
  33.0 1.2 %collective-permute-start.10 = (f32[16,64]{1,0:T(8,128)S(1)}, f32[16,64]{1,0:T(8,128)S(1)}, u32[]{:S(2)}, u32[]{:S(2)}) collective-permute-start(f32[16,64]{1,0:T(8,128)S(1)} %pad_maximum_fusion.1), channel_id=1, source_target_pairs={{0,4},{4,0},{8,12},{12,8},{16,20},{20,16},{24,28},{28,24},{1,5},{5... | collective-permute-start | bytes 12296 | tf_op jit(solution)/shard_map/ppermute | solution.py:94
  34.2 6.4 %collective-permute-start.12 = (f32[16,16]{1,0:T(8,128)S(1)}, f32[16,16]{1,0:T(8,128)S(1)}, u32[]{:S(2)}, u32[]{:S(2)}) collective-permute-start(f32[16,16]{1,0:T(8,128)S(1)} %slice.49), channel_id=1, source_target_pairs={{0,16},{4,20},{8,24},{12,28},{16,0},{20,4},{24,8},{28,12},{1,17},{... | collective-permute-start | bytes 3080 | tf_op jit(solution)/shard_map/ppermute | solution.py:119
  36.0 5.6 %collective-permute-start.13 = (f32[16,16]{1,0:T(8,128)S(1)}, f32[16,16]{1,0:T(8,128)S(1)}, u32[]{:S(2)}, u32[]{:S(2)}) collective-permute-start(f32[16,16]{1,0:T(8,128)S(1)} %slice.49), channel_id=1, source_target_pairs={{0,24},{4,28},{8,16},{12,20},{16,8},{20,12},{24,0},{28,4},{1,25},{... | collective-permute-start | bytes 3080 | tf_op jit(solution)/shard_map/ppermute | solution.py:119
  37.1 4.4 %collective-permute-start.11 = (f32[16,16]{1,0:T(8,128)S(1)}, f32[16,16]{1,0:T(8,128)S(1)}, u32[]{:S(2)}, u32[]{:S(2)}) collective-permute-start(f32[16,16]{1,0:T(8,128)S(1)} %slice.49), channel_id=1, source_target_pairs={{0,8},{4,12},{8,0},{12,4},{16,24},{20,28},{24,16},{28,20},{1,9},{5... | collective-permute-start | bytes 3080 | tf_op jit(solution)/shard_map/ppermute | solution.py:119
  37.9 5.9 %collective-permute-start.9 = (f32[16,512]{1,0:T(8,128)S(1)}, f32[16,512]{1,0:T(8,128)S(1)}, u32[]{:S(2)}, u32[]{:S(2)}) collective-permute-start(f32[16,512]{1,0:T(8,128)S(1)} %dynamic-slice_add_fusion), channel_id=1, source_target_pairs={{24,0},{28,4},{16,1},{20,5},{8,2},{12,6},{0,3},{4,7},{25,9},{29,13... | collective-permute-start | bytes 98312 | tf_op jit(solution)/shard_map/ppermute | solution.py:133
  43.9 4.0 %collective-permute-start.15 = (f32[16,576]{1,0:T(8,128)S(1)}, f32[16,576]{1,0:T(8,128)S(1)}, u32[]{:S(2)}, u32[]{:S(2)}) collective-permute-start(f32[16,576]{1,0:T(8,128)S(1)} %pad_maximum_fusion), channel_id=1, source_target_pairs={{0,2},{1,3},{2,0},{3,1},{4,6},{5,7},{6,4},{7,5},{8,10},{9,11},{10,... | collective-permute-start | bytes 110600 | tf_op jit(solution)/shard_map/ppermute | solution.py:108
  44.8 4.9 %collective-permute-start.16 = (f32[16,576]{1,0:T(8,128)S(1)}, f32[16,576]{1,0:T(8,128)S(1)}, u32[]{:S(2)}, u32[]{:S(2)}) collective-permute-start(f32[16,576]{1,0:T(8,128)S(1)} %pad_maximum_fusion), channel_id=1, source_target_pairs={{0,3},{1,2},{2,1},{3,0},{4,7},{5,6},{6,5},{7,4},{8,11},{9,10},{10,... | collective-permute-start | bytes 110600 | tf_op jit(solution)/shard_map/ppermute | solution.py:108
  47.0 4.0 %collective-permute-start.14 = (f32[16,576]{1,0:T(8,128)S(1)}, f32[16,576]{1,0:T(8,128)S(1)}, u32[]{:S(2)}, u32[]{:S(2)}) collective-permute-start(f32[16,576]{1,0:T(8,128)S(1)} %pad_maximum_fusion), channel_id=1, source_target_pairs={{0,1},{1,0},{2,3},{3,2},{4,5},{5,4},{6,7},{7,6},{8,9},{9,8},{10,11... | collective-permute-start | bytes 110600 | tf_op jit(solution)/shard_map/ppermute | solution.py:108

commit v2 on v1

v2 whole, which is shorter than its diff:
```python
import functools

import jax
import jax.numpy as jnp
from jax import lax
from jax.experimental import pallas as pl
from jax.experimental.pallas import tpu as pltpu
from jax.sharding import PartitionSpec as P

highest = lax.Precision.HIGHEST
both = ("row", "col")
f32 = jnp.float32
vmem = pl.BlockSpec(memory_space=pltpu.VMEM)
smem = pl.BlockSpec(memory_space=pltpu.SMEM)


def call(kernel, out_shape, in_specs, scratch=(), flops=0, bytes_accessed=0):
    room = 2 * bytes_accessed + (1 << 20)
    return pl.pallas_call(
        kernel,
        out_shape=out_shape,
        in_specs=in_specs,
        out_specs=jax.tree.map(lambda _: vmem, out_shape),
        scratch_shapes=scratch,
        compiler_params=pltpu.CompilerParams(vmem_limit_bytes=room),
        cost_estimate=pl.CostEstimate(
            flops=flops, bytes_accessed=bytes_accessed, transcendentals=0
        ),
    )


def each_block(columns_ref, counts_ref, block_total, visit):
    row_blocks = counts_ref.shape[0]
    if block_total <= 16:
        ends = [counts_ref[0]]
        for index in range(1, row_blocks - 1):
            ends.append(ends[-1] + counts_ref[index])
        for block in range(block_total):
            visit(block, sum((block >= end).astype(jnp.int32) for end in ends), columns_ref[block])
        return

    def step(block, carry):
        row, end = carry
        later = block >= end
        row = row + later.astype(jnp.int32)
        end = end + jnp.where(later, counts_ref[row], 0)
        visit(block, row, columns_ref[block])
        return row, end

    lax.fori_loop(0, block_total, step, (jnp.int32(0), counts_ref[0]))


def split_into(pieces_ref, source, start=0):
    size = pieces_ref.shape[2]
    for index in range(source.shape[1] // size):
        pieces_ref[start + index] = source[:, index * size : (index + 1) * size]


def run_forward(columns_ref, counts_ref, values_ref, pieces, sums):
    sums[...] = jnp.zeros_like(sums)

    def visit(block, row, column):
        sums[row] += lax.dot_general(
            pieces[column],
            values_ref[block],
            (((1,), (1,)), ((), ())),
            preferred_element_type=f32,
        )

    each_block(columns_ref, counts_ref, values_ref.shape[0], visit)


def run_backward(columns_ref, counts_ref, values_ref, pieces, sums, base):
    sums[...] = jnp.zeros_like(sums)

    def visit(block, row, column):
        sums[column] += jnp.dot(
            pieces[base + row], values_ref[block], preferred_element_type=f32
        )

    each_block(columns_ref, counts_ref, values_ref.shape[0], visit)


def forward_kernel(columns_ref, counts_ref, source_ref, values_ref, out_ref, pieces, sums):
    split_into(pieces, source_ref[...])
    run_forward(columns_ref, counts_ref, values_ref, pieces, sums)
    size = sums.shape[2]
    for row in range(sums.shape[0]):
        out_ref[:, row * size : (row + 1) * size] = sums[row]


def backward_kernel(
    ratio, columns_ref, counts_ref, turn_ref, source_ref, values_ref, *rest
):
    outs, (pieces, sums) = rest[:ratio], rest[ratio:]
    turn = turn_ref[0]
    row_blocks = counts_ref.shape[0]
    whole = source_ref.shape[1] == sums.shape[0] * sums.shape[2]
    split_into(pieces, source_ref[...])
    base = turn * row_blocks if whole and ratio > 1 else 0
    run_backward(columns_ref, counts_ref, values_ref, pieces, sums, base)
    size = sums.shape[2]
    for step, out_ref in enumerate(outs):
        first = jnp.bitwise_xor(turn, step) * row_blocks
        for row in range(row_blocks):
            out_ref[:, row * size : (row + 1) * size] = sums[first + row]


def gram_kernel(ratio, scale, turn_ref, start_ref, once_ref, backward_ref, out_ref):
    width = once_ref.shape[1]
    vectors = once_ref.shape[0]
    start = start_ref[:, :width]
    for place in range(1, ratio):
        start = jnp.where(
            turn_ref[0] == place, start_ref[:, place * width : (place + 1) * width], start
        )
    once = once_ref[...]
    contract = (((1,), (1,)), ((), ()))
    gram = functools.partial(lax.dot_general, dimension_numbers=contract)
    basis = jnp.concatenate([start, once], axis=0)
    square = gram(basis, basis, preferred_element_type=f32) * scale
    wide = once.astype(f32)
    backward = backward_ref[...]
    cross = gram(wide, backward, precision=highest, preferred_element_type=f32)
    cross = cross + gram(backward, wide, precision=highest, preferred_element_type=f32)
    out_ref[:, :width] = wide
    out_ref[:, width:] = jnp.zeros((vectors, out_ref.shape[1] - width), f32)
    out_ref[:, width : width + 2 * vectors] = square[:vectors]
    out_ref[:, width + 2 * vectors : width + 4 * vectors] = square[vectors:]
    out_ref[:, width + 4 * vectors : width + 5 * vectors] = cross


def second_kernel(
    ratio, columns_ref, counts_ref, turn_ref, values_ref, *rest
):
    parts, (out_ref, pieces, sums) = rest[:ratio], rest[ratio:]
    turn = turn_ref[0]
    row_blocks = counts_ref.shape[0]
    size = sums.shape[2]
    for step, part_ref in enumerate(parts):
        first = jnp.bitwise_xor(turn, step) * row_blocks
        for row in range(row_blocks):
            pieces[first + row] = part_ref[:, row * size : (row + 1) * size].astype(pieces.dtype)
    run_forward(columns_ref, counts_ref, values_ref, pieces, sums)
    for row in range(row_blocks):
        out_ref[:, row * size : (row + 1) * size] = sums[row]


def last_kernel(norm_scale, *refs):
    messages, (twice_ref, basis_ref, projected_ref) = refs[:-3], refs[-3:]
    width = twice_ref.shape[1]
    vectors = twice_ref.shape[0]
    total = xor_sum(messages[0][...], [message[...] for message in messages[1:]])
    twice_ref[...] = total[:, :width].astype(twice_ref.dtype)
    grams = total[:, width:] * norm_scale

    def tile(index, count=1):
        return grams[:, index * vectors : (index + count) * vectors]

    basis_ref[:vectors] = tile(0, 2)
    basis_ref[vectors:] = tile(2, 2)
    projected_ref[:vectors, :vectors] = tile(1)
    projected_ref[:vectors, vectors:] = tile(3)
    projected_ref[vectors:] = tile(3, 2)


def to_plane_of(col_count, ratio):
    pairs = []
    for column in range(col_count):
        planes = sorted(range(col_count), key=lambda a: -abs(a - column))
        places = sorted(range(col_count), key=lambda c: bin(c ^ column).count("1"))
        for plane, place in zip(planes, places):
            for turn in range(ratio):
                source = (plane * ratio + turn) * col_count + column
                target = (column * ratio + turn) * col_count + place
                pairs.append((source, target))
    return pairs


def xor_sum(value, others):
    level = [value, *others]
    while len(level) > 1:
        level = [level[i] + level[i + 1] for i in range(0, len(level), 2)]
    return level[0]


def local(start_block, block_values, block_columns, block_counts):
    row_count, col_count = lax.axis_size("row"), lax.axis_size("col")
    ratio = row_count // col_count
    values = block_values[0, 0]
    columns = block_columns[0, 0]
    counts = block_counts[0, 0]
    block_total, block_size = values.shape[:2]
    row_blocks = counts.shape[0]
    row_width = row_blocks * block_size
    vectors, col_width = start_block.shape
    col_blocks = col_width // block_size
    turn = (lax.axis_index("row") % ratio).reshape(1)
    norm_scale = 1.0 / (row_width * row_count)
    gather_pairs = to_plane_of(col_count, ratio)
    spread_pairs = [(target, source) for source, target in gather_pairs]
    few = col_count <= 8
    flops = 2 * vectors * block_total * block_size**2
    bytes_accessed = 2 * block_total * block_size**2
    slab = jax.ShapeDtypeStruct((vectors, row_width), f32)

    def row_swap(value, step):
        return lax.ppermute(value, "row", [(i, i ^ step) for i in range(row_count)])

    def col_others(value):
        return [
            lax.ppermute(value, "col", [(i, i ^ step) for i in range(col_count)])
            for step in range(1, col_count)
        ]

    def plane_sum(value):
        if not few:
            return lax.psum(value, "row") * (1.0 / ratio)
        return xor_sum(value, [row_swap(value, ratio * step) for step in range(1, col_count)])

    def backward_of(source):
        outs = call(
            functools.partial(backward_kernel, ratio),
            [slab] * ratio,
            [smem, smem, smem, vmem, vmem],
            [
                pltpu.VMEM((source.shape[1] // block_size, vectors, block_size), source.dtype),
                pltpu.VMEM((col_blocks, vectors, block_size), f32),
            ],
            flops,
            bytes_accessed,
        )(columns, counts, turn, source, values)
        total = outs[0]
        for step in range(1, ratio):
            total = total + row_swap(outs[step], step)
        return total

    product_scratch = [
        pltpu.VMEM((col_blocks, vectors, block_size), start_block.dtype),
        pltpu.VMEM((row_blocks, vectors, block_size), f32),
    ]
    start_rows = lax.ppermute(start_block, both, gather_pairs)
    forward = call(
        forward_kernel, slab, [smem, smem, vmem, vmem], product_scratch, flops, bytes_accessed
    )(columns, counts, start_block, values)
    backward = backward_of(start_rows)
    term = forward + lax.ppermute(backward, both, gather_pairs)
    if few:
        applied_once = xor_sum(term, col_others(term)).astype(jnp.bfloat16)
    else:
        applied_once = lax.psum(term, "col").astype(jnp.bfloat16)

    once_part = lax.ppermute(applied_once, both, spread_pairs)
    backward = backward_of(applied_once)
    backward_term = lax.ppermute(backward, both, gather_pairs)
    message = call(
        functools.partial(gram_kernel, ratio, 1.0 / col_count),
        jax.ShapeDtypeStruct((vectors, row_width + 128), f32),
        [smem, vmem, vmem, vmem],
        (),
        8 * vectors * vectors * row_width,
        8 * vectors * row_width,
    )(turn, start_block, once_part, backward)
    messages = [message] + [row_swap(message, step) for step in range(1, ratio)]
    grams = plane_sum(sum(part[:, row_width:] for part in messages))
    forward = call(
        functools.partial(second_kernel, ratio),
        slab,
        [smem, smem, smem, vmem] + [vmem] * ratio,
        product_scratch,
        flops,
        bytes_accessed,
    )(columns, counts, turn, values, *messages)
    message = jnp.concatenate([forward + backward_term, grams], axis=1)
    others = col_others(message) if few else []
    if not few:
        message = lax.psum(message, "col")
    small = jax.ShapeDtypeStruct((2 * vectors, 2 * vectors), f32)
    applied_twice, basis_gram, projected_gram = call(
        functools.partial(last_kernel, norm_scale),
        [jax.ShapeDtypeStruct((vectors, row_width), jnp.bfloat16), small, small],
        [vmem] * (1 + len(others)),
    )(message, *others)
    return (applied_once, applied_twice, basis_gram, projected_gram)


def solution(mesh):
    return jax.shard_map(
        local,
        mesh=mesh,
        in_specs=(
            P(None, "col"),
            P("row", "col", None, None, None),
            P("row", "col", None),
            P("row", "col", None),
        ),
        out_specs=(P(None, "row"), P(None, "row"), P(), P()),
        check_vma=False,
    )
```

time: 52.9 us -> 47.8 us (0.904)
  local copies, waits for them, and re-layouts: 5.93 us -> 1.68 us
  Pallas kernels: 0 us -> 4.2 us
  between operations: 3.47 us -> 0.74 us
  other arithmetic: 2.49 us -> 0.06 us
  matrix products: 2.24 us -> 0 us
  waiting for transfers between devices: 15.7 us -> 17.2 us
  starting transfers between devices: 22.8 us -> 23.8 us
    ppermute x4 -> x6, starting transfers between devices: 0.32 us -> 4.55 us  [row_swap(): return lax.ppermute(value, 'row', [(i, i ^ step) for i in range(row_count)])]
    pallas_call x0 -> x6, Pallas kernels: none -> 4.2 us  [the longest x2 1.53 us: backward_of(): call(functools.partial(backward_kernel, ratio), [slab] * ratio, [smem, sm...]
    ppermute x10 -> x7, starting transfers between devices: 14.4 us -> 11 us  [the longest x6 7.07 us: col_others(): lax.ppermute(value, 'col', [(i, i ^ step) for i in range(col_count)])]
    gather x4 -> x0, local copies, waits for them, and re-layouts: 2.26 us -> none  [the longest x2 1.13 us: forward_tile(): pieces = source.reshape(vector_count, -1, block_size)[:, columns, :]]
    dot_general x12 -> x0, matrix products: 2.24 us -> none  [the longest x2 0.6 us: forward_tile(): jnp.einsum('bij,kbj->kbi', values, pieces, preferred_element_type=jnp.flo...]
    ppermute x1, starting transfers between devices: 1.81 us -> 4.03 us  [local(): once_part = lax.ppermute(applied_once, both, spread_pairs)]
    ppermute x1, waiting for transfers between devices: 2.19 us -> 0.01 us  [local(): backward_term = lax.ppermute(backward, both, gather_pairs)]
    ppermute x10 -> x7, waiting for transfers between devices: 7.58 us -> 9.23 us  [the longest x6 5.96 us: col_others(): lax.ppermute(value, 'col', [(i, i ^ step) for i in range(col_count)])]
  transfers between devices with their start and end apart: 17 -> 16, of which waited for: 13 -> 11; matrix products, arithmetic and copies ran while one was open for 10% -> 0% of each run, Pallas kernels for 0% -> 4%
where the time goes in v2:
time: 47.8 us; the launch traced here: 47.6 us
  starting transfers between devices  23.8 us (50%)
  waiting for transfers between devices  17.2 us (36%)
  Pallas kernels  4.2 us (9%)
  local copies, waits for them, and re-layouts  1.68 us (4%)
  between operations  0.74 us (2%)
    ppermute x6, starting transfers between devices, col_others(): lax.ppermute(value, 'col', [(i, i ^ step) for i in range(col_count)])  7.07 us
    ppermute x6, waiting for transfers between devices, col_others(): lax.ppermute(value, 'col', [(i, i ^ step) for i in range(col_count)])  5.96 us
    ppermute x6, starting transfers between devices, row_swap(): return lax.ppermute(value, 'row', [(i, i ^ step) for i in range(row_count)])  4.55 us
    ppermute x1, starting transfers between devices, local(): once_part = lax.ppermute(applied_once, both, spread_pairs)  4.03 us
    ppermute x1, starting transfers between devices, local(): start_rows = lax.ppermute(start_block, both, gather_pairs)  3.95 us
    ppermute x6, waiting for transfers between devices, row_swap(): return lax.ppermute(value, 'row', [(i, i ^ step) for i in range(row_count)])  3.9 us
    ppermute x1, waiting for transfers between devices, local(): start_rows = lax.ppermute(start_block, both, gather_pairs)  3.26 us
    ppermute x1, waiting for transfers between devices, local(): term = forward + lax.ppermute(backward, both, gather_pairs)  2.6 us
  transfers between devices with their start and end apart: 16, of which 11 were waited for; matrix products, arithmetic and copies ran while one was open for 0% of the time, Pallas kernels for 4%

profile of v2, /device:TPU:0, one launch (start us, length us, event | category | flops | bytes accessed | tf_op | source)
XLA Modules:
  0.0 47.6 jit_solution(5950891370232399297)
XLA Ops:
  0.6 3.9 %collective-permute-start = (bf16[16,1024]{1,0:T(8,128)(2,1)}, bf16[16,1024]{1,0:T(8,128)(2,1)S(1)}, u32[]{:S(2)}, u32[]{:S(2)}) collective-permute-start(bf16[16,1024]{1,0:T(8,128)(2,1)} %start_ref.1), channel_id=1, source_target_pairs={{24,0},{28,4},{16,1},{20,5},{8,2},{12,6},{0,3},{4,7},{25,9},{29,13... | collective-permute-start | bytes 98312 | tf_op jit(solution)/shard_map/ppermute | solution.py:242
  4.6 3.3 %collective-permute-done.source_ref = bf16[16,1024]{1,0:T(8,128)(2,1)S(1)} collective-permute-done((bf16[16,1024]{1,0:T(8,128)(2,1)}, bf16[16,1024]{1,0:T(8,128)(2,1)S(1)}, u32[]{:S(2)}, u32[]{:S(2)}) %collective-permute-start) | collective-permute-done | bytes 32800 | tf_op jit(solution)/shard_map/ppermute | solution.py:242
  8.5 1.0 %copy-done = bf16[1,1,12,128,128]{4,3,2,1,0:T(8,128)(2,1)S(1)} copy-done((bf16[1,1,12,128,128]{4,3,2,1,0:T(8,128)(2,1)S(1)}, bf16[1,1,12,128,128]{4,3,2,1,0:T(8,128)(2,1)}, u32[]{:S(2)}) %copy-start) | copy-done | bytes 393240
  10.4 1.2 %collective-permute-done.1 = f32[16,512]{1,0:T(8,128)S(1)} collective-permute-done((f32[16,512]{1,0:T(8,128)S(1)}, f32[16,512]{1,0:T(8,128)S(1)}, u32[]{:S(2)}, u32[]{:S(2)}) %collective-permute-start.1) | collective-permute-done | bytes 32800 | tf_op jit(solution)/shard_map/ppermute | solution.py:208
  11.6 2.3 %collective-permute-start.2 = (f32[16,512]{1,0:T(8,128)S(1)}, f32[16,512]{1,0:T(8,128)S(1)}, u32[]{:S(2)}, u32[]{:S(2)}) collective-permute-start(f32[16,512]{1,0:T(8,128)S(1)} %add.38), channel_id=1, source_target_pairs={{24,0},{28,4},{16,1},{20,5},{8,2},{12,6},{0,3},{4,7},{25,9},{29,13... | collective-permute-start | bytes 98312 | tf_op jit(solution)/shard_map/ppermute | solution.py:247
  13.9 0.9 %shard_map.75 = f32[16,512]{1,0:T(8,128)S(1)} custom-call(s32[12]{0:T(128)S(1)} %bitcast.9, s32[4]{0:T(128)S(1)} %bitcast.13, bf16[16,1024]{1,0:T(8,128)(2,1)S(1)} %copy-done.2, bf16[12,128,128]{2,1,0:T(8,128)(2,1)S(1)} %bitcast.5), custom_call_target="tpu_custom_call" | custom-call | flops 6291456 | bytes 393216 | tf_op jit(solution)/shard_map/pallas_call | solution.py:243
  14.7 2.6 %collective-permute-done.2 = f32[16,512]{1,0:T(8,128)S(1)} collective-permute-done((f32[16,512]{1,0:T(8,128)S(1)}, f32[16,512]{1,0:T(8,128)S(1)}, u32[]{:S(2)}, u32[]{:S(2)}) %collective-permute-start.2) | collective-permute-done | bytes 32800 | tf_op jit(solution)/shard_map/ppermute | solution.py:247
  17.3 2.1 %collective-permute-start.5 = (f32[16,512]{1,0:T(8,128)S(1)}, f32[16,512]{1,0:T(8,128)S(1)}, u32[]{:S(2)}, u32[]{:S(2)}) collective-permute-start(f32[16,512]{1,0:T(8,128)S(1)} %add.39), channel_id=1, source_target_pairs={{0,3},{1,2},{2,1},{3,0},{4,7},{5,6},{6,5},{7,4},{8,11},{9,10},{10,... | collective-permute-start | bytes 98312 | tf_op jit(solution)/shard_map/ppermute | solution.py:212
  19.5 1.1 %collective-permute-start.4 = (f32[16,512]{1,0:T(8,128)S(1)}, f32[16,512]{1,0:T(8,128)S(1)}, u32[]{:S(2)}, u32[]{:S(2)}) collective-permute-start(f32[16,512]{1,0:T(8,128)S(1)} %add.39), channel_id=1, source_target_pairs={{0,2},{1,3},{2,0},{3,1},{4,6},{5,7},{6,4},{7,5},{8,10},{9,11},{10,... | collective-permute-start | bytes 98312 | tf_op jit(solution)/shard_map/ppermute | solution.py:212
  20.9 1.3 %collective-permute-done.5 = f32[16,512]{1,0:T(8,128)S(1)} collective-permute-done((f32[16,512]{1,0:T(8,128)S(1)}, f32[16,512]{1,0:T(8,128)S(1)}, u32[]{:S(2)}, u32[]{:S(2)}) %collective-permute-start.5) | collective-permute-done | bytes 32800 | tf_op jit(solution)/shard_map/ppermute | solution.py:212
  22.2 1.2 %collective-permute-done.4 = f32[16,512]{1,0:T(8,128)S(1)} collective-permute-done((f32[16,512]{1,0:T(8,128)S(1)}, f32[16,512]{1,0:T(8,128)S(1)}, u32[]{:S(2)}, u32[]{:S(2)}) %collective-permute-start.4) | collective-permute-done | bytes 32800 | tf_op jit(solution)/shard_map/ppermute | solution.py:212
  23.4 1.1 %collective-permute-done.3 = f32[16,512]{1,0:T(8,128)S(1)} collective-permute-done((f32[16,512]{1,0:T(8,128)S(1)}, f32[16,512]{1,0:T(8,128)S(1)}, u32[]{:S(2)}, u32[]{:S(2)}) %collective-permute-start.3) | collective-permute-done | bytes 32800 | tf_op jit(solution)/shard_map/ppermute | solution.py:212
  24.6 0.8 %shard_map.77 = (f32[16,512]{1,0:T(8,128)S(1)}, f32[16,512]{1,0:T(8,128)S(1)}) custom-call(s32[12]{0:T(128)S(1)} %bitcast.10, s32[4]{0:T(128)S(1)} %bitcast.14, s32[1]{0:T(128)} %bitcast.3.turn_ref, bf16[16,512]{1,0:T(8,128)(2,1)S(1)} %add_convert_fusion.source_ref, bf16[12,128,128]{2,1,0:T(8,128)(2,1)S(1)} %bitcast.6), custom_call_target="tpu_custom_call" | custom-call | flops 6291456 | bytes 393216 | tf_op jit(solution)/shard_map/pallas_call | solution.py:222
  25.4 4.0 %collective-permute-start.6 = (bf16[16,512]{1,0:T(8,128)(2,1)S(1)}, bf16[16,512]{1,0:T(8,128)(2,1)S(1)}, u32[]{:S(2)}, u32[]{:S(2)}) collective-permute-start(bf16[16,512]{1,0:T(8,128)(2,1)S(1)} %add_convert_fusion.source_ref), channel_id=1, source_target_pairs={{0,24},{4,28},{1,16},{5,20},{2,8},{6,12},{3,0},{7,4},{9,25},{13,29... | collective-permute-start | bytes 49160 | tf_op jit(solution)/shard_map/ppermute | solution.py:253
  29.5 1.4 %collective-permute-done.6.once_ref = bf16[16,512]{1,0:T(8,128)(2,1)S(1)} collective-permute-done((bf16[16,512]{1,0:T(8,128)(2,1)S(1)}, bf16[16,512]{1,0:T(8,128)(2,1)S(1)}, u32[]{:S(2)}, u32[]{:S(2)}) %collective-permute-start.6) | collective-permute-done | bytes 16416 | tf_op jit(solution)/shard_map/ppermute | solution.py:253
  31.2 1.9 %collective-permute-start.9 = (f32[16,512]{1,0:T(8,128)S(1)}, f32[16,512]{1,0:T(8,128)S(1)}, u32[]{:S(2)}, u32[]{:S(2)}) collective-permute-start(f32[16,512]{1,0:T(8,128)S(1)} %add.43.backward_ref), channel_id=1, source_target_pairs={{24,0},{28,4},{16,1},{20,5},{8,2},{12,6},{0,3},{4,7},{25,9},{29,13... | collective-permute-start | bytes 98312 | tf_op jit(solution)/shard_map/ppermute | solution.py:255
  33.1 3.4 %collective-permute-start.12 = (f32[16,128]{1,0:T(8,128)S(1)}, f32[16,128]{1,0:T(8,128)S(1)}, u32[]{:S(2)}, u32[]{:S(2)}) collective-permute-start(f32[16,128]{1,0:T(8,128)S(1)} %slice_add_fusion), channel_id=1, source_target_pairs={{0,24},{4,28},{8,16},{12,20},{16,8},{20,12},{24,0},{28,4},{1,25},{... | collective-permute-start | bytes 24584 | tf_op jit(solution)/shard_map/ppermute | solution.py:208
  36.5 1.0 %collective-permute-start.10 = (f32[16,128]{1,0:T(8,128)S(1)}, f32[16,128]{1,0:T(8,128)S(1)}, u32[]{:S(2)}, u32[]{:S(2)}) collective-permute-start(f32[16,128]{1,0:T(8,128)S(1)} %slice_add_fusion), channel_id=1, source_target_pairs={{0,8},{4,12},{8,0},{12,4},{16,24},{20,28},{24,16},{28,20},{1,9},{5... | collective-permute-start | bytes 24584 | tf_op jit(solution)/shard_map/ppermute | solution.py:208
  37.5 0.9 %shard_map.79 = f32[16,512]{1,0:T(8,128)S(1)} custom-call(s32[12]{0:T(128)S(1)} %bitcast.11, s32[4]{0:T(128)S(1)} %bitcast.15, s32[1]{0:T(128)} %bitcast.3.turn_ref, bf16[12,128,128]{2,1,0:T(8,128)(2,1)S(1)} %bitcast.7, f32[16,640]{1,0:T(8,128)S(1)} %shard_map.78.rest_0_, f32[16,640]{1,0:T(8,128)S(1)} %collective-permute-done.8.rest_1_), custom_call_target="tpu_custom_call" | custom-call | flops 6291456 | bytes 393216 | tf_op jit(solution)/shard_map/pallas_call | solution.py:266
  38.5 2.5 %collective-permute-done.11 = f32[16,128]{1,0:T(8,128)S(1)} collective-permute-done((f32[16,128]{1,0:T(8,128)S(1)}, f32[16,128]{1,0:T(8,128)S(1)}, u32[]{:S(2)}, u32[]{:S(2)}) %collective-permute-start.11) | collective-permute-done | bytes 8224 | tf_op jit(solution)/shard_map/ppermute | solution.py:208
  41.1 1.8 %collective-permute-start.15 = (f32[16,640]{1,0:T(8,128)S(1)}, f32[16,640]{1,0:T(8,128)S(1)}, u32[]{:S(2)}, u32[]{:S(2)}) collective-permute-start(f32[16,640]{1,0:T(8,128)S(1)} %pad_maximum_fusion.refs_0_), channel_id=1, source_target_pairs={{0,3},{1,2},{2,1},{3,0},{4,7},{5,6},{6,5},{7,4},{8,11},{9,10},{10,... | collective-permute-start | bytes 122888 | tf_op jit(solution)/shard_map/ppermute | solution.py:212
  42.9 1.7 %collective-permute-start.13 = (f32[16,640]{1,0:T(8,128)S(1)}, f32[16,640]{1,0:T(8,128)S(1)}, u32[]{:S(2)}, u32[]{:S(2)}) collective-permute-start(f32[16,640]{1,0:T(8,128)S(1)} %pad_maximum_fusion.refs_0_), channel_id=1, source_target_pairs={{0,1},{1,0},{2,3},{3,2},{4,5},{5,4},{6,7},{7,6},{8,9},{9,8},{10,11... | collective-permute-start | bytes 122888 | tf_op jit(solution)/shard_map/ppermute | solution.py:212
  44.6 1.4 %collective-permute-done.15.refs_3_ = f32[16,640]{1,0:T(8,128)S(1)} collective-permute-done((f32[16,640]{1,0:T(8,128)S(1)}, f32[16,640]{1,0:T(8,128)S(1)}, u32[]{:S(2)}, u32[]{:S(2)}) %collective-permute-start.15) | collective-permute-done | bytes 40992 | tf_op jit(solution)/shard_map/ppermute | solution.py:212
  46.0 0.9 %collective-permute-done.14.refs_2_ = f32[16,640]{1,0:T(8,128)S(1)} collective-permute-done((f32[16,640]{1,0:T(8,128)S(1)}, f32[16,640]{1,0:T(8,128)S(1)}, u32[]{:S(2)}, u32[]{:S(2)}) %collective-permute-start.14) | collective-permute-done | bytes 40992 | tf_op jit(solution)/shard_map/ppermute | solution.py:212
  (34 shorter events, 3.1 us)
Async XLA Ops:
  0.6 7.2 %collective-permute-start = (bf16[16,1024]{1,0:T(8,128)(2,1)}, bf16[16,1024]{1,0:T(8,128)(2,1)S(1)}, u32[]{:S(2)}, u32[]{:S(2)}) collective-permute-start(bf16[16,1024]{1,0:T(8,128)(2,1)} %start_ref.1), channel_id=1, source_target_pairs={{24,0},{28,4},{16,1},{20,5},{8,2},{12,6},{0,3},{4,7},{25,9},{29,13... | collective-permute-start | bytes 98312 | tf_op jit(solution)/shard_map/ppermute | solution.py:242
  7.8 0.7 %copy-start.4 = (s32[1,1,12]{2,1,0:T(1,128)S(1)}, s32[1,1,12]{2,1,0:T(1,128)}, u32[]{:S(2)}) copy-start(s32[1,1,12]{2,1,0:T(1,128)} %param.6) | copy-start | bytes 148
  7.8 0.7 %copy-start.5 = (s32[1,1,4]{2,1,0:T(1,128)S(1)}, s32[1,1,4]{2,1,0:T(1,128)}, u32[]{:S(2)}) copy-start(s32[1,1,4]{2,1,0:T(1,128)} %param.7) | copy-start | bytes 52
  8.5 1.0 %copy-start = (bf16[1,1,12,128,128]{4,3,2,1,0:T(8,128)(2,1)S(1)}, bf16[1,1,12,128,128]{4,3,2,1,0:T(8,128)(2,1)}, u32[]{:S(2)}) copy-start(bf16[1,1,12,128,128]{4,3,2,1,0:T(8,128)(2,1)} %param.5) | copy-start | bytes 1179652
  9.5 4.4 %copy-start.1 = (bf16[1,1,12,128,128]{4,3,2,1,0:T(8,128)(2,1)S(1)}, bf16[1,1,12,128,128]{4,3,2,1,0:T(8,128)(2,1)}, u32[]{:S(2)}) copy-start(bf16[1,1,12,128,128]{4,3,2,1,0:T(8,128)(2,1)} %param.5) | copy-start | bytes 1179652
  10.3 1.3 %collective-permute-start.1 = (f32[16,512]{1,0:T(8,128)S(1)}, f32[16,512]{1,0:T(8,128)S(1)}, u32[]{:S(2)}, u32[]{:S(2)}) collective-permute-start(f32[16,512]{1,0:T(8,128)S(1)} %get-tuple-element.12), channel_id=1, source_target_pairs={{0,4},{4,0},{8,12},{12,8},{16,20},{20,16},{24,28},{28,24},{1,5},{5... | collective-permute-start | bytes 98312 | tf_op jit(solution)/shard_map/ppermute | solution.py:208
  11.6 2.3 %copy-start.2 = (bf16[16,1024]{1,0:T(8,128)(2,1)S(1)}, bf16[16,1024]{1,0:T(8,128)(2,1)}, u32[]{:S(2)}) copy-start(bf16[16,1024]{1,0:T(8,128)(2,1)} %start_ref.1) | copy-start | bytes 98308
  11.6 5.8 %collective-permute-start.2 = (f32[16,512]{1,0:T(8,128)S(1)}, f32[16,512]{1,0:T(8,128)S(1)}, u32[]{:S(2)}, u32[]{:S(2)}) collective-permute-start(f32[16,512]{1,0:T(8,128)S(1)} %add.38), channel_id=1, source_target_pairs={{24,0},{28,4},{16,1},{20,5},{8,2},{12,6},{0,3},{4,7},{25,9},{29,13... | collective-permute-start | bytes 98312 | tf_op jit(solution)/shard_map/ppermute | solution.py:247
  17.3 4.8 %collective-permute-start.5 = (f32[16,512]{1,0:T(8,128)S(1)}, f32[16,512]{1,0:T(8,128)S(1)}, u32[]{:S(2)}, u32[]{:S(2)}) collective-permute-start(f32[16,512]{1,0:T(8,128)S(1)} %add.39), channel_id=1, source_target_pairs={{0,3},{1,2},{2,1},{3,0},{4,7},{5,6},{6,5},{7,4},{8,11},{9,10},{10,... | collective-permute-start | bytes 98312 | tf_op jit(solution)/shard_map/ppermute | solution.py:212
  19.5 3.9 %collective-permute-start.4 = (f32[16,512]{1,0:T(8,128)S(1)}, f32[16,512]{1,0:T(8,128)S(1)}, u32[]{:S(2)}, u32[]{:S(2)}) collective-permute-start(f32[16,512]{1,0:T(8,128)S(1)} %add.39), channel_id=1, source_target_pairs={{0,2},{1,3},{2,0},{3,1},{4,6},{5,7},{6,4},{7,5},{8,10},{9,11},{10,... | collective-permute-start | bytes 98312 | tf_op jit(solution)/shard_map/ppermute | solution.py:212
  20.6 3.9 %collective-permute-start.3 = (f32[16,512]{1,0:T(8,128)S(1)}, f32[16,512]{1,0:T(8,128)S(1)}, u32[]{:S(2)}, u32[]{:S(2)}) collective-permute-start(f32[16,512]{1,0:T(8,128)S(1)} %add.39), channel_id=1, source_target_pairs={{0,1},{1,0},{2,3},{3,2},{4,5},{5,4},{6,7},{7,6},{8,9},{9,8},{10,11... | collective-permute-start | bytes 98312 | tf_op jit(solution)/shard_map/ppermute | solution.py:212
  24.6 0.9 %copy-start.3 = (bf16[16,512]{1,0:T(8,128)(2,1)}, bf16[16,512]{1,0:T(8,128)(2,1)S(1)}, u32[]{:S(2)}) copy-start(bf16[16,512]{1,0:T(8,128)(2,1)S(1)} %add_convert_fusion.source_ref) | copy-start | bytes 49156
  25.3 4.1 %collective-permute-start.7 = (f32[16,512]{1,0:T(8,128)S(1)}, f32[16,512]{1,0:T(8,128)S(1)}, u32[]{:S(2)}, u32[]{:S(2)}) collective-permute-start(f32[16,512]{1,0:T(8,128)S(1)} %get-tuple-element.14), channel_id=1, source_target_pairs={{0,4},{4,0},{8,12},{12,8},{16,20},{20,16},{24,28},{28,24},{1,5},{5... | collective-permute-start | bytes 98312 | tf_op jit(solution)/shard_map/ppermute | solution.py:208
  25.4 5.5 %collective-permute-start.6 = (bf16[16,512]{1,0:T(8,128)(2,1)S(1)}, bf16[16,512]{1,0:T(8,128)(2,1)S(1)}, u32[]{:S(2)}, u32[]{:S(2)}) collective-permute-start(bf16[16,512]{1,0:T(8,128)(2,1)S(1)} %add_convert_fusion.source_ref), channel_id=1, source_target_pairs={{0,24},{4,28},{1,16},{5,20},{2,8},{6,12},{3,0},{7,4},{9,25},{13,29... | collective-permute-start | bytes 49160 | tf_op jit(solution)/shard_map/ppermute | solution.py:253
  31.2 1.9 %collective-permute-start.8 = (f32[16,640]{1,0:T(8,128)S(1)}, f32[16,640]{1,0:T(8,128)S(1)}, u32[]{:S(2)}, u32[]{:S(2)}) collective-permute-start(f32[16,640]{1,0:T(8,128)S(1)} %shard_map.78.rest_0_), channel_id=1, source_target_pairs={{0,4},{4,0},{8,12},{12,8},{16,20},{20,16},{24,28},{28,24},{1,5},{5... | collective-permute-start | bytes 122888 | tf_op jit(solution)/shard_map/ppermute | solution.py:208
  31.2 7.1 %collective-permute-start.9 = (f32[16,512]{1,0:T(8,128)S(1)}, f32[16,512]{1,0:T(8,128)S(1)}, u32[]{:S(2)}, u32[]{:S(2)}) collective-permute-start(f32[16,512]{1,0:T(8,128)S(1)} %add.43.backward_ref), channel_id=1, source_target_pairs={{24,0},{28,4},{16,1},{20,5},{8,2},{12,6},{0,3},{4,7},{25,9},{29,13... | collective-permute-start | bytes 98312 | tf_op jit(solution)/shard_map/ppermute | solution.py:255
  33.1 5.4 %collective-permute-start.12 = (f32[16,128]{1,0:T(8,128)S(1)}, f32[16,128]{1,0:T(8,128)S(1)}, u32[]{:S(2)}, u32[]{:S(2)}) collective-permute-start(f32[16,128]{1,0:T(8,128)S(1)} %slice_add_fusion), channel_id=1, source_target_pairs={{0,24},{4,28},{8,16},{12,20},{16,8},{20,12},{24,0},{28,4},{1,25},{... | collective-permute-start | bytes 24584 | tf_op jit(solution)/shard_map/ppermute | solution.py:208
  36.5 4.5 %collective-permute-start.11 = (f32[16,128]{1,0:T(8,128)S(1)}, f32[16,128]{1,0:T(8,128)S(1)}, u32[]{:S(2)}, u32[]{:S(2)}) collective-permute-start(f32[16,128]{1,0:T(8,128)S(1)} %slice_add_fusion), channel_id=1, source_target_pairs={{0,16},{4,20},{8,24},{12,28},{16,0},{20,4},{24,8},{28,12},{1,17},{... | collective-permute-start | bytes 24584 | tf_op jit(solution)/shard_map/ppermute | solution.py:208
  36.5 4.5 %collective-permute-start.10 = (f32[16,128]{1,0:T(8,128)S(1)}, f32[16,128]{1,0:T(8,128)S(1)}, u32[]{:S(2)}, u32[]{:S(2)}) collective-permute-start(f32[16,128]{1,0:T(8,128)S(1)} %slice_add_fusion), channel_id=1, source_target_pairs={{0,8},{4,12},{8,0},{12,4},{16,24},{20,28},{24,16},{28,20},{1,9},{5... | collective-permute-start | bytes 24584 | tf_op jit(solution)/shard_map/ppermute | solution.py:208
  41.1 5.0 %collective-permute-start.15 = (f32[16,640]{1,0:T(8,128)S(1)}, f32[16,640]{1,0:T(8,128)S(1)}, u32[]{:S(2)}, u32[]{:S(2)}) collective-permute-start(f32[16,640]{1,0:T(8,128)S(1)} %pad_maximum_fusion.refs_0_), channel_id=1, source_target_pairs={{0,3},{1,2},{2,1},{3,0},{4,7},{5,6},{6,5},{7,4},{8,11},{9,10},{10,... | collective-permute-start | bytes 122888 | tf_op jit(solution)/shard_map/ppermute | solution.py:212
  42.9 4.0 %collective-permute-start.14 = (f32[16,640]{1,0:T(8,128)S(1)}, f32[16,640]{1,0:T(8,128)S(1)}, u32[]{:S(2)}, u32[]{:S(2)}) collective-permute-start(f32[16,640]{1,0:T(8,128)S(1)} %pad_maximum_fusion.refs_0_), channel_id=1, source_target_pairs={{0,2},{1,3},{2,0},{3,1},{4,6},{5,7},{6,4},{7,5},{8,10},{9,11},{10,... | collective-permute-start | bytes 122888 | tf_op jit(solution)/shard_map/ppermute | solution.py:212
  42.9 4.0 %collective-permute-start.13 = (f32[16,640]{1,0:T(8,128)S(1)}, f32[16,640]{1,0:T(8,128)S(1)}, u32[]{:S(2)}, u32[]{:S(2)}) collective-permute-start(f32[16,640]{1,0:T(8,128)S(1)} %pad_maximum_fusion.refs_0_), channel_id=1, source_target_pairs={{0,1},{1,0},{2,3},{3,2},{4,5},{5,4},{6,7},{7,6},{8,9},{9,8},{10,11... | collective-permute-start | bytes 122888 | tf_op jit(solution)/shard_map/ppermute | solution.py:212

commit v3 on v0

v3 whole, which is shorter than its diff:
```python
import functools

import jax
import jax.numpy as jnp
from jax import lax
from jax.experimental import pallas as pl
from jax.experimental.pallas import tpu as pltpu
from jax.sharding import PartitionSpec as P

highest = lax.Precision.HIGHEST
both = ("row", "col")
f32 = jnp.float32
vmem = pl.BlockSpec(memory_space=pltpu.VMEM)
smem = pl.BlockSpec(memory_space=pltpu.SMEM)


def call(kernel, out_shape, in_specs, scratch=(), flops=0, bytes_accessed=0):
    room = 2 * bytes_accessed + (1 << 20)
    return pl.pallas_call(
        kernel,
        out_shape=out_shape,
        in_specs=in_specs,
        out_specs=jax.tree.map(lambda _: vmem, out_shape),
        scratch_shapes=scratch,
        compiler_params=pltpu.CompilerParams(vmem_limit_bytes=room),
        cost_estimate=pl.CostEstimate(
            flops=flops, bytes_accessed=bytes_accessed, transcendentals=0
        ),
    )


def products(columns_ref, counts_ref, values_ref, first_row, product, sums, into):
    row_blocks = counts_ref.shape[0]
    block_total = values_ref.shape[0]
    if block_total <= 16:
        ends = [counts_ref[0]]
        for index in range(1, row_blocks - 1):
            ends.append(ends[-1] + counts_ref[index])
        found = []
        for block in range(block_total):
            row = first_row + sum((block >= end).astype(jnp.int32) for end in ends)
            column = columns_ref[block]
            found.append((into(row, column), product(values_ref[block], row, column)))
        for place, value in found:
            sums[place] += value
        return

    def step(block, carry):
        row, end = carry
        later = block >= end
        row = jnp.minimum(row + later.astype(jnp.int32), row_blocks - 1)
        end = end + jnp.where(later, counts_ref[row], 0)
        column = columns_ref[block]
        place = into(first_row + row, column)
        sums[place] += product(values_ref[block], first_row + row, column)
        return row, end

    lax.fori_loop(0, block_total, step, (jnp.int32(0), counts_ref[0]))


def split_into(pieces, source_ref):
    size = pieces.shape[2]
    for index in range(pieces.shape[0]):
        pieces[index] = source_ref[:, index * size : (index + 1) * size]


def forward_kernel(columns_ref, counts_ref, values_ref, source_ref, *refs):
    term_refs, (out_ref, pieces, sums) = refs[:-3], refs[-3:]
    split_into(pieces, source_ref)
    if term_refs:
        split_into(sums, term_refs[0])
    else:
        sums[...] = jnp.zeros_like(sums)

    def product(block, row, column):
        return lax.dot_general(
            pieces[column], block, (((1,), (1,)), ((), ())), preferred_element_type=f32
        )

    products(columns_ref, counts_ref, values_ref, 0, product, sums, lambda row, column: row)
    size = sums.shape[2]
    for index in range(sums.shape[0]):
        out_ref[:, index * size : (index + 1) * size] = sums[index]


def backward_kernel(tiles, mask, turn_ref, *refs):
    columns, counts, values = refs[:tiles], refs[tiles : 2 * tiles], refs[2 * tiles : 3 * tiles]
    source_ref, *out_refs = refs[3 * tiles : -2]
    pieces, sums = refs[-2:]
    size = sums.shape[3]
    row_blocks = counts[0].shape[0]
    split_into(pieces, source_ref)
    sums[...] = jnp.zeros_like(sums)

    def product(block, row, column):
        return jnp.dot(pieces[row], block, preferred_element_type=f32)

    for tile in range(tiles):
        products(
            columns[tile],
            counts[tile],
            values[tile],
            jnp.bitwise_xor(turn_ref[0], tile) * row_blocks,
            product,
            sums.at[tile],
            lambda row, column: column,
        )

    def total(index):
        return xor_sum(sums[0, index], [sums[tile, index] for tile in range(1, tiles)])

    first = jnp.bitwise_xor(turn_ref[0], mask) * row_blocks
    for index in range(row_blocks):
        out_refs[0][:, index * size : (index + 1) * size] = total(first + index)
    for out_ref in out_refs[1:]:
        for index in range(sums.shape[1]):
            out_ref[:, index * size : (index + 1) * size] = total(index)


def gram_kernel(scale, start_ref, once_ref, backward_ref, out_ref):
    vectors = once_ref.shape[0]
    once = once_ref[...]
    gram = functools.partial(
        lax.dot_general,
        dimension_numbers=(((1,), (1,)), ((), ())),
        preferred_element_type=f32,
    )
    basis = jnp.concatenate([start_ref[...], once], axis=0)
    square = gram(basis, basis) * scale
    wide = once.astype(f32)
    backward = backward_ref[...]
    cross = gram(wide, backward, precision=highest) + gram(backward, wide, precision=highest)
    out_ref[...] = jnp.zeros_like(out_ref)
    out_ref[:, : 2 * vectors] = square[:vectors]
    out_ref[:, 2 * vectors : 4 * vectors] = square[vectors:]
    out_ref[:, 4 * vectors : 5 * vectors] = cross


def last_kernel(norm_scale, total_ref, twice_ref, basis_ref, projected_ref):
    vectors, width = twice_ref.shape
    twice_ref[...] = total_ref[:, :width].astype(twice_ref.dtype)
    grams = total_ref[:, width:] * norm_scale

    def tile(index, count=1):
        return grams[:, index * vectors : (index + count) * vectors]

    basis_ref[:vectors] = tile(0, 2)
    basis_ref[vectors:] = tile(2, 2)
    projected_ref[:vectors, :vectors] = tile(1)
    projected_ref[:vectors, vectors:] = tile(3)
    projected_ref[vectors:] = tile(3, 2)


def to_plane_of(col_count):
    pairs = []
    for column in range(col_count):
        planes = sorted(range(col_count), key=lambda a: -abs(a - column))
        places = sorted(range(col_count), key=lambda c: bin(c ^ column).count("1"))
        pairs += [((plane, column), (column, place)) for plane, place in zip(planes, places)]
    return pairs


def xor_sum(value, others):
    level = [value, *others]
    while len(level) > 1:
        level = [level[i] + level[i + 1] for i in range(0, len(level), 2)]
    return level[0]


def local(start_block, block_values, block_columns, block_counts):
    row_count, col_count = lax.axis_size("row"), lax.axis_size("col")
    ratio = row_count // col_count
    values = block_values[0, 0]
    columns = block_columns[0, 0]
    counts = block_counts[0, 0]
    block_total, block_size = values.shape[:2]
    row_blocks = counts.shape[0]
    row_width = row_blocks * block_size
    vectors, col_width = start_block.shape
    col_blocks = col_width // block_size
    turn = lax.axis_index("row") % ratio
    norm_scale = 1.0 / (row_width * row_count)
    few = col_count <= 8
    crossed = few and ratio > 1
    grid = range(col_count)
    chips = [(plane, column) for plane in grid for column in grid]
    opposite = ratio - 1

    def send(value, pairs, mask=opposite):
        def device(plane, column, member):
            return (plane * ratio + member) * col_count + column

        return lax.ppermute(
            value,
            both,
            [
                (device(*source, member), device(*target, member ^ mask))
                for source, target in pairs
                for member in range(ratio)
            ],
        )

    gather_pairs = to_plane_of(col_count)
    spread_pairs = [(target, source) for source, target in gather_pairs]
    stay = [(chip, chip) for chip in chips]

    def of_chip(value):
        return [value] + [send(value, stay, step) for step in range(1, ratio)]

    def col_sum(value):
        if not few:
            return lax.psum(value, "col")
        mask = opposite if crossed else 0
        own = send(value, stay, mask) if crossed else value
        steps = range(1, col_count)
        return xor_sum(
            own, [send(value, [((a, c), (a, c ^ step)) for a, c in chips], mask) for step in steps]
        )

    def plane_sum(value):
        if not few:
            return lax.psum(value, "row") * (1.0 / ratio)
        steps = range(1, col_count)
        return xor_sum(
            value, [send(value, [((a, c), (a ^ step, c)) for a, c in chips]) for step in steps]
        )

    def whole_slab(part):
        parts = of_chip(part)
        slab = []
        for place in range(ratio):
            piece = parts[0]
            for step in range(1, ratio):
                piece = jnp.where(turn == (place ^ step), parts[step], piece)
            slab.append(piece)
        return jnp.concatenate(slab, axis=1)

    tiles = [of_chip(columns), of_chip(counts), of_chip(values)]
    flops = 2 * vectors * block_total * block_size**2
    bytes_accessed = 2 * block_total * block_size**2
    part_shape = jax.ShapeDtypeStruct((vectors, row_width), f32)
    slab_shape = jax.ShapeDtypeStruct((vectors, col_width), f32)
    pieces = pltpu.VMEM((col_blocks, vectors, block_size), start_block.dtype)

    def forward_of(source, *term):
        tile = [arrays[opposite if crossed else 0] for arrays in tiles]
        return call(
            forward_kernel,
            part_shape,
            [smem] * 2 + [vmem] * (2 + len(term)),
            [pieces, pltpu.VMEM((row_blocks, vectors, block_size), f32)],
            flops,
            bytes_accessed,
        )(*tile, source, *term)

    def backward_of(source, outputs):
        return call(
            functools.partial(backward_kernel, ratio, 0 if crossed else opposite),
            [part_shape, slab_shape][:outputs],
            [smem] * (2 * ratio + 1) + [vmem] * (ratio + 1),
            [pieces, pltpu.VMEM((ratio, col_blocks, vectors, block_size), f32)],
            ratio * flops,
            ratio * bytes_accessed,
        )(turn.reshape(1), *tiles[0], *tiles[1], *tiles[2], source)

    start_rows = send(start_block, gather_pairs)
    forward = forward_of(start_block)
    start_rows, forward = lax.optimization_barrier((start_rows, forward))
    backward = send(backward_of(start_rows, 1)[0], gather_pairs)
    applied_once = col_sum(forward + backward).astype(jnp.bfloat16)

    once = whole_slab(applied_once)
    once_columns = send(once, spread_pairs)
    backward, backward_whole = backward_of(once, 2)
    backward = send(backward, gather_pairs)
    grams = call(
        functools.partial(gram_kernel, 1.0 / col_count),
        jax.ShapeDtypeStruct((vectors, 128), f32),
        [vmem] * 3,
        (),
        8 * vectors * vectors * col_width,
        8 * vectors * col_width,
    )(start_block, once_columns, backward_whole)
    grams = plane_sum(grams)
    total = col_sum(jnp.concatenate([forward_of(once_columns, backward), grams], axis=1))
    small = jax.ShapeDtypeStruct((2 * vectors, 2 * vectors), f32)
    applied_twice, basis_gram, projected_gram = call(
        functools.partial(last_kernel, norm_scale),
        [jax.ShapeDtypeStruct((vectors, row_width), jnp.bfloat16), small, small],
        [vmem],
    )(total)
    return (applied_once, applied_twice, basis_gram, projected_gram)


def solution(mesh):
    return jax.shard_map(
        local,
        mesh=mesh,
        in_specs=(
            P(None, "col"),
            P("row", "col", None, None, None),
            P("row", "col", None),
            P("row", "col", None),
        ),
        out_specs=(P(None, "row"), P(None, "row"), P(), P()),
        check_vma=False,
    )
```

time: 241 us -> 40.2 us (0.17)
  blocking collectives: 115 us -> 0 us
  waiting for transfers between devices: 102 us -> 11.4 us
  starting transfers between devices: 0.08 us -> 21.9 us
  between operations: 14.3 us -> 0.73 us
  Pallas kernels: 0 us -> 4.57 us
  other arithmetic: 3.19 us -> 0.06 us
  local copies, waits for them, and re-layouts: 4.37 us -> 1.31 us
  matrix products: 2.45 us -> 0 us
    psum x5 -> x0, blocking collectives: 115 us -> none  [the longest x2 43.7 us: broadcast(): return lax.psum(block, axis)]
    psum x2 -> x0, waiting for transfers between devices: 102 us -> none  [apply_operator(): column_total = lax.psum(backward, 'row')]
    ppermute x0 -> x19, starting transfers between devices: none -> 21.9 us  [send(): lax.ppermute(value, both, [(device(*source, member), device(*target, memb...]
    ppermute x0 -> x19, waiting for transfers between devices: none -> 11.4 us  [send(): lax.ppermute(value, both, [(device(*source, member), device(*target, memb...]
    pallas_call x0 -> x6, Pallas kernels: none -> 4.57 us  [the longest x2 1.78 us: backward_of(): call(functools.partial(backward_kernel, ratio, 0 if crossed else opposite...]
    dot_general x12 -> x0, matrix products: 2.45 us -> none  [the longest x4 0.65 us: inner_products(): return jnp.dot(left_block, right_block.T, precision=highest)]
  transfers between devices with their start and end apart: 2 -> 19, of which waited for: 2 -> 12; matrix products, arithmetic and copies ran while one was open for 1% -> 0% of each run, Pallas kernels for 0% -> 8%
where the time goes in v3:
time: 40.2 us; the launch traced here: 40 us
  starting transfers between devices  21.9 us (54%)
  waiting for transfers between devices  11.4 us (28%)
  Pallas kernels  4.57 us (11%)
  local copies, waits for them, and re-layouts  1.31 us (3%)
  between operations  0.73 us (2%)
    ppermute x19, starting transfers between devices, send(): lax.ppermute(value, both, [(device(*source, member), device(*target, memb...  21.9 us
    ppermute x19, waiting for transfers between devices, send(): lax.ppermute(value, both, [(device(*source, member), device(*target, memb...  11.4 us
    pallas_call x2, Pallas kernels, backward_of(): call(functools.partial(backward_kernel, ratio, 0 if crossed else opposite...  1.78 us
    pallas_call x2, Pallas kernels, forward_of(): call(forward_kernel, part_shape, [smem] * 2 + [vmem] * (2 + len(term)), [...  1.72 us
    unnamed x12, local copies, waits for them, and re-layouts  1.31 us
  transfers between devices with their start and end apart: 19, of which 12 were waited for; matrix products, arithmetic and copies ran while one was open for 0% of the time, Pallas kernels for 8%

profile of v3, /device:TPU:0, one launch (start us, length us, event | category | flops | bytes accessed | tf_op | source)
XLA Modules:
  0.0 40.0 jit_solution(2011060672007509284)
XLA Ops:
  1.2 3.6 %collective-permute-start = (bf16[16,1024]{1,0:T(8,128)(2,1)}, bf16[16,1024]{1,0:T(8,128)(2,1)S(1)}, u32[]{:S(2)}, u32[]{:S(2)}) collective-permute-start(bf16[16,1024]{1,0:T(8,128)(2,1)} %start_ref.1), channel_id=1, source_target_pairs={{24,4},{28,0},{16,5},{20,1},{8,6},{12,2},{0,7},{4,3},{25,13},{29,9... | collective-permute-start | bytes 98312 | tf_op jit(solution)/shard_map/ppermute | solution.py:193
  5.2 1.0 %collective-permute-done.2.counts_ref.refs_3_ = s32[4]{0:T(128)S(1)} collective-permute-done((s32[4]{0:T(128)}, s32[4]{0:T(128)S(1)}, u32[]{:S(2)}, u32[]{:S(2)}) %collective-permute-start.2) | collective-permute-done | bytes 48 | tf_op jit(solution)/shard_map/ppermute | solution.py:193
  6.2 0.8 %copy-done.1 = bf16[16,1024]{1,0:T(8,128)(2,1)S(1)} copy-done((bf16[16,1024]{1,0:T(8,128)(2,1)S(1)}, bf16[16,1024]{1,0:T(8,128)(2,1)}, u32[]{:S(2)}) %copy-start.1) | copy-done | bytes 32792
  6.9 0.9 %shard_map.75 = f32[16,512]{1,0:T(8,128)S(1)} custom-call(s32[12]{0:T(128)S(1)} %collective-permute-done.1.columns_ref.refs_1_, s32[4]{0:T(128)S(1)} %collective-permute-done.2.counts_ref.refs_3_, bf16[12,128,128]{2,1,0:T(8,128)(2,1)S(1)} %collective-permute-done.3.values_ref.refs_5_, bf16[16,1024]{1,0:T(8,128)(2,1)S(1)} %copy-done.1), custom_call_target="tpu_custom_call" | custom-call | flops 6291456 | bytes 393216 | tf_op jit(solution)/shard_map/pallas_call | solution.py:247
  8.5 0.9 %shard_map.76 = f32[16,512]{1,0:T(8,128)S(1)} custom-call(s32[1]{0:T(128)} %bitcast.3.turn_ref, s32[12]{0:T(128)S(1)} %bitcast.8, s32[12]{0:T(128)S(1)} %collective-permute-done.1.columns_ref.refs_1_, s32[4]{0:T(128)S(1)} %bitcast.11, s32[4]{0:T(128)S(1)} %collective-permute-done.2.counts_ref.refs_3_, bf16[12,128,128]{2,1,0:T(8,128)(2,1)S(1)} %bitcast.5, ...), custom_call_target="tpu_custom_call" | custom-call | flops 12582912 | bytes 786432 | tf_op jit(solution)/shard_map/pallas_call | solution.py:257
  9.4 3.6 %collective-permute-start.4 = (f32[16,512]{1,0:T(8,128)S(1)}, f32[16,512]{1,0:T(8,128)S(1)}, u32[]{:S(2)}, u32[]{:S(2)}) collective-permute-start(f32[16,512]{1,0:T(8,128)S(1)} %shard_map.76), channel_id=1, source_target_pairs={{24,4},{28,0},{16,5},{20,1},{8,6},{12,2},{0,7},{4,3},{25,13},{29,9... | collective-permute-start | bytes 98312 | tf_op jit(solution)/shard_map/ppermute | solution.py:193
  13.0 2.0 %collective-permute-done.4 = f32[16,512]{1,0:T(8,128)S(1)} collective-permute-done((f32[16,512]{1,0:T(8,128)S(1)}, f32[16,512]{1,0:T(8,128)S(1)}, u32[]{:S(2)}, u32[]{:S(2)}) %collective-permute-start.4) | collective-permute-done | bytes 32800 | tf_op jit(solution)/shard_map/ppermute | solution.py:193
  15.0 2.8 %collective-permute-start.8 = (f32[16,512]{1,0:T(8,128)S(1)}, f32[16,512]{1,0:T(8,128)S(1)}, u32[]{:S(2)}, u32[]{:S(2)}) collective-permute-start(f32[16,512]{1,0:T(8,128)S(1)} %add.35), channel_id=1, source_target_pairs={{0,7},{4,3},{1,6},{5,2},{2,5},{6,1},{3,4},{7,0},{8,15},{12,11},{9,... | collective-permute-start | bytes 98312 | tf_op jit(solution)/shard_map/ppermute | solution.py:193
  18.5 1.1 %collective-permute-done.8 = f32[16,512]{1,0:T(8,128)S(1)} collective-permute-done((f32[16,512]{1,0:T(8,128)S(1)}, f32[16,512]{1,0:T(8,128)S(1)}, u32[]{:S(2)}, u32[]{:S(2)}) %collective-permute-start.8) | collective-permute-done | bytes 32800 | tf_op jit(solution)/shard_map/ppermute | solution.py:193
  19.7 1.7 %collective-permute-done.7 = f32[16,512]{1,0:T(8,128)S(1)} collective-permute-done((f32[16,512]{1,0:T(8,128)S(1)}, f32[16,512]{1,0:T(8,128)S(1)}, u32[]{:S(2)}, u32[]{:S(2)}) %collective-permute-start.7) | collective-permute-done | bytes 32800 | tf_op jit(solution)/shard_map/ppermute | solution.py:193
  22.0 1.1 %collective-permute-done.9 = bf16[16,512]{1,0:T(8,128)(2,1)S(1)} collective-permute-done((bf16[16,512]{1,0:T(8,128)(2,1)S(1)}, bf16[16,512]{1,0:T(8,128)(2,1)S(1)}, u32[]{:S(2)}, u32[]{:S(2)}) %collective-permute-start.9) | collective-permute-done | bytes 16416 | tf_op jit(solution)/shard_map/ppermute | solution.py:193
  23.1 1.6 %collective-permute-start.10 = (bf16[16,1024]{1,0:T(8,128)(2,1)S(1)}, bf16[16,1024]{1,0:T(8,128)(2,1)S(1)}, u32[]{:S(2)}, u32[]{:S(2)}) collective-permute-start(bf16[16,1024]{1,0:T(8,128)(2,1)S(1)} %pad_maximum_fusion.1.refs_6_), channel_id=1, source_target_pairs={{0,28},{4,24},{1,20},{5,16},{2,12},{6,8},{3,4},{7,0},{9,29},{13,25... | collective-permute-start | bytes 98312 | tf_op jit(solution)/shard_map/ppermute | solution.py:193
  24.7 0.9 %shard_map.77 = (f32[16,512]{1,0:T(8,128)S(1)}, f32[16,1024]{1,0:T(8,128)S(1)}) custom-call(s32[1]{0:T(128)} %bitcast.3.turn_ref, s32[12]{0:T(128)S(1)} %bitcast.9, s32[12]{0:T(128)S(1)} %collective-permute-done.1.columns_ref.refs_1_, s32[4]{0:T(128)S(1)} %bitcast.12, s32[4]{0:T(128)S(1)} %collective-permute-done.2.counts_ref.refs_3_, ...), custom_call_target="tpu_custom_call" | custom-call | flops 12582912 | bytes 786432 | tf_op jit(solution)/shard_map/pallas_call | solution.py:257
  25.6 1.2 %collective-permute-start.11 = (f32[16,512]{1,0:T(8,128)S(1)}, f32[16,512]{1,0:T(8,128)S(1)}, u32[]{:S(2)}, u32[]{:S(2)}) collective-permute-start(f32[16,512]{1,0:T(8,128)S(1)} %get-tuple-element.13), channel_id=1, source_target_pairs={{24,4},{28,0},{16,5},{20,1},{8,6},{12,2},{0,7},{4,3},{25,13},{29,9... | collective-permute-start | bytes 98312 | tf_op jit(solution)/shard_map/ppermute | solution.py:193
  26.8 0.6 %collective-permute-done.10.source_ref.once_ref = bf16[16,1024]{1,0:T(8,128)(2,1)S(1)} collective-permute-done((bf16[16,1024]{1,0:T(8,128)(2,1)S(1)}, bf16[16,1024]{1,0:T(8,128)(2,1)S(1)}, u32[]{:S(2)}, u32[]{:S(2)}) %collective-permute-start.10) | collective-permute-done | bytes 32800 | tf_op jit(solution)/shard_map/ppermute | solution.py:193
  27.8 2.4 %collective-permute-start.14 = (f32[16,128]{1,0:T(8,128)S(1)}, f32[16,128]{1,0:T(8,128)S(1)}, u32[]{:S(2)}, u32[]{:S(2)}) collective-permute-start(f32[16,128]{1,0:T(8,128)S(1)} %shard_map.79), channel_id=1, source_target_pairs={{0,28},{4,24},{1,29},{5,25},{2,30},{6,26},{3,31},{7,27},{8,20},{12... | collective-permute-start | bytes 24584 | tf_op jit(solution)/shard_map/ppermute | solution.py:193
  30.3 1.5 %collective-permute-start.12 = (f32[16,128]{1,0:T(8,128)S(1)}, f32[16,128]{1,0:T(8,128)S(1)}, u32[]{:S(2)}, u32[]{:S(2)}) collective-permute-start(f32[16,128]{1,0:T(8,128)S(1)} %shard_map.79), channel_id=1, source_target_pairs={{0,12},{4,8},{1,13},{5,9},{2,14},{6,10},{3,15},{7,11},{8,4},{12,0}... | collective-permute-start | bytes 24584 | tf_op jit(solution)/shard_map/ppermute | solution.py:193
  31.7 0.9 %shard_map.78 = f32[16,512]{1,0:T(8,128)S(1)} custom-call(s32[12]{0:T(128)S(1)} %collective-permute-done.1.columns_ref.refs_1_, s32[4]{0:T(128)S(1)} %collective-permute-done.2.counts_ref.refs_3_, bf16[12,128,128]{2,1,0:T(8,128)(2,1)S(1)} %collective-permute-done.3.values_ref.refs_5_, bf16[16,1024]{1,0:T(8,128)(2,1)S(1)} %collective-permute-done.10.source_ref.once_ref, ...), custom_call_target="tpu_custom_call" | custom-call | flops 6291456 | bytes 393216 | tf_op jit(solution)/shard_map/pallas_call | solution.py:247
  32.7 1.5 %collective-permute-done.13 = f32[16,128]{1,0:T(8,128)S(1)} collective-permute-done((f32[16,128]{1,0:T(8,128)S(1)}, f32[16,128]{1,0:T(8,128)S(1)}, u32[]{:S(2)}, u32[]{:S(2)}) %collective-permute-start.13) | collective-permute-done | bytes 8224 | tf_op jit(solution)/shard_map/ppermute | solution.py:193
  34.3 0.7 %collective-permute-start.18 = (f32[16,640]{1,0:T(8,128)S(1)}, f32[16,640]{1,0:T(8,128)S(1)}, u32[]{:S(2)}, u32[]{:S(2)}) collective-permute-start(f32[16,640]{1,0:T(8,128)S(1)} %pad_maximum_fusion), channel_id=1, source_target_pairs={{0,7},{4,3},{1,6},{5,2},{2,5},{6,1},{3,4},{7,0},{8,15},{12,11},{9,... | collective-permute-start | bytes 122888 | tf_op jit(solution)/shard_map/ppermute | solution.py:193
  34.9 0.8 %collective-permute-start.17 = (f32[16,640]{1,0:T(8,128)S(1)}, f32[16,640]{1,0:T(8,128)S(1)}, u32[]{:S(2)}, u32[]{:S(2)}) collective-permute-start(f32[16,640]{1,0:T(8,128)S(1)} %pad_maximum_fusion), channel_id=1, source_target_pairs={{0,6},{4,2},{1,7},{5,3},{2,4},{6,0},{3,5},{7,1},{8,14},{12,10},{9,... | collective-permute-start | bytes 122888 | tf_op jit(solution)/shard_map/ppermute | solution.py:193
  35.8 1.6 %collective-permute-start.16 = (f32[16,640]{1,0:T(8,128)S(1)}, f32[16,640]{1,0:T(8,128)S(1)}, u32[]{:S(2)}, u32[]{:S(2)}) collective-permute-start(f32[16,640]{1,0:T(8,128)S(1)} %pad_maximum_fusion), channel_id=1, source_target_pairs={{0,5},{4,1},{1,4},{5,0},{2,7},{6,3},{3,6},{7,2},{8,13},{12,9},{9,1... | collective-permute-start | bytes 122888 | tf_op jit(solution)/shard_map/ppermute | solution.py:193
  37.7 1.2 %collective-permute-done.18 = f32[16,640]{1,0:T(8,128)S(1)} collective-permute-done((f32[16,640]{1,0:T(8,128)S(1)}, f32[16,640]{1,0:T(8,128)S(1)}, u32[]{:S(2)}, u32[]{:S(2)}) %collective-permute-start.18) | collective-permute-done | bytes 40992 | tf_op jit(solution)/shard_map/ppermute | solution.py:193
  39.3 0.7 %shard_map.80 = (bf16[16,512]{1,0:T(8,128)(2,1)}, f32[32,32]{1,0:T(8,128)}, f32[32,32]{1,0:T(8,128)}) custom-call(f32[16,640]{1,0:T(8,128)S(1)} %add_add_fusion.total_ref), custom_call_target="tpu_custom_call" | custom-call | tf_op jit(solution)/shard_map/pallas_call | solution.py:287
  (39 shorter events, 4.5 us)
Async XLA Ops:
  0.6 7.3 %copy-start = (bf16[1,1,12,128,128]{4,3,2,1,0:T(8,128)(2,1)S(1)}, bf16[1,1,12,128,128]{4,3,2,1,0:T(8,128)(2,1)}, u32[]{:S(2)}) copy-start(bf16[1,1,12,128,128]{4,3,2,1,0:T(8,128)(2,1)} %param.5) | copy-start | bytes 1179652
  0.6 5.5 %collective-permute-start.3 = (bf16[12,128,128]{2,1,0:T(8,128)(2,1)}, bf16[12,128,128]{2,1,0:T(8,128)(2,1)S(1)}, u32[]{:S(2)}, u32[]{:S(2)}) collective-permute-start(bf16[12,128,128]{2,1,0:T(8,128)(2,1)} %bitcast.4), channel_id=1, source_target_pairs={{0,4},{4,0},{1,5},{5,1},{2,6},{6,2},{3,7},{7,3},{8,12},{12,8},{9,1... | collective-permute-start | bytes 1179656 | tf_op jit(solution)/shard_map/ppermute | solution.py:193
  1.2 6.8 %collective-permute-start = (bf16[16,1024]{1,0:T(8,128)(2,1)}, bf16[16,1024]{1,0:T(8,128)(2,1)S(1)}, u32[]{:S(2)}, u32[]{:S(2)}) collective-permute-start(bf16[16,1024]{1,0:T(8,128)(2,1)} %start_ref.1), channel_id=1, source_target_pairs={{24,4},{28,0},{16,5},{20,1},{8,6},{12,2},{0,7},{4,3},{25,13},{29,9... | collective-permute-start | bytes 98312 | tf_op jit(solution)/shard_map/ppermute | solution.py:193
  4.7 1.5 %collective-permute-start.1 = (s32[12]{0:T(128)}, s32[12]{0:T(128)S(1)}, u32[]{:S(2)}, u32[]{:S(2)}) collective-permute-start(s32[12]{0:T(128)} %bitcast.7), channel_id=1, source_target_pairs={{0,4},{4,0},{1,5},{5,1},{2,6},{6,2},{3,7},{7,3},{8,12},{12,8},{9,1... | collective-permute-start | bytes 152 | tf_op jit(solution)/shard_map/ppermute | solution.py:193
  4.8 1.4 %collective-permute-start.2 = (s32[4]{0:T(128)}, s32[4]{0:T(128)S(1)}, u32[]{:S(2)}, u32[]{:S(2)}) collective-permute-start(s32[4]{0:T(128)} %bitcast.10), channel_id=1, source_target_pairs={{0,4},{4,0},{1,5},{5,1},{2,6},{6,2},{3,7},{7,3},{8,12},{12,8},{9,1... | collective-permute-start | bytes 56 | tf_op jit(solution)/shard_map/ppermute | solution.py:193
  6.2 0.8 %copy-start.1 = (bf16[16,1024]{1,0:T(8,128)(2,1)S(1)}, bf16[16,1024]{1,0:T(8,128)(2,1)}, u32[]{:S(2)}) copy-start(bf16[16,1024]{1,0:T(8,128)(2,1)} %start_ref.1) | copy-start | bytes 98308
  7.8 0.7 %copy-start.4 = (s32[1,1,4]{2,1,0:T(1,128)S(1)}, s32[1,1,4]{2,1,0:T(1,128)}, u32[]{:S(2)}) copy-start(s32[1,1,4]{2,1,0:T(1,128)} %param.7) | copy-start | bytes 52
  9.4 5.6 %collective-permute-start.4 = (f32[16,512]{1,0:T(8,128)S(1)}, f32[16,512]{1,0:T(8,128)S(1)}, u32[]{:S(2)}, u32[]{:S(2)}) collective-permute-start(f32[16,512]{1,0:T(8,128)S(1)} %shard_map.76), channel_id=1, source_target_pairs={{24,4},{28,0},{16,5},{20,1},{8,6},{12,2},{0,7},{4,3},{25,13},{29,9... | collective-permute-start | bytes 98312 | tf_op jit(solution)/shard_map/ppermute | solution.py:193
  15.0 4.7 %collective-permute-start.8 = (f32[16,512]{1,0:T(8,128)S(1)}, f32[16,512]{1,0:T(8,128)S(1)}, u32[]{:S(2)}, u32[]{:S(2)}) collective-permute-start(f32[16,512]{1,0:T(8,128)S(1)} %add.35), channel_id=1, source_target_pairs={{0,7},{4,3},{1,6},{5,2},{2,5},{6,1},{3,4},{7,0},{8,15},{12,11},{9,... | collective-permute-start | bytes 98312 | tf_op jit(solution)/shard_map/ppermute | solution.py:193
  17.8 3.6 %collective-permute-start.7 = (f32[16,512]{1,0:T(8,128)S(1)}, f32[16,512]{1,0:T(8,128)S(1)}, u32[]{:S(2)}, u32[]{:S(2)}) collective-permute-start(f32[16,512]{1,0:T(8,128)S(1)} %add.35), channel_id=1, source_target_pairs={{0,6},{4,2},{1,7},{5,3},{2,4},{6,0},{3,5},{7,1},{8,14},{12,10},{9,... | collective-permute-start | bytes 98312 | tf_op jit(solution)/shard_map/ppermute | solution.py:193
  18.4 3.5 %collective-permute-start.6 = (f32[16,512]{1,0:T(8,128)S(1)}, f32[16,512]{1,0:T(8,128)S(1)}, u32[]{:S(2)}, u32[]{:S(2)}) collective-permute-start(f32[16,512]{1,0:T(8,128)S(1)} %add.35), channel_id=1, source_target_pairs={{0,5},{4,1},{1,4},{5,0},{2,7},{6,3},{3,6},{7,2},{8,13},{12,9},{9,1... | collective-permute-start | bytes 98312 | tf_op jit(solution)/shard_map/ppermute | solution.py:193
  18.4 3.5 %collective-permute-start.5 = (f32[16,512]{1,0:T(8,128)S(1)}, f32[16,512]{1,0:T(8,128)S(1)}, u32[]{:S(2)}, u32[]{:S(2)}) collective-permute-start(f32[16,512]{1,0:T(8,128)S(1)} %add.35), channel_id=1, source_target_pairs={{0,4},{4,0},{1,5},{5,1},{2,6},{6,2},{3,7},{7,3},{8,12},{12,8},{9,1... | collective-permute-start | bytes 98312 | tf_op jit(solution)/shard_map/ppermute | solution.py:193
  21.8 1.3 %copy-start.5 = (bf16[16,512]{1,0:T(8,128)(2,1)}, bf16[16,512]{1,0:T(8,128)(2,1)S(1)}, u32[]{:S(2)}) copy-start(bf16[16,512]{1,0:T(8,128)(2,1)S(1)} %add_convert_fusion) | copy-start | bytes 49156
  21.9 1.2 %collective-permute-start.9 = (bf16[16,512]{1,0:T(8,128)(2,1)S(1)}, bf16[16,512]{1,0:T(8,128)(2,1)S(1)}, u32[]{:S(2)}, u32[]{:S(2)}) collective-permute-start(bf16[16,512]{1,0:T(8,128)(2,1)S(1)} %add_convert_fusion), channel_id=1, source_target_pairs={{0,4},{4,0},{1,5},{5,1},{2,6},{6,2},{3,7},{7,3},{8,12},{12,8},{9,1... | collective-permute-start | bytes 49160 | tf_op jit(solution)/shard_map/ppermute | solution.py:193
  23.1 4.3 %copy-start.2 = (bf16[16,1024]{1,0:T(8,128)(2,1)S(1)}, bf16[16,1024]{1,0:T(8,128)(2,1)}, u32[]{:S(2)}) copy-start(bf16[16,1024]{1,0:T(8,128)(2,1)} %start_ref.1) | copy-start | bytes 98308
  23.1 4.3 %collective-permute-start.10 = (bf16[16,1024]{1,0:T(8,128)(2,1)S(1)}, bf16[16,1024]{1,0:T(8,128)(2,1)S(1)}, u32[]{:S(2)}, u32[]{:S(2)}) collective-permute-start(bf16[16,1024]{1,0:T(8,128)(2,1)S(1)} %pad_maximum_fusion.1.refs_6_), channel_id=1, source_target_pairs={{0,28},{4,24},{1,20},{5,16},{2,12},{6,8},{3,4},{7,0},{9,29},{13,25... | collective-permute-start | bytes 98312 | tf_op jit(solution)/shard_map/ppermute | solution.py:193
  25.6 6.1 %collective-permute-start.11 = (f32[16,512]{1,0:T(8,128)S(1)}, f32[16,512]{1,0:T(8,128)S(1)}, u32[]{:S(2)}, u32[]{:S(2)}) collective-permute-start(f32[16,512]{1,0:T(8,128)S(1)} %get-tuple-element.13), channel_id=1, source_target_pairs={{24,4},{28,0},{16,5},{20,1},{8,6},{12,2},{0,7},{4,3},{25,13},{29,9... | collective-permute-start | bytes 98312 | tf_op jit(solution)/shard_map/ppermute | solution.py:193
  27.8 4.9 %collective-permute-start.14 = (f32[16,128]{1,0:T(8,128)S(1)}, f32[16,128]{1,0:T(8,128)S(1)}, u32[]{:S(2)}, u32[]{:S(2)}) collective-permute-start(f32[16,128]{1,0:T(8,128)S(1)} %shard_map.79), channel_id=1, source_target_pairs={{0,28},{4,24},{1,29},{5,25},{2,30},{6,26},{3,31},{7,27},{8,20},{12... | collective-permute-start | bytes 24584 | tf_op jit(solution)/shard_map/ppermute | solution.py:193
  30.3 4.0 %collective-permute-start.13 = (f32[16,128]{1,0:T(8,128)S(1)}, f32[16,128]{1,0:T(8,128)S(1)}, u32[]{:S(2)}, u32[]{:S(2)}) collective-permute-start(f32[16,128]{1,0:T(8,128)S(1)} %shard_map.79), channel_id=1, source_target_pairs={{0,20},{4,16},{1,21},{5,17},{2,22},{6,18},{3,23},{7,19},{8,28},{12... | collective-permute-start | bytes 24584 | tf_op jit(solution)/shard_map/ppermute | solution.py:193
  30.3 4.0 %collective-permute-start.12 = (f32[16,128]{1,0:T(8,128)S(1)}, f32[16,128]{1,0:T(8,128)S(1)}, u32[]{:S(2)}, u32[]{:S(2)}) collective-permute-start(f32[16,128]{1,0:T(8,128)S(1)} %shard_map.79), channel_id=1, source_target_pairs={{0,12},{4,8},{1,13},{5,9},{2,14},{6,10},{3,15},{7,11},{8,4},{12,0}... | collective-permute-start | bytes 24584 | tf_op jit(solution)/shard_map/ppermute | solution.py:193
  34.3 4.6 %collective-permute-start.18 = (f32[16,640]{1,0:T(8,128)S(1)}, f32[16,640]{1,0:T(8,128)S(1)}, u32[]{:S(2)}, u32[]{:S(2)}) collective-permute-start(f32[16,640]{1,0:T(8,128)S(1)} %pad_maximum_fusion), channel_id=1, source_target_pairs={{0,7},{4,3},{1,6},{5,2},{2,5},{6,1},{3,4},{7,0},{8,15},{12,11},{9,... | collective-permute-start | bytes 122888 | tf_op jit(solution)/shard_map/ppermute | solution.py:193
  34.9 4.4 %collective-permute-start.17 = (f32[16,640]{1,0:T(8,128)S(1)}, f32[16,640]{1,0:T(8,128)S(1)}, u32[]{:S(2)}, u32[]{:S(2)}) collective-permute-start(f32[16,640]{1,0:T(8,128)S(1)} %pad_maximum_fusion), channel_id=1, source_target_pairs={{0,6},{4,2},{1,7},{5,3},{2,4},{6,0},{3,5},{7,1},{8,14},{12,10},{9,... | collective-permute-start | bytes 122888 | tf_op jit(solution)/shard_map/ppermute | solution.py:193
  35.8 3.6 %collective-permute-start.16 = (f32[16,640]{1,0:T(8,128)S(1)}, f32[16,640]{1,0:T(8,128)S(1)}, u32[]{:S(2)}, u32[]{:S(2)}) collective-permute-start(f32[16,640]{1,0:T(8,128)S(1)} %pad_maximum_fusion), channel_id=1, source_target_pairs={{0,5},{4,1},{1,4},{5,0},{2,7},{6,3},{3,6},{7,2},{8,13},{12,9},{9,1... | collective-permute-start | bytes 122888 | tf_op jit(solution)/shard_map/ppermute | solution.py:193
  37.3 2.0 %collective-permute-start.15 = (f32[16,640]{1,0:T(8,128)S(1)}, f32[16,640]{1,0:T(8,128)S(1)}, u32[]{:S(2)}, u32[]{:S(2)}) collective-permute-start(f32[16,640]{1,0:T(8,128)S(1)} %pad_maximum_fusion), channel_id=1, source_target_pairs={{0,4},{4,0},{1,5},{5,1},{2,6},{6,2},{3,7},{7,3},{8,12},{12,8},{9,1... | collective-permute-start | bytes 122888 | tf_op jit(solution)/shard_map/ppermute | solution.py:193
  (1 other events, 0.7 us)

commit v4 on v3

--- a/solution.py
+++ b/solution.py
@@ -30,16 +30,16 @@
 
 
 def products(columns_ref, counts_ref, values_ref, first_row, product, sums, into):
-    row_blocks = counts_ref.shape[0]
     block_total = values_ref.shape[0]
-    if block_total <= 16:
-        ends = [counts_ref[0]]
-        for index in range(1, row_blocks - 1):
-            ends.append(ends[-1] + counts_ref[index])
+    if not in_smem(block_total):
+        columns, counts = columns_ref[...], counts_ref[...]
+        ends = [counts[0, 0]]
+        for index in range(1, counts.shape[1] - 1):
+            ends.append(ends[-1] + counts[0, index])
         found = []
         for block in range(block_total):
             row = first_row + sum((block >= end).astype(jnp.int32) for end in ends)
-            column = columns_ref[block]
+            column = columns[0, block]
             found.append((into(row, column), product(values_ref[block], row, column)))
         for place, value in found:
             sums[place] += value
@@ -48,14 +48,18 @@
     def step(block, carry):
         row, end = carry
         later = block >= end
-        row = jnp.minimum(row + later.astype(jnp.int32), row_blocks - 1)
-        end = end + jnp.where(later, counts_ref[row], 0)
-        column = columns_ref[block]
+        row = jnp.minimum(row + later.astype(jnp.int32), counts_ref.shape[1] - 1)
+        end = end + jnp.where(later, counts_ref[0, row], 0)
+        column = columns_ref[0, block]
         place = into(first_row + row, column)
         sums[place] += product(values_ref[block], first_row + row, column)
         return row, end
 
-    lax.fori_loop(0, block_total, step, (jnp.int32(0), counts_ref[0]))
+    lax.fori_loop(0, block_total, step, (jnp.int32(0), counts_ref[0, 0]))
+
+
+def in_smem(block_total):
+    return block_total > 16
 
 
 def split_into(pieces, source_ref):
@@ -83,12 +87,13 @@
         out_ref[:, index * size : (index + 1) * size] = sums[index]
 
 
-def backward_kernel(tiles, mask, turn_ref, *refs):
+def backward_kernel(tiles, mask, *refs):
     columns, counts, values = refs[:tiles], refs[tiles : 2 * tiles], refs[2 * tiles : 3 * tiles]
     source_ref, *out_refs = refs[3 * tiles : -2]
     pieces, sums = refs[-2:]
     size = sums.shape[3]
-    row_blocks = counts[0].shape[0]
+    row_blocks = counts[0].shape[1]
+    turn = lax.axis_index("row") % tiles
     split_into(pieces, source_ref)
     sums[...] = jnp.zeros_like(sums)
 
@@ -100,7 +105,7 @@
             columns[tile],
             counts[tile],
             values[tile],
-            jnp.bitwise_xor(turn_ref[0], tile) * row_blocks,
+            jnp.bitwise_xor(turn, tile) * row_blocks,
             product,
             sums.at[tile],
             lambda row, column: column,
@@ -109,7 +114,7 @@
     def total(index):
         return xor_sum(sums[0, index], [sums[tile, index] for tile in range(1, tiles)])
 
-    first = jnp.bitwise_xor(turn_ref[0], mask) * row_blocks
+    first = jnp.bitwise_xor(turn, mask) * row_blocks
     for index in range(row_blocks):
         out_refs[0][:, index * size : (index + 1) * size] = total(first + index)
     for out_ref in out_refs[1:]:
@@ -119,21 +124,26 @@
 
 def gram_kernel(scale, start_ref, once_ref, backward_ref, out_ref):
     vectors = once_ref.shape[0]
-    once = once_ref[...]
-    gram = functools.partial(
+    rest = backward_ref[...]
+    rows = [start_ref[...], once_ref[...]]
+    for _ in range(3):
+        rows.append(rest.astype(jnp.bfloat16))
+        rest = rest - rows[-1].astype(f32)
+    basis = jnp.concatenate(rows[:2], axis=0)
+    dot = functools.partial(
         lax.dot_general,
         dimension_numbers=(((1,), (1,)), ((), ())),
         preferred_element_type=f32,
     )
-    basis = jnp.concatenate([start_ref[...], once], axis=0)
-    square = gram(basis, basis) * scale
-    wide = once.astype(f32)
-    backward = backward_ref[...]
-    cross = gram(wide, backward, precision=highest) + gram(backward, wide, precision=highest)
+    gram = dot(jnp.concatenate(rows, axis=0), basis)
+    square = gram[: 2 * vectors] * scale
+    cross = [gram[place * vectors : (place + 1) * vectors, vectors:] for place in (2, 3, 4)]
+    cross = cross[0] + (cross[1] + cross[2])
+    turned = dot(rows[1], rows[2]) + (dot(rows[1], rows[3]) + dot(rows[1], rows[4]))
     out_ref[...] = jnp.zeros_like(out_ref)
     out_ref[:, : 2 * vectors] = square[:vectors]
     out_ref[:, 2 * vectors : 4 * vectors] = square[vectors:]
-    out_ref[:, 4 * vectors : 5 * vectors] = cross
+    out_ref[:, 4 * vectors : 5 * vectors] = cross + turned
 
 
 def last_kernel(norm_scale, total_ref, twice_ref, basis_ref, projected_ref):
@@ -171,10 +181,10 @@
     row_count, col_count = lax.axis_size("row"), lax.axis_size("col")
     ratio = row_count // col_count
     values = block_values[0, 0]
-    columns = block_columns[0, 0]
-    counts = block_counts[0, 0]
+    columns = block_columns[0]
+    counts = block_counts[0]
     block_total, block_size = values.shape[:2]
-    row_blocks = counts.shape[0]
+    row_blocks = counts.shape[1]
     row_width = row_blocks * block_size
     vectors, col_width = start_block.shape
     col_blocks = col_width // block_size
@@ -235,6 +245,7 @@
             slab.append(piece)
         return jnp.concatenate(slab, axis=1)
 
+    table = smem if in_smem(block_total) else vmem
     tiles = [of_chip(columns), of_chip(counts), of_chip(values)]
     flops = 2 * vectors * block_total * block_size**2
     bytes_accessed = 2 * block_total * block_size**2
@@ -247,7 +258,7 @@
         return call(
             forward_kernel,
             part_shape,
-            [smem] * 2 + [vmem] * (2 + len(term)),
+            [table] * 2 + [vmem] * (2 + len(term)),
             [pieces, pltpu.VMEM((row_blocks, vectors, block_size), f32)],
             flops,
             bytes_accessed,
@@ -257,11 +268,11 @@
         return call(
             functools.partial(backward_kernel, ratio, 0 if crossed else opposite),
             [part_shape, slab_shape][:outputs],
-            [smem] * (2 * ratio + 1) + [vmem] * (ratio + 1),
+            [table] * (2 * ratio) + [vmem] * (ratio + 1),
             [pieces, pltpu.VMEM((ratio, col_blocks, vectors, block_size), f32)],
             ratio * flops,
             ratio * bytes_accessed,
-        )(turn.reshape(1), *tiles[0], *tiles[1], *tiles[2], source)
+        )(*tiles[0], *tiles[1], *tiles[2], source)
 
     start_rows = send(start_block, gather_pairs)
     forward = forward_of(start_block)

time: 40.2 us -> 39.4 us (0.980)
  waiting for transfers between devices: 11.4 us -> 13.5 us
  Pallas kernels: 4.57 us -> 2.69 us
  local copies, waits for them, and re-layouts: 1.31 us -> 0.78 us
    ppermute x19, waiting for transfers between devices: 11.4 us -> 13.5 us  [send(): lax.ppermute(value, both, [(device(*source, member), device(*target, memb...]
    pallas_call x2, Pallas kernels: 1.72 us -> 0.8 us  [forward_of(): call(forward_kernel, part_shape, [table] * 2 + [vmem] * (2 + len(term)),...]
    pallas_call x2, Pallas kernels: 1.78 us -> 0.86 us  [backward_of(): call(functools.partial(backward_kernel, ratio, 0 if crossed else opposite...]
    unnamed x12, local copies, waits for them, and re-layouts: 1.31 us -> 0.78 us
  transfers between devices with their start and end apart: 19 -> 19, of which waited for: 12 -> 12; matrix products, arithmetic and copies ran while one was open for 0% -> 0% of each run, Pallas kernels for 8% -> 4%
where the time goes in v4:
time: 39.4 us; the launch traced here: 39.3 us
  starting transfers between devices  21.5 us (55%)
  waiting for transfers between devices  13.5 us (34%)
  Pallas kernels  2.69 us (7%)
  local copies, waits for them, and re-layouts  0.78 us (2%)
  between operations  0.72 us (2%)
    ppermute x19, starting transfers between devices, send(): lax.ppermute(value, both, [(device(*source, member), device(*target, memb...  21.5 us
    ppermute x19, waiting for transfers between devices, send(): lax.ppermute(value, both, [(device(*source, member), device(*target, memb...  13.5 us
    pallas_call x2, Pallas kernels, backward_of(): call(functools.partial(backward_kernel, ratio, 0 if crossed else opposite...  0.86 us
    pallas_call x2, Pallas kernels, forward_of(): call(forward_kernel, part_shape, [table] * 2 + [vmem] * (2 + len(term)),...  0.8 us
  transfers between devices with their start and end apart: 19, of which 12 were waited for; matrix products, arithmetic and copies ran while one was open for 0% of the time, Pallas kernels for 4%

profile of v4, /device:TPU:0, one launch (start us, length us, event | category | flops | bytes accessed | tf_op | source)
XLA Modules:
  0.0 39.3 jit_solution(8417786151025473045)
XLA Ops:
  0.6 0.5 %collective-permute-start.3 = (bf16[12,128,128]{2,1,0:T(8,128)(2,1)}, bf16[12,128,128]{2,1,0:T(8,128)(2,1)S(1)}, u32[]{:S(2)}, u32[]{:S(2)}) collective-permute-start(bf16[12,128,128]{2,1,0:T(8,128)(2,1)} %bitcast.3), channel_id=1, source_target_pairs={{0,4},{4,0},{1,5},{5,1},{2,6},{6,2},{3,7},{7,3},{8,12},{12,8},{9,1... | collective-permute-start | bytes 1179656 | tf_op jit(solution)/shard_map/ppermute | solution.py:203
  1.2 3.6 %collective-permute-start = (bf16[16,1024]{1,0:T(8,128)(2,1)}, bf16[16,1024]{1,0:T(8,128)(2,1)S(1)}, u32[]{:S(2)}, u32[]{:S(2)}) collective-permute-start(bf16[16,1024]{1,0:T(8,128)(2,1)} %start_ref.1), channel_id=1, source_target_pairs={{24,4},{28,0},{16,5},{20,1},{8,6},{12,2},{0,7},{4,3},{25,13},{29,9... | collective-permute-start | bytes 98312 | tf_op jit(solution)/shard_map/ppermute | solution.py:203
  5.2 1.0 %collective-permute-done.2.counts_ref.refs_3_ = s32[1,4]{1,0:T(1,128)S(1)} collective-permute-done((s32[1,4]{1,0:T(1,128)}, s32[1,4]{1,0:T(1,128)S(1)}, u32[]{:S(2)}, u32[]{:S(2)}) %collective-permute-start.2) | collective-permute-done | bytes 48 | tf_op jit(solution)/shard_map/ppermute | solution.py:203
  6.2 0.8 %copy-done.1 = bf16[16,1024]{1,0:T(8,128)(2,1)S(1)} copy-done((bf16[16,1024]{1,0:T(8,128)(2,1)S(1)}, bf16[16,1024]{1,0:T(8,128)(2,1)}, u32[]{:S(2)}) %copy-start.1) | copy-done | bytes 32792
  7.4 0.6 %collective-permute-done.refs_6_ = bf16[16,1024]{1,0:T(8,128)(2,1)S(1)} collective-permute-done((bf16[16,1024]{1,0:T(8,128)(2,1)}, bf16[16,1024]{1,0:T(8,128)(2,1)S(1)}, u32[]{:S(2)}, u32[]{:S(2)}) %collective-permute-start) | collective-permute-done | bytes 32800 | tf_op jit(solution)/shard_map/ppermute | solution.py:203
  8.4 3.2 %collective-permute-start.4 = (f32[16,512]{1,0:T(8,128)S(1)}, f32[16,512]{1,0:T(8,128)S(1)}, u32[]{:S(2)}, u32[]{:S(2)}) collective-permute-start(f32[16,512]{1,0:T(8,128)S(1)} %shard_map.76), channel_id=1, source_target_pairs={{24,4},{28,0},{16,5},{20,1},{8,6},{12,2},{0,7},{4,3},{25,13},{29,9... | collective-permute-start | bytes 98312 | tf_op jit(solution)/shard_map/ppermute | solution.py:203
  11.6 2.2 %collective-permute-done.4 = f32[16,512]{1,0:T(8,128)S(1)} collective-permute-done((f32[16,512]{1,0:T(8,128)S(1)}, f32[16,512]{1,0:T(8,128)S(1)}, u32[]{:S(2)}, u32[]{:S(2)}) %collective-permute-start.4) | collective-permute-done | bytes 32800 | tf_op jit(solution)/shard_map/ppermute | solution.py:203
  13.8 2.0 %collective-permute-start.8 = (f32[16,512]{1,0:T(8,128)S(1)}, f32[16,512]{1,0:T(8,128)S(1)}, u32[]{:S(2)}, u32[]{:S(2)}) collective-permute-start(f32[16,512]{1,0:T(8,128)S(1)} %add.34), channel_id=1, source_target_pairs={{0,7},{4,3},{1,6},{5,2},{2,5},{6,1},{3,4},{7,0},{8,15},{12,11},{9,... | collective-permute-start | bytes 98312 | tf_op jit(solution)/shard_map/ppermute | solution.py:203
  15.9 1.4 %collective-permute-start.7 = (f32[16,512]{1,0:T(8,128)S(1)}, f32[16,512]{1,0:T(8,128)S(1)}, u32[]{:S(2)}, u32[]{:S(2)}) collective-permute-start(f32[16,512]{1,0:T(8,128)S(1)} %add.34), channel_id=1, source_target_pairs={{0,6},{4,2},{1,7},{5,3},{2,4},{6,0},{3,5},{7,1},{8,14},{12,10},{9,... | collective-permute-start | bytes 98312 | tf_op jit(solution)/shard_map/ppermute | solution.py:203
  17.4 0.8 %collective-permute-done.8 = f32[16,512]{1,0:T(8,128)S(1)} collective-permute-done((f32[16,512]{1,0:T(8,128)S(1)}, f32[16,512]{1,0:T(8,128)S(1)}, u32[]{:S(2)}, u32[]{:S(2)}) %collective-permute-start.8) | collective-permute-done | bytes 32800 | tf_op jit(solution)/shard_map/ppermute | solution.py:203
  18.1 1.1 %collective-permute-done.7 = f32[16,512]{1,0:T(8,128)S(1)} collective-permute-done((f32[16,512]{1,0:T(8,128)S(1)}, f32[16,512]{1,0:T(8,128)S(1)}, u32[]{:S(2)}, u32[]{:S(2)}) %collective-permute-start.7) | collective-permute-done | bytes 32800 | tf_op jit(solution)/shard_map/ppermute | solution.py:203
  19.2 1.5 %collective-permute-done.6 = f32[16,512]{1,0:T(8,128)S(1)} collective-permute-done((f32[16,512]{1,0:T(8,128)S(1)}, f32[16,512]{1,0:T(8,128)S(1)}, u32[]{:S(2)}, u32[]{:S(2)}) %collective-permute-start.6) | collective-permute-done | bytes 32800 | tf_op jit(solution)/shard_map/ppermute | solution.py:203
  20.9 1.1 %collective-permute-done.9 = bf16[16,512]{1,0:T(8,128)(2,1)S(1)} collective-permute-done((bf16[16,512]{1,0:T(8,128)(2,1)S(1)}, bf16[16,512]{1,0:T(8,128)(2,1)S(1)}, u32[]{:S(2)}, u32[]{:S(2)}) %collective-permute-start.9) | collective-permute-done | bytes 16416 | tf_op jit(solution)/shard_map/ppermute | solution.py:203
  22.1 2.2 %collective-permute-start.10 = (bf16[16,1024]{1,0:T(8,128)(2,1)S(1)}, bf16[16,1024]{1,0:T(8,128)(2,1)S(1)}, u32[]{:S(2)}, u32[]{:S(2)}) collective-permute-start(bf16[16,1024]{1,0:T(8,128)(2,1)S(1)} %pad_maximum_fusion.1.refs_6_), channel_id=1, source_target_pairs={{0,28},{4,24},{1,20},{5,16},{2,12},{6,8},{3,4},{7,0},{9,29},{13,25... | collective-permute-start | bytes 98312 | tf_op jit(solution)/shard_map/ppermute | solution.py:203
  24.7 0.5 %collective-permute-start.11 = (f32[16,512]{1,0:T(8,128)S(1)}, f32[16,512]{1,0:T(8,128)S(1)}, u32[]{:S(2)}, u32[]{:S(2)}) collective-permute-start(f32[16,512]{1,0:T(8,128)S(1)} %get-tuple-element.13), channel_id=1, source_target_pairs={{24,4},{28,0},{16,5},{20,1},{8,6},{12,2},{0,7},{4,3},{25,13},{29,9... | collective-permute-start | bytes 98312 | tf_op jit(solution)/shard_map/ppermute | solution.py:203
  25.2 1.1 %collective-permute-done.10.source_ref.once_ref = bf16[16,1024]{1,0:T(8,128)(2,1)S(1)} collective-permute-done((bf16[16,1024]{1,0:T(8,128)(2,1)S(1)}, bf16[16,1024]{1,0:T(8,128)(2,1)S(1)}, u32[]{:S(2)}, u32[]{:S(2)}) %collective-permute-start.10) | collective-permute-done | bytes 32800 | tf_op jit(solution)/shard_map/ppermute | solution.py:203
  26.7 3.1 %collective-permute-start.14 = (f32[16,128]{1,0:T(8,128)S(1)}, f32[16,128]{1,0:T(8,128)S(1)}, u32[]{:S(2)}, u32[]{:S(2)}) collective-permute-start(f32[16,128]{1,0:T(8,128)S(1)} %shard_map.79), channel_id=1, source_target_pairs={{0,28},{4,24},{1,29},{5,25},{2,30},{6,26},{3,31},{7,27},{8,20},{12... | collective-permute-start | bytes 24584 | tf_op jit(solution)/shard_map/ppermute | solution.py:203
  29.8 0.8 %collective-permute-start.12 = (f32[16,128]{1,0:T(8,128)S(1)}, f32[16,128]{1,0:T(8,128)S(1)}, u32[]{:S(2)}, u32[]{:S(2)}) collective-permute-start(f32[16,128]{1,0:T(8,128)S(1)} %shard_map.79), channel_id=1, source_target_pairs={{0,12},{4,8},{1,13},{5,9},{2,14},{6,10},{3,15},{7,11},{8,4},{12,0}... | collective-permute-start | bytes 24584 | tf_op jit(solution)/shard_map/ppermute | solution.py:203
  31.0 0.6 %collective-permute-done.14 = f32[16,128]{1,0:T(8,128)S(1)} collective-permute-done((f32[16,128]{1,0:T(8,128)S(1)}, f32[16,128]{1,0:T(8,128)S(1)}, u32[]{:S(2)}, u32[]{:S(2)}) %collective-permute-start.14) | collective-permute-done | bytes 8224 | tf_op jit(solution)/shard_map/ppermute | solution.py:203
  31.6 2.2 %collective-permute-done.13 = f32[16,128]{1,0:T(8,128)S(1)} collective-permute-done((f32[16,128]{1,0:T(8,128)S(1)}, f32[16,128]{1,0:T(8,128)S(1)}, u32[]{:S(2)}, u32[]{:S(2)}) %collective-permute-start.13) | collective-permute-done | bytes 8224 | tf_op jit(solution)/shard_map/ppermute | solution.py:203
  34.0 0.6 %collective-permute-start.17 = (f32[16,640]{1,0:T(8,128)S(1)}, f32[16,640]{1,0:T(8,128)S(1)}, u32[]{:S(2)}, u32[]{:S(2)}) collective-permute-start(f32[16,640]{1,0:T(8,128)S(1)} %pad_maximum_fusion), channel_id=1, source_target_pairs={{0,6},{4,2},{1,7},{5,3},{2,4},{6,0},{3,5},{7,1},{8,14},{12,10},{9,... | collective-permute-start | bytes 122888 | tf_op jit(solution)/shard_map/ppermute | solution.py:203
  34.7 2.2 %collective-permute-start.16 = (f32[16,640]{1,0:T(8,128)S(1)}, f32[16,640]{1,0:T(8,128)S(1)}, u32[]{:S(2)}, u32[]{:S(2)}) collective-permute-start(f32[16,640]{1,0:T(8,128)S(1)} %pad_maximum_fusion), channel_id=1, source_target_pairs={{0,5},{4,1},{1,4},{5,0},{2,7},{6,3},{3,6},{7,2},{8,13},{12,9},{9,1... | collective-permute-start | bytes 122888 | tf_op jit(solution)/shard_map/ppermute | solution.py:203
  37.2 1.2 %collective-permute-done.18 = f32[16,640]{1,0:T(8,128)S(1)} collective-permute-done((f32[16,640]{1,0:T(8,128)S(1)}, f32[16,640]{1,0:T(8,128)S(1)}, u32[]{:S(2)}, u32[]{:S(2)}) %collective-permute-start.18) | collective-permute-done | bytes 40992 | tf_op jit(solution)/shard_map/ppermute | solution.py:203
  38.6 0.7 %shard_map.80 = (bf16[16,512]{1,0:T(8,128)(2,1)}, f32[32,32]{1,0:T(8,128)}, f32[32,32]{1,0:T(8,128)}) custom-call(f32[16,640]{1,0:T(8,128)S(1)} %add_add_fusion.total_ref), custom_call_target="tpu_custom_call" | custom-call | tf_op jit(solution)/shard_map/pallas_call | solution.py:298
  (39 shorter events, 3.7 us)
Async XLA Ops:
  0.6 7.3 %copy-start = (bf16[1,1,12,128,128]{4,3,2,1,0:T(8,128)(2,1)S(1)}, bf16[1,1,12,128,128]{4,3,2,1,0:T(8,128)(2,1)}, u32[]{:S(2)}) copy-start(bf16[1,1,12,128,128]{4,3,2,1,0:T(8,128)(2,1)} %param.5) | copy-start | bytes 1179652
  0.6 5.5 %collective-permute-start.3 = (bf16[12,128,128]{2,1,0:T(8,128)(2,1)}, bf16[12,128,128]{2,1,0:T(8,128)(2,1)S(1)}, u32[]{:S(2)}, u32[]{:S(2)}) collective-permute-start(bf16[12,128,128]{2,1,0:T(8,128)(2,1)} %bitcast.3), channel_id=1, source_target_pairs={{0,4},{4,0},{1,5},{5,1},{2,6},{6,2},{3,7},{7,3},{8,12},{12,8},{9,1... | collective-permute-start | bytes 1179656 | tf_op jit(solution)/shard_map/ppermute | solution.py:203
  1.2 6.8 %collective-permute-start = (bf16[16,1024]{1,0:T(8,128)(2,1)}, bf16[16,1024]{1,0:T(8,128)(2,1)S(1)}, u32[]{:S(2)}, u32[]{:S(2)}) collective-permute-start(bf16[16,1024]{1,0:T(8,128)(2,1)} %start_ref.1), channel_id=1, source_target_pairs={{24,4},{28,0},{16,5},{20,1},{8,6},{12,2},{0,7},{4,3},{25,13},{29,9... | collective-permute-start | bytes 98312 | tf_op jit(solution)/shard_map/ppermute | solution.py:203
  4.7 1.5 %collective-permute-start.1 = (s32[1,12]{1,0:T(1,128)}, s32[1,12]{1,0:T(1,128)S(1)}, u32[]{:S(2)}, u32[]{:S(2)}) collective-permute-start(s32[1,12]{1,0:T(1,128)} %bitcast.6), channel_id=1, source_target_pairs={{0,4},{4,0},{1,5},{5,1},{2,6},{6,2},{3,7},{7,3},{8,12},{12,8},{9,1... | collective-permute-start | bytes 152 | tf_op jit(solution)/shard_map/ppermute | solution.py:203
  4.8 1.4 %collective-permute-start.2 = (s32[1,4]{1,0:T(1,128)}, s32[1,4]{1,0:T(1,128)S(1)}, u32[]{:S(2)}, u32[]{:S(2)}) collective-permute-start(s32[1,4]{1,0:T(1,128)} %bitcast.9), channel_id=1, source_target_pairs={{0,4},{4,0},{1,5},{5,1},{2,6},{6,2},{3,7},{7,3},{8,12},{12,8},{9,1... | collective-permute-start | bytes 56 | tf_op jit(solution)/shard_map/ppermute | solution.py:203
  6.9 1.0 %copy-start.3 = (s32[1,1,12]{2,1,0:T(1,128)S(1)}, s32[1,1,12]{2,1,0:T(1,128)}, u32[]{:S(2)}) copy-start(s32[1,1,12]{2,1,0:T(1,128)} %param.6) | copy-start | bytes 148
  7.0 1.0 %copy-start.4 = (s32[1,1,4]{2,1,0:T(1,128)S(1)}, s32[1,1,4]{2,1,0:T(1,128)}, u32[]{:S(2)}) copy-start(s32[1,1,4]{2,1,0:T(1,128)} %param.7) | copy-start | bytes 52
  8.4 5.4 %collective-permute-start.4 = (f32[16,512]{1,0:T(8,128)S(1)}, f32[16,512]{1,0:T(8,128)S(1)}, u32[]{:S(2)}, u32[]{:S(2)}) collective-permute-start(f32[16,512]{1,0:T(8,128)S(1)} %shard_map.76), channel_id=1, source_target_pairs={{24,4},{28,0},{16,5},{20,1},{8,6},{12,2},{0,7},{4,3},{25,13},{29,9... | collective-permute-start | bytes 98312 | tf_op jit(solution)/shard_map/ppermute | solution.py:203
  13.8 4.3 %collective-permute-start.8 = (f32[16,512]{1,0:T(8,128)S(1)}, f32[16,512]{1,0:T(8,128)S(1)}, u32[]{:S(2)}, u32[]{:S(2)}) collective-permute-start(f32[16,512]{1,0:T(8,128)S(1)} %add.34), channel_id=1, source_target_pairs={{0,7},{4,3},{1,6},{5,2},{2,5},{6,1},{3,4},{7,0},{8,15},{12,11},{9,... | collective-permute-start | bytes 98312 | tf_op jit(solution)/shard_map/ppermute | solution.py:203
  15.9 3.3 %collective-permute-start.7 = (f32[16,512]{1,0:T(8,128)S(1)}, f32[16,512]{1,0:T(8,128)S(1)}, u32[]{:S(2)}, u32[]{:S(2)}) collective-permute-start(f32[16,512]{1,0:T(8,128)S(1)} %add.34), channel_id=1, source_target_pairs={{0,6},{4,2},{1,7},{5,3},{2,4},{6,0},{3,5},{7,1},{8,14},{12,10},{9,... | collective-permute-start | bytes 98312 | tf_op jit(solution)/shard_map/ppermute | solution.py:203
  17.3 3.4 %collective-permute-start.6 = (f32[16,512]{1,0:T(8,128)S(1)}, f32[16,512]{1,0:T(8,128)S(1)}, u32[]{:S(2)}, u32[]{:S(2)}) collective-permute-start(f32[16,512]{1,0:T(8,128)S(1)} %add.34), channel_id=1, source_target_pairs={{0,5},{4,1},{1,4},{5,0},{2,7},{6,3},{3,6},{7,2},{8,13},{12,9},{9,1... | collective-permute-start | bytes 98312 | tf_op jit(solution)/shard_map/ppermute | solution.py:203
  17.3 3.4 %collective-permute-start.5 = (f32[16,512]{1,0:T(8,128)S(1)}, f32[16,512]{1,0:T(8,128)S(1)}, u32[]{:S(2)}, u32[]{:S(2)}) collective-permute-start(f32[16,512]{1,0:T(8,128)S(1)} %add.34), channel_id=1, source_target_pairs={{0,4},{4,0},{1,5},{5,1},{2,6},{6,2},{3,7},{7,3},{8,12},{12,8},{9,1... | collective-permute-start | bytes 98312 | tf_op jit(solution)/shard_map/ppermute | solution.py:203
  20.8 1.3 %copy-start.5 = (bf16[16,512]{1,0:T(8,128)(2,1)}, bf16[16,512]{1,0:T(8,128)(2,1)S(1)}, u32[]{:S(2)}) copy-start(bf16[16,512]{1,0:T(8,128)(2,1)S(1)} %add_convert_fusion) | copy-start | bytes 49156
  20.8 1.2 %collective-permute-start.9 = (bf16[16,512]{1,0:T(8,128)(2,1)S(1)}, bf16[16,512]{1,0:T(8,128)(2,1)S(1)}, u32[]{:S(2)}, u32[]{:S(2)}) collective-permute-start(bf16[16,512]{1,0:T(8,128)(2,1)S(1)} %add_convert_fusion), channel_id=1, source_target_pairs={{0,4},{4,0},{1,5},{5,1},{2,6},{6,2},{3,7},{7,3},{8,12},{12,8},{9,1... | collective-permute-start | bytes 49160 | tf_op jit(solution)/shard_map/ppermute | solution.py:203
  22.0 4.3 %copy-start.2 = (bf16[16,1024]{1,0:T(8,128)(2,1)S(1)}, bf16[16,1024]{1,0:T(8,128)(2,1)}, u32[]{:S(2)}) copy-start(bf16[16,1024]{1,0:T(8,128)(2,1)} %start_ref.1) | copy-start | bytes 98308
  22.1 4.3 %collective-permute-start.10 = (bf16[16,1024]{1,0:T(8,128)(2,1)S(1)}, bf16[16,1024]{1,0:T(8,128)(2,1)S(1)}, u32[]{:S(2)}, u32[]{:S(2)}) collective-permute-start(bf16[16,1024]{1,0:T(8,128)(2,1)S(1)} %pad_maximum_fusion.1.refs_6_), channel_id=1, source_target_pairs={{0,28},{4,24},{1,20},{5,16},{2,12},{6,8},{3,4},{7,0},{9,29},{13,25... | collective-permute-start | bytes 98312 | tf_op jit(solution)/shard_map/ppermute | solution.py:203
  24.7 5.9 %collective-permute-start.11 = (f32[16,512]{1,0:T(8,128)S(1)}, f32[16,512]{1,0:T(8,128)S(1)}, u32[]{:S(2)}, u32[]{:S(2)}) collective-permute-start(f32[16,512]{1,0:T(8,128)S(1)} %get-tuple-element.13), channel_id=1, source_target_pairs={{24,4},{28,0},{16,5},{20,1},{8,6},{12,2},{0,7},{4,3},{25,13},{29,9... | collective-permute-start | bytes 98312 | tf_op jit(solution)/shard_map/ppermute | solution.py:203
  26.7 4.9 %collective-permute-start.14 = (f32[16,128]{1,0:T(8,128)S(1)}, f32[16,128]{1,0:T(8,128)S(1)}, u32[]{:S(2)}, u32[]{:S(2)}) collective-permute-start(f32[16,128]{1,0:T(8,128)S(1)} %shard_map.79), channel_id=1, source_target_pairs={{0,28},{4,24},{1,29},{5,25},{2,30},{6,26},{3,31},{7,27},{8,20},{12... | collective-permute-start | bytes 24584 | tf_op jit(solution)/shard_map/ppermute | solution.py:203
  29.8 4.0 %collective-permute-start.13 = (f32[16,128]{1,0:T(8,128)S(1)}, f32[16,128]{1,0:T(8,128)S(1)}, u32[]{:S(2)}, u32[]{:S(2)}) collective-permute-start(f32[16,128]{1,0:T(8,128)S(1)} %shard_map.79), channel_id=1, source_target_pairs={{0,20},{4,16},{1,21},{5,17},{2,22},{6,18},{3,23},{7,19},{8,28},{12... | collective-permute-start | bytes 24584 | tf_op jit(solution)/shard_map/ppermute | solution.py:203
  29.8 4.0 %collective-permute-start.12 = (f32[16,128]{1,0:T(8,128)S(1)}, f32[16,128]{1,0:T(8,128)S(1)}, u32[]{:S(2)}, u32[]{:S(2)}) collective-permute-start(f32[16,128]{1,0:T(8,128)S(1)} %shard_map.79), channel_id=1, source_target_pairs={{0,12},{4,8},{1,13},{5,9},{2,14},{6,10},{3,15},{7,11},{8,4},{12,0}... | collective-permute-start | bytes 24584 | tf_op jit(solution)/shard_map/ppermute | solution.py:203
  33.8 4.6 %collective-permute-start.18 = (f32[16,640]{1,0:T(8,128)S(1)}, f32[16,640]{1,0:T(8,128)S(1)}, u32[]{:S(2)}, u32[]{:S(2)}) collective-permute-start(f32[16,640]{1,0:T(8,128)S(1)} %pad_maximum_fusion), channel_id=1, source_target_pairs={{0,7},{4,3},{1,6},{5,2},{2,5},{6,1},{3,4},{7,0},{8,15},{12,11},{9,... | collective-permute-start | bytes 122888 | tf_op jit(solution)/shard_map/ppermute | solution.py:203
  34.0 4.3 %collective-permute-start.17 = (f32[16,640]{1,0:T(8,128)S(1)}, f32[16,640]{1,0:T(8,128)S(1)}, u32[]{:S(2)}, u32[]{:S(2)}) collective-permute-start(f32[16,640]{1,0:T(8,128)S(1)} %pad_maximum_fusion), channel_id=1, source_target_pairs={{0,6},{4,2},{1,7},{5,3},{2,4},{6,0},{3,5},{7,1},{8,14},{12,10},{9,... | collective-permute-start | bytes 122888 | tf_op jit(solution)/shard_map/ppermute | solution.py:203
  34.7 3.9 %collective-permute-start.16 = (f32[16,640]{1,0:T(8,128)S(1)}, f32[16,640]{1,0:T(8,128)S(1)}, u32[]{:S(2)}, u32[]{:S(2)}) collective-permute-start(f32[16,640]{1,0:T(8,128)S(1)} %pad_maximum_fusion), channel_id=1, source_target_pairs={{0,5},{4,1},{1,4},{5,0},{2,7},{6,3},{3,6},{7,2},{8,13},{12,9},{9,1... | collective-permute-start | bytes 122888 | tf_op jit(solution)/shard_map/ppermute | solution.py:203
  36.8 1.7 %collective-permute-start.15 = (f32[16,640]{1,0:T(8,128)S(1)}, f32[16,640]{1,0:T(8,128)S(1)}, u32[]{:S(2)}, u32[]{:S(2)}) collective-permute-start(f32[16,640]{1,0:T(8,128)S(1)} %pad_maximum_fusion), channel_id=1, source_target_pairs={{0,4},{4,0},{1,5},{5,1},{2,6},{6,2},{3,7},{7,3},{8,12},{12,8},{9,1... | collective-permute-start | bytes 122888 | tf_op jit(solution)/shard_map/ppermute | solution.py:203
  (1 other events, 0.8 us)

commit v5 on v4

--- a/solution.py
+++ b/solution.py
@@ -68,13 +68,9 @@
         pieces[index] = source_ref[:, index * size : (index + 1) * size]
 
 
-def forward_kernel(columns_ref, counts_ref, values_ref, source_ref, *refs):
-    term_refs, (out_ref, pieces, sums) = refs[:-3], refs[-3:]
+def forward_kernel(columns_ref, counts_ref, values_ref, source_ref, out_ref, pieces, sums):
     split_into(pieces, source_ref)
-    if term_refs:
-        split_into(sums, term_refs[0])
-    else:
-        sums[...] = jnp.zeros_like(sums)
+    sums[...] = jnp.zeros_like(sums)
 
     def product(block, row, column):
         return lax.dot_general(
@@ -89,8 +85,7 @@
 
 def backward_kernel(tiles, mask, *refs):
     columns, counts, values = refs[:tiles], refs[tiles : 2 * tiles], refs[2 * tiles : 3 * tiles]
-    source_ref, *out_refs = refs[3 * tiles : -2]
-    pieces, sums = refs[-2:]
+    source_ref, out_ref, pieces, sums = refs[3 * tiles :]
     size = sums.shape[3]
     row_blocks = counts[0].shape[1]
     turn = lax.axis_index("row") % tiles
@@ -114,36 +109,39 @@
     def total(index):
         return xor_sum(sums[0, index], [sums[tile, index] for tile in range(1, tiles)])
 
-    first = jnp.bitwise_xor(turn, mask) * row_blocks
-    for index in range(row_blocks):
-        out_refs[0][:, index * size : (index + 1) * size] = total(first + index)
-    for out_ref in out_refs[1:]:
-        for index in range(sums.shape[1]):
-            out_ref[:, index * size : (index + 1) * size] = total(index)
-
-
-def gram_kernel(scale, start_ref, once_ref, backward_ref, out_ref):
-    vectors = once_ref.shape[0]
-    rest = backward_ref[...]
-    rows = [start_ref[...], once_ref[...]]
-    for _ in range(3):
-        rows.append(rest.astype(jnp.bfloat16))
-        rest = rest - rows[-1].astype(f32)
-    basis = jnp.concatenate(rows[:2], axis=0)
+    first = 0 if mask is None else jnp.bitwise_xor(turn, mask) * row_blocks
+    for index in range(out_ref.shape[1] // size):
+        out_ref[:, index * size : (index + 1) * size] = total(first + index).astype(out_ref.dtype)
+
+
+def merge_kernel(ratio, mask, start_ref, once_ref, forward_ref, *refs):
+    terms = [term_ref[...] for term_ref in refs[:-1]]
+    out_ref = refs[-1]
+    vectors, width = forward_ref.shape
+    start, once = start_ref[...], once_ref[...]
     dot = functools.partial(
         lax.dot_general,
         dimension_numbers=(((1,), (1,)), ((), ())),
         preferred_element_type=f32,
     )
-    gram = dot(jnp.concatenate(rows, axis=0), basis)
-    square = gram[: 2 * vectors] * scale
-    cross = [gram[place * vectors : (place + 1) * vectors, vectors:] for place in (2, 3, 4)]
-    cross = cross[0] + (cross[1] + cross[2])
-    turned = dot(rows[1], rows[2]) + (dot(rows[1], rows[3]) + dot(rows[1], rows[4]))
-    out_ref[...] = jnp.zeros_like(out_ref)
-    out_ref[:, : 2 * vectors] = square[:vectors]
-    out_ref[:, 2 * vectors : 4 * vectors] = square[vectors:]
-    out_ref[:, 4 * vectors : 5 * vectors] = cross + turned
+    gram = dot(jnp.concatenate([start, once, *terms], axis=0), jnp.concatenate([start, once], axis=0))
+    rows = [gram[place * vectors : (place + 1) * vectors] for place in range(2 + len(terms))]
+    cross = [row[:, vectors:] for row in rows[2:]]
+    turned = [dot(once, term) for term in terms]
+    row, column = lax.axis_index("row"), lax.axis_index("col")
+    part = (row % ratio) ^ mask
+    due = row // ratio == column
+    backward = jnp.zeros((vectors, width), f32)
+    for place in range(ratio):
+        here = [term[:, place * width : (place + 1) * width].astype(f32) for term in terms]
+        backward = jnp.where(due & (part == place), xor_sum(here[0], here[1:]), backward)
+    out_ref[:, :width] = forward_ref[...] + backward
+    out_ref[:, width:] = jnp.zeros((vectors, out_ref.shape[1] - width), f32)
+    out_ref[:, width : width + 2 * vectors] = rows[0]
+    out_ref[:, width + 2 * vectors : width + 4 * vectors] = rows[1]
+    out_ref[:, width + 4 * vectors : width + 5 * vectors] = xor_sum(cross[0], cross[1:]) + xor_sum(
+        turned[0], turned[1:]
+    )
 
 
 def last_kernel(norm_scale, total_ref, twice_ref, basis_ref, projected_ref):
@@ -173,7 +171,7 @@
 def xor_sum(value, others):
     level = [value, *others]
     while len(level) > 1:
-        level = [level[i] + level[i + 1] for i in range(0, len(level), 2)]
+        level = [sum(level[i + 1 : i + 2], level[i]) for i in range(0, len(level), 2)]
     return level[0]
 
 
@@ -221,19 +219,24 @@
         if not few:
             return lax.psum(value, "col")
         mask = opposite if crossed else 0
-        own = send(value, stay, mask) if crossed else value
-        steps = range(1, col_count)
-        return xor_sum(
-            own, [send(value, [((a, c), (a, c ^ step)) for a, c in chips], mask) for step in steps]
-        )
-
-    def plane_sum(value):
-        if not few:
-            return lax.psum(value, "row") * (1.0 / ratio)
-        steps = range(1, col_count)
-        return xor_sum(
-            value, [send(value, [((a, c), (a ^ step, c)) for a, c in chips]) for step in steps]
-        )
+        sums = {0: value}
+        for step in range(col_count):
+            if step or crossed:
+                sums[step] = send(value, [((a, c), (a, c ^ step)) for a, c in chips], mask)
+        order = [step ^ 1 for step in range(col_count)]
+        return xor_sum(sums[order[0]], [sums[step] for step in order[1:]])
+
+    def over_planes(value):
+        if few:
+            terms = {0: value}
+            for step in range(1, col_count):
+                terms[step] = send(value, [((a, c), (a ^ step, c)) for a, c in chips])
+            return [terms[step] for step in reversed(range(col_count))]
+        rest, terms = lax.psum(value, "row") * (1.0 / ratio), []
+        for _ in range(3):
+            terms.append(rest.astype(jnp.bfloat16))
+            rest = rest - terms[-1].astype(f32)
+        return terms
 
     def whole_slab(part):
         parts = of_chip(part)
@@ -250,24 +253,24 @@
     flops = 2 * vectors * block_total * block_size**2
     bytes_accessed = 2 * block_total * block_size**2
     part_shape = jax.ShapeDtypeStruct((vectors, row_width), f32)
-    slab_shape = jax.ShapeDtypeStruct((vectors, col_width), f32)
+    slab_shape = jax.ShapeDtypeStruct((vectors, col_width), jnp.bfloat16 if few else f32)
     pieces = pltpu.VMEM((col_blocks, vectors, block_size), start_block.dtype)
 
-    def forward_of(source, *term):
+    def forward_of(source):
         tile = [arrays[opposite if crossed else 0] for arrays in tiles]
         return call(
             forward_kernel,
             part_shape,
-            [table] * 2 + [vmem] * (2 + len(term)),
+            [table] * 2 + [vmem] * 2,
             [pieces, pltpu.VMEM((row_blocks, vectors, block_size), f32)],
             flops,
             bytes_accessed,
-        )(*tile, source, *term)
-
-    def backward_of(source, outputs):
+        )(*tile, source)
+
+    def backward_of(source, out_shape, mask):
         return call(
-            functools.partial(backward_kernel, ratio, 0 if crossed else opposite),
-            [part_shape, slab_shape][:outputs],
+            functools.partial(backward_kernel, ratio, mask),
+            out_shape,
             [table] * (2 * ratio) + [vmem] * (ratio + 1),
             [pieces, pltpu.VMEM((ratio, col_blocks, vectors, block_size), f32)],
             ratio * flops,
@@ -277,23 +280,23 @@
     start_rows = send(start_block, gather_pairs)
     forward = forward_of(start_block)
     start_rows, forward = lax.optimization_barrier((start_rows, forward))
-    backward = send(backward_of(start_rows, 1)[0], gather_pairs)
+    backward = backward_of(start_rows, part_shape, 0 if crossed else opposite)
+    backward = send(backward, gather_pairs)
     applied_once = col_sum(forward + backward).astype(jnp.bfloat16)
 
     once = whole_slab(applied_once)
     once_columns = send(once, spread_pairs)
-    backward, backward_whole = backward_of(once, 2)
-    backward = send(backward, gather_pairs)
-    grams = call(
-        functools.partial(gram_kernel, 1.0 / col_count),
-        jax.ShapeDtypeStruct((vectors, 128), f32),
-        [vmem] * 3,
+    terms = over_planes(backward_of(once, slab_shape, None))
+    forward = forward_of(once_columns)
+    message = call(
+        functools.partial(merge_kernel, ratio, opposite if crossed else 0),
+        jax.ShapeDtypeStruct((vectors, row_width + 128), f32),
+        [vmem] * (3 + len(terms)),
         (),
         8 * vectors * vectors * col_width,
         8 * vectors * col_width,
-    )(start_block, once_columns, backward_whole)
-    grams = plane_sum(grams)
-    total = col_sum(jnp.concatenate([forward_of(once_columns, backward), grams], axis=1))
+    )(start_block, once_columns, forward, *terms)
+    total = col_sum(message)
     small = jax.ShapeDtypeStruct((2 * vectors, 2 * vectors), f32)
     applied_twice, basis_gram, projected_gram = call(
         functools.partial(last_kernel, norm_scale),

time: 39.4 us -> 37.5 us (0.952)
  waiting for transfers between devices: 13.5 us -> 12.1 us
  starting transfers between devices: 21.5 us -> 21 us
    ppermute x19 -> x18, waiting for transfers between devices: 13.5 us -> 12.1 us  [send(): lax.ppermute(value, both, [(device(*source, member), device(*target, memb...]
    ppermute x19 -> x18, starting transfers between devices: 21.5 us -> 21 us  [send(): lax.ppermute(value, both, [(device(*source, member), device(*target, memb...]
  transfers between devices with their start and end apart: 19 -> 18, of which waited for: 12 -> 11; matrix products, arithmetic and copies ran while one was open for 0% -> 0% of each run, Pallas kernels for 4% -> 3%
where the time goes in v5:
time: 37.5 us; the launch traced here: 37.4 us
  starting transfers between devices  21 us (56%)
  waiting for transfers between devices  12.1 us (32%)
  Pallas kernels  2.73 us (7%)
  local copies, waits for them, and re-layouts  0.78 us (2%)
  between operations  0.71 us (2%)
    ppermute x18, starting transfers between devices, send(): lax.ppermute(value, both, [(device(*source, member), device(*target, memb...  21 us
    ppermute x18, waiting for transfers between devices, send(): lax.ppermute(value, both, [(device(*source, member), device(*target, memb...  12.1 us
    pallas_call x2, Pallas kernels, backward_of(): call(functools.partial(backward_kernel, ratio, mask), out_shape, [table]...  0.86 us
    pallas_call x2, Pallas kernels, forward_of(): call(forward_kernel, part_shape, [table] * 2 + [vmem] * 2, [pieces, pltpu...  0.8 us
    unnamed x12, local copies, waits for them, and re-layouts  0.78 us
  transfers between devices with their start and end apart: 18, of which 11 were waited for; matrix products, arithmetic and copies ran while one was open for 0% of the time, Pallas kernels for 3%

profile of v5, /device:TPU:0, one launch (start us, length us, event | category | flops | bytes accessed | tf_op | source)
XLA Modules:
  0.0 37.4 jit_solution(8202529969813904769)
XLA Ops:
  0.6 0.5 %collective-permute-start.3 = (bf16[12,128,128]{2,1,0:T(8,128)(2,1)}, bf16[12,128,128]{2,1,0:T(8,128)(2,1)S(1)}, u32[]{:S(2)}, u32[]{:S(2)}) collective-permute-start(bf16[12,128,128]{2,1,0:T(8,128)(2,1)} %bitcast.3), channel_id=1, source_target_pairs={{0,4},{4,0},{1,5},{5,1},{2,6},{6,2},{3,7},{7,3},{8,12},{12,8},{9,1... | collective-permute-start | bytes 1179656 | tf_op jit(solution)/shard_map/ppermute | solution.py:201
  1.2 3.6 %collective-permute-start = (bf16[16,1024]{1,0:T(8,128)(2,1)}, bf16[16,1024]{1,0:T(8,128)(2,1)S(1)}, u32[]{:S(2)}, u32[]{:S(2)}) collective-permute-start(bf16[16,1024]{1,0:T(8,128)(2,1)} %start_ref.1), channel_id=1, source_target_pairs={{24,4},{28,0},{16,5},{20,1},{8,6},{12,2},{0,7},{4,3},{25,13},{29,9... | collective-permute-start | bytes 98312 | tf_op jit(solution)/shard_map/ppermute | solution.py:201
  4.8 0.4 %collective-permute-start.2 = (s32[1,4]{1,0:T(1,128)}, s32[1,4]{1,0:T(1,128)S(1)}, u32[]{:S(2)}, u32[]{:S(2)}) collective-permute-start(s32[1,4]{1,0:T(1,128)} %bitcast.9), channel_id=1, source_target_pairs={{0,4},{4,0},{1,5},{5,1},{2,6},{6,2},{3,7},{7,3},{8,12},{12,8},{9,1... | collective-permute-start | bytes 56 | tf_op jit(solution)/shard_map/ppermute | solution.py:201
  5.2 1.0 %collective-permute-done.2.counts_ref.refs_3_ = s32[1,4]{1,0:T(1,128)S(1)} collective-permute-done((s32[1,4]{1,0:T(1,128)}, s32[1,4]{1,0:T(1,128)S(1)}, u32[]{:S(2)}, u32[]{:S(2)}) %collective-permute-start.2) | collective-permute-done | bytes 48 | tf_op jit(solution)/shard_map/ppermute | solution.py:201
  6.2 0.8 %copy-done.1 = bf16[16,1024]{1,0:T(8,128)(2,1)S(1)} copy-done((bf16[16,1024]{1,0:T(8,128)(2,1)S(1)}, bf16[16,1024]{1,0:T(8,128)(2,1)}, u32[]{:S(2)}) %copy-start.1) | copy-done | bytes 32792
  7.4 0.6 %collective-permute-done.refs_6_ = bf16[16,1024]{1,0:T(8,128)(2,1)S(1)} collective-permute-done((bf16[16,1024]{1,0:T(8,128)(2,1)}, bf16[16,1024]{1,0:T(8,128)(2,1)S(1)}, u32[]{:S(2)}, u32[]{:S(2)}) %collective-permute-start) | collective-permute-done | bytes 32800 | tf_op jit(solution)/shard_map/ppermute | solution.py:201
  8.0 0.4 %shard_map.76 = f32[16,512]{1,0:T(8,128)S(1)} custom-call(s32[1,12]{1,0:T(1,128)S(1)} %bitcast.7, s32[1,12]{1,0:T(1,128)S(1)} %collective-permute-done.1.columns_ref.refs_1_, s32[1,4]{1,0:T(1,128)S(1)} %bitcast.10, s32[1,4]{1,0:T(1,128)S(1)} %collective-permute-done.2.counts_ref.refs_3_, bf16[12,128,128]{2,1,0:T(8,128)(2,1)S(1)} %bitcast.4, ...), custom_call_target="tpu_custom_call" | custom-call | flops 12582912 | bytes 786432 | tf_op jit(solution)/shard_map/pallas_call | solution.py:271
  8.4 3.2 %collective-permute-start.4 = (f32[16,512]{1,0:T(8,128)S(1)}, f32[16,512]{1,0:T(8,128)S(1)}, u32[]{:S(2)}, u32[]{:S(2)}) collective-permute-start(f32[16,512]{1,0:T(8,128)S(1)} %shard_map.76), channel_id=1, source_target_pairs={{24,4},{28,0},{16,5},{20,1},{8,6},{12,2},{0,7},{4,3},{25,13},{29,9... | collective-permute-start | bytes 98312 | tf_op jit(solution)/shard_map/ppermute | solution.py:201
  11.6 2.2 %collective-permute-done.4 = f32[16,512]{1,0:T(8,128)S(1)} collective-permute-done((f32[16,512]{1,0:T(8,128)S(1)}, f32[16,512]{1,0:T(8,128)S(1)}, u32[]{:S(2)}, u32[]{:S(2)}) %collective-permute-start.4) | collective-permute-done | bytes 32800 | tf_op jit(solution)/shard_map/ppermute | solution.py:201
  13.8 2.1 %collective-permute-start.7 = (f32[16,512]{1,0:T(8,128)S(1)}, f32[16,512]{1,0:T(8,128)S(1)}, u32[]{:S(2)}, u32[]{:S(2)}) collective-permute-start(f32[16,512]{1,0:T(8,128)S(1)} %add.25), channel_id=1, source_target_pairs={{0,7},{4,3},{1,6},{5,2},{2,5},{6,1},{3,4},{7,0},{8,15},{12,11},{9,... | collective-permute-start | bytes 98312 | tf_op jit(solution)/shard_map/ppermute | solution.py:201
  15.9 1.4 %collective-permute-start.8 = (f32[16,512]{1,0:T(8,128)S(1)}, f32[16,512]{1,0:T(8,128)S(1)}, u32[]{:S(2)}, u32[]{:S(2)}) collective-permute-start(f32[16,512]{1,0:T(8,128)S(1)} %add.25), channel_id=1, source_target_pairs={{0,6},{4,2},{1,7},{5,3},{2,4},{6,0},{3,5},{7,1},{8,14},{12,10},{9,... | collective-permute-start | bytes 98312 | tf_op jit(solution)/shard_map/ppermute | solution.py:201
  17.4 0.8 %collective-permute-done.7 = f32[16,512]{1,0:T(8,128)S(1)} collective-permute-done((f32[16,512]{1,0:T(8,128)S(1)}, f32[16,512]{1,0:T(8,128)S(1)}, u32[]{:S(2)}, u32[]{:S(2)}) %collective-permute-start.7) | collective-permute-done | bytes 32800 | tf_op jit(solution)/shard_map/ppermute | solution.py:201
  18.1 1.1 %collective-permute-done.8 = f32[16,512]{1,0:T(8,128)S(1)} collective-permute-done((f32[16,512]{1,0:T(8,128)S(1)}, f32[16,512]{1,0:T(8,128)S(1)}, u32[]{:S(2)}, u32[]{:S(2)}) %collective-permute-start.8) | collective-permute-done | bytes 32800 | tf_op jit(solution)/shard_map/ppermute | solution.py:201
  19.2 1.5 %collective-permute-done.5 = f32[16,512]{1,0:T(8,128)S(1)} collective-permute-done((f32[16,512]{1,0:T(8,128)S(1)}, f32[16,512]{1,0:T(8,128)S(1)}, u32[]{:S(2)}, u32[]{:S(2)}) %collective-permute-start.5) | collective-permute-done | bytes 32800 | tf_op jit(solution)/shard_map/ppermute | solution.py:201
  21.0 1.1 %collective-permute-done.9 = bf16[16,512]{1,0:T(8,128)(2,1)S(1)} collective-permute-done((bf16[16,512]{1,0:T(8,128)(2,1)S(1)}, bf16[16,512]{1,0:T(8,128)(2,1)S(1)}, u32[]{:S(2)}, u32[]{:S(2)}) %collective-permute-start.9) | collective-permute-done | bytes 16416 | tf_op jit(solution)/shard_map/ppermute | solution.py:201
  22.0 2.2 %collective-permute-start.10 = (bf16[16,1024]{1,0:T(8,128)(2,1)S(1)}, bf16[16,1024]{1,0:T(8,128)(2,1)S(1)}, u32[]{:S(2)}, u32[]{:S(2)}) collective-permute-start(bf16[16,1024]{1,0:T(8,128)(2,1)S(1)} %pad_maximum_fusion.refs_6_), channel_id=1, source_target_pairs={{0,28},{4,24},{1,20},{5,16},{2,12},{6,8},{3,4},{7,0},{9,29},{13,25... | collective-permute-start | bytes 98312 | tf_op jit(solution)/shard_map/ppermute | solution.py:201
  24.2 0.4 %shard_map.78.refs_3_ = bf16[16,1024]{1,0:T(8,128)(2,1)S(1)} custom-call(s32[1,12]{1,0:T(1,128)S(1)} %bitcast.8, s32[1,12]{1,0:T(1,128)S(1)} %collective-permute-done.1.columns_ref.refs_1_, s32[1,4]{1,0:T(1,128)S(1)} %bitcast.11, s32[1,4]{1,0:T(1,128)S(1)} %collective-permute-done.2.counts_ref.refs_3_, bf16[12,128,128]{2,1,0:T(8,128)(2,1)S(1)} %bitcast.5, ...), custom_call_target="tpu_custom_call" | custom-call | flops 12582912 | bytes 786432 | tf_op jit(solution)/shard_map/pallas_call | solution.py:271
  24.7 1.1 %collective-permute-start.11 = (bf16[16,1024]{1,0:T(8,128)(2,1)S(1)}, bf16[16,1024]{1,0:T(8,128)(2,1)S(1)}, u32[]{:S(2)}, u32[]{:S(2)}) collective-permute-start(bf16[16,1024]{1,0:T(8,128)(2,1)S(1)} %shard_map.78.refs_3_), channel_id=1, source_target_pairs={{0,28},{4,24},{1,29},{5,25},{2,30},{6,26},{3,31},{7,27},{8,20},{12... | collective-permute-start | bytes 98312 | tf_op jit(solution)/shard_map/ppermute | solution.py:201
  25.8 2.8 %collective-permute-start.13 = (bf16[16,1024]{1,0:T(8,128)(2,1)S(1)}, bf16[16,1024]{1,0:T(8,128)(2,1)S(1)}, u32[]{:S(2)}, u32[]{:S(2)}) collective-permute-start(bf16[16,1024]{1,0:T(8,128)(2,1)S(1)} %shard_map.78.refs_3_), channel_id=1, source_target_pairs={{0,12},{4,8},{1,13},{5,9},{2,14},{6,10},{3,15},{7,11},{8,4},{12,0}... | collective-permute-start | bytes 98312 | tf_op jit(solution)/shard_map/ppermute | solution.py:201
  29.0 0.9 %collective-permute-done.11.refs_0_ = bf16[16,1024]{1,0:T(8,128)(2,1)S(1)} collective-permute-done((bf16[16,1024]{1,0:T(8,128)(2,1)S(1)}, bf16[16,1024]{1,0:T(8,128)(2,1)S(1)}, u32[]{:S(2)}, u32[]{:S(2)}) %collective-permute-start.11) | collective-permute-done | bytes 32800 | tf_op jit(solution)/shard_map/ppermute | solution.py:201
  29.9 1.7 %collective-permute-done.12.refs_1_ = bf16[16,1024]{1,0:T(8,128)(2,1)S(1)} collective-permute-done((bf16[16,1024]{1,0:T(8,128)(2,1)S(1)}, bf16[16,1024]{1,0:T(8,128)(2,1)S(1)}, u32[]{:S(2)}, u32[]{:S(2)}) %collective-permute-start.12) | collective-permute-done | bytes 32800 | tf_op jit(solution)/shard_map/ppermute | solution.py:201
  32.6 2.3 %collective-permute-start.14 = (f32[16,640]{1,0:T(8,128)S(1)}, f32[16,640]{1,0:T(8,128)S(1)}, u32[]{:S(2)}, u32[]{:S(2)}) collective-permute-start(f32[16,640]{1,0:T(8,128)S(1)} %shard_map.79), channel_id=1, source_target_pairs={{0,5},{4,1},{1,4},{5,0},{2,7},{6,3},{3,6},{7,2},{8,13},{12,9},{9,1... | collective-permute-start | bytes 122888 | tf_op jit(solution)/shard_map/ppermute | solution.py:201
  35.4 1.2 %collective-permute-done.16 = f32[16,640]{1,0:T(8,128)S(1)} collective-permute-done((f32[16,640]{1,0:T(8,128)S(1)}, f32[16,640]{1,0:T(8,128)S(1)}, u32[]{:S(2)}, u32[]{:S(2)}) %collective-permute-start.16) | collective-permute-done | bytes 40992 | tf_op jit(solution)/shard_map/ppermute | solution.py:201
  36.7 0.7 %shard_map.80 = (bf16[16,512]{1,0:T(8,128)(2,1)}, f32[32,32]{1,0:T(8,128)}, f32[32,32]{1,0:T(8,128)}) custom-call(f32[16,640]{1,0:T(8,128)S(1)} %add_add_fusion.total_ref), custom_call_target="tpu_custom_call" | custom-call | tf_op jit(solution)/shard_map/pallas_call | solution.py:301
  (35 shorter events, 2.7 us)
Async XLA Ops:
  0.6 7.3 %copy-start = (bf16[1,1,12,128,128]{4,3,2,1,0:T(8,128)(2,1)S(1)}, bf16[1,1,12,128,128]{4,3,2,1,0:T(8,128)(2,1)}, u32[]{:S(2)}) copy-start(bf16[1,1,12,128,128]{4,3,2,1,0:T(8,128)(2,1)} %param.5) | copy-start | bytes 1179652
  0.6 5.5 %collective-permute-start.3 = (bf16[12,128,128]{2,1,0:T(8,128)(2,1)}, bf16[12,128,128]{2,1,0:T(8,128)(2,1)S(1)}, u32[]{:S(2)}, u32[]{:S(2)}) collective-permute-start(bf16[12,128,128]{2,1,0:T(8,128)(2,1)} %bitcast.3), channel_id=1, source_target_pairs={{0,4},{4,0},{1,5},{5,1},{2,6},{6,2},{3,7},{7,3},{8,12},{12,8},{9,1... | collective-permute-start | bytes 1179656 | tf_op jit(solution)/shard_map/ppermute | solution.py:201
  1.2 6.8 %collective-permute-start = (bf16[16,1024]{1,0:T(8,128)(2,1)}, bf16[16,1024]{1,0:T(8,128)(2,1)S(1)}, u32[]{:S(2)}, u32[]{:S(2)}) collective-permute-start(bf16[16,1024]{1,0:T(8,128)(2,1)} %start_ref.1), channel_id=1, source_target_pairs={{24,4},{28,0},{16,5},{20,1},{8,6},{12,2},{0,7},{4,3},{25,13},{29,9... | collective-permute-start | bytes 98312 | tf_op jit(solution)/shard_map/ppermute | solution.py:201
  4.7 1.5 %collective-permute-start.1 = (s32[1,12]{1,0:T(1,128)}, s32[1,12]{1,0:T(1,128)S(1)}, u32[]{:S(2)}, u32[]{:S(2)}) collective-permute-start(s32[1,12]{1,0:T(1,128)} %bitcast.6), channel_id=1, source_target_pairs={{0,4},{4,0},{1,5},{5,1},{2,6},{6,2},{3,7},{7,3},{8,12},{12,8},{9,1... | collective-permute-start | bytes 152 | tf_op jit(solution)/shard_map/ppermute | solution.py:201
  4.8 1.4 %collective-permute-start.2 = (s32[1,4]{1,0:T(1,128)}, s32[1,4]{1,0:T(1,128)S(1)}, u32[]{:S(2)}, u32[]{:S(2)}) collective-permute-start(s32[1,4]{1,0:T(1,128)} %bitcast.9), channel_id=1, source_target_pairs={{0,4},{4,0},{1,5},{5,1},{2,6},{6,2},{3,7},{7,3},{8,12},{12,8},{9,1... | collective-permute-start | bytes 56 | tf_op jit(solution)/shard_map/ppermute | solution.py:201
  6.2 0.8 %copy-start.1 = (bf16[16,1024]{1,0:T(8,128)(2,1)S(1)}, bf16[16,1024]{1,0:T(8,128)(2,1)}, u32[]{:S(2)}) copy-start(bf16[16,1024]{1,0:T(8,128)(2,1)} %start_ref.1) | copy-start | bytes 98308
  6.9 1.0 %copy-start.3 = (s32[1,1,12]{2,1,0:T(1,128)S(1)}, s32[1,1,12]{2,1,0:T(1,128)}, u32[]{:S(2)}) copy-start(s32[1,1,12]{2,1,0:T(1,128)} %param.6) | copy-start | bytes 148
  7.0 1.0 %copy-start.4 = (s32[1,1,4]{2,1,0:T(1,128)S(1)}, s32[1,1,4]{2,1,0:T(1,128)}, u32[]{:S(2)}) copy-start(s32[1,1,4]{2,1,0:T(1,128)} %param.7) | copy-start | bytes 52
  8.4 5.4 %collective-permute-start.4 = (f32[16,512]{1,0:T(8,128)S(1)}, f32[16,512]{1,0:T(8,128)S(1)}, u32[]{:S(2)}, u32[]{:S(2)}) collective-permute-start(f32[16,512]{1,0:T(8,128)S(1)} %shard_map.76), channel_id=1, source_target_pairs={{24,4},{28,0},{16,5},{20,1},{8,6},{12,2},{0,7},{4,3},{25,13},{29,9... | collective-permute-start | bytes 98312 | tf_op jit(solution)/shard_map/ppermute | solution.py:201
  13.8 4.3 %collective-permute-start.7 = (f32[16,512]{1,0:T(8,128)S(1)}, f32[16,512]{1,0:T(8,128)S(1)}, u32[]{:S(2)}, u32[]{:S(2)}) collective-permute-start(f32[16,512]{1,0:T(8,128)S(1)} %add.25), channel_id=1, source_target_pairs={{0,7},{4,3},{1,6},{5,2},{2,5},{6,1},{3,4},{7,0},{8,15},{12,11},{9,... | collective-permute-start | bytes 98312 | tf_op jit(solution)/shard_map/ppermute | solution.py:201
  15.9 3.3 %collective-permute-start.8 = (f32[16,512]{1,0:T(8,128)S(1)}, f32[16,512]{1,0:T(8,128)S(1)}, u32[]{:S(2)}, u32[]{:S(2)}) collective-permute-start(f32[16,512]{1,0:T(8,128)S(1)} %add.25), channel_id=1, source_target_pairs={{0,6},{4,2},{1,7},{5,3},{2,4},{6,0},{3,5},{7,1},{8,14},{12,10},{9,... | collective-permute-start | bytes 98312 | tf_op jit(solution)/shard_map/ppermute | solution.py:201
  17.3 3.5 %collective-permute-start.5 = (f32[16,512]{1,0:T(8,128)S(1)}, f32[16,512]{1,0:T(8,128)S(1)}, u32[]{:S(2)}, u32[]{:S(2)}) collective-permute-start(f32[16,512]{1,0:T(8,128)S(1)} %add.25), channel_id=1, source_target_pairs={{0,5},{4,1},{1,4},{5,0},{2,7},{6,3},{3,6},{7,2},{8,13},{12,9},{9,1... | collective-permute-start | bytes 98312 | tf_op jit(solution)/shard_map/ppermute | solution.py:201
  17.3 3.5 %collective-permute-start.6 = (f32[16,512]{1,0:T(8,128)S(1)}, f32[16,512]{1,0:T(8,128)S(1)}, u32[]{:S(2)}, u32[]{:S(2)}) collective-permute-start(f32[16,512]{1,0:T(8,128)S(1)} %add.25), channel_id=1, source_target_pairs={{0,4},{4,0},{1,5},{5,1},{2,6},{6,2},{3,7},{7,3},{8,12},{12,8},{9,1... | collective-permute-start | bytes 98312 | tf_op jit(solution)/shard_map/ppermute | solution.py:201
  20.8 1.3 %copy-start.5 = (bf16[16,512]{1,0:T(8,128)(2,1)}, bf16[16,512]{1,0:T(8,128)(2,1)S(1)}, u32[]{:S(2)}) copy-start(bf16[16,512]{1,0:T(8,128)(2,1)S(1)} %add_convert_fusion) | copy-start | bytes 49156
  20.8 1.2 %collective-permute-start.9 = (bf16[16,512]{1,0:T(8,128)(2,1)S(1)}, bf16[16,512]{1,0:T(8,128)(2,1)S(1)}, u32[]{:S(2)}, u32[]{:S(2)}) collective-permute-start(bf16[16,512]{1,0:T(8,128)(2,1)S(1)} %add_convert_fusion), channel_id=1, source_target_pairs={{0,4},{4,0},{1,5},{5,1},{2,6},{6,2},{3,7},{7,3},{8,12},{12,8},{9,1... | collective-permute-start | bytes 49160 | tf_op jit(solution)/shard_map/ppermute | solution.py:201
  22.0 6.6 %collective-permute-start.10 = (bf16[16,1024]{1,0:T(8,128)(2,1)S(1)}, bf16[16,1024]{1,0:T(8,128)(2,1)S(1)}, u32[]{:S(2)}, u32[]{:S(2)}) collective-permute-start(bf16[16,1024]{1,0:T(8,128)(2,1)S(1)} %pad_maximum_fusion.refs_6_), channel_id=1, source_target_pairs={{0,28},{4,24},{1,20},{5,16},{2,12},{6,8},{3,4},{7,0},{9,29},{13,25... | collective-permute-start | bytes 98312 | tf_op jit(solution)/shard_map/ppermute | solution.py:201
  24.7 6.9 %copy-start.2 = (bf16[16,1024]{1,0:T(8,128)(2,1)S(1)}, bf16[16,1024]{1,0:T(8,128)(2,1)}, u32[]{:S(2)}) copy-start(bf16[16,1024]{1,0:T(8,128)(2,1)} %start_ref.1) | copy-start | bytes 98308
  24.7 5.2 %collective-permute-start.11 = (bf16[16,1024]{1,0:T(8,128)(2,1)S(1)}, bf16[16,1024]{1,0:T(8,128)(2,1)S(1)}, u32[]{:S(2)}, u32[]{:S(2)}) collective-permute-start(bf16[16,1024]{1,0:T(8,128)(2,1)S(1)} %shard_map.78.refs_3_), channel_id=1, source_target_pairs={{0,28},{4,24},{1,29},{5,25},{2,30},{6,26},{3,31},{7,27},{8,20},{12... | collective-permute-start | bytes 98312 | tf_op jit(solution)/shard_map/ppermute | solution.py:201
  25.8 5.8 %collective-permute-start.12 = (bf16[16,1024]{1,0:T(8,128)(2,1)S(1)}, bf16[16,1024]{1,0:T(8,128)(2,1)S(1)}, u32[]{:S(2)}, u32[]{:S(2)}) collective-permute-start(bf16[16,1024]{1,0:T(8,128)(2,1)S(1)} %shard_map.78.refs_3_), channel_id=1, source_target_pairs={{0,20},{4,16},{1,21},{5,17},{2,22},{6,18},{3,23},{7,19},{8,28},{12... | collective-permute-start | bytes 98312 | tf_op jit(solution)/shard_map/ppermute | solution.py:201
  25.8 5.8 %collective-permute-start.13 = (bf16[16,1024]{1,0:T(8,128)(2,1)S(1)}, bf16[16,1024]{1,0:T(8,128)(2,1)S(1)}, u32[]{:S(2)}, u32[]{:S(2)}) collective-permute-start(bf16[16,1024]{1,0:T(8,128)(2,1)S(1)} %shard_map.78.refs_3_), channel_id=1, source_target_pairs={{0,12},{4,8},{1,13},{5,9},{2,14},{6,10},{3,15},{7,11},{8,4},{12,0}... | collective-permute-start | bytes 98312 | tf_op jit(solution)/shard_map/ppermute | solution.py:201
  32.0 4.6 %collective-permute-start.16 = (f32[16,640]{1,0:T(8,128)S(1)}, f32[16,640]{1,0:T(8,128)S(1)}, u32[]{:S(2)}, u32[]{:S(2)}) collective-permute-start(f32[16,640]{1,0:T(8,128)S(1)} %shard_map.79), channel_id=1, source_target_pairs={{0,7},{4,3},{1,6},{5,2},{2,5},{6,1},{3,4},{7,0},{8,15},{12,11},{9,... | collective-permute-start | bytes 122888 | tf_op jit(solution)/shard_map/ppermute | solution.py:201
  32.4 4.2 %collective-permute-start.17 = (f32[16,640]{1,0:T(8,128)S(1)}, f32[16,640]{1,0:T(8,128)S(1)}, u32[]{:S(2)}, u32[]{:S(2)}) collective-permute-start(f32[16,640]{1,0:T(8,128)S(1)} %shard_map.79), channel_id=1, source_target_pairs={{0,6},{4,2},{1,7},{5,3},{2,4},{6,0},{3,5},{7,1},{8,14},{12,10},{9,... | collective-permute-start | bytes 122888 | tf_op jit(solution)/shard_map/ppermute | solution.py:201
  32.6 4.0 %collective-permute-start.14 = (f32[16,640]{1,0:T(8,128)S(1)}, f32[16,640]{1,0:T(8,128)S(1)}, u32[]{:S(2)}, u32[]{:S(2)}) collective-permute-start(f32[16,640]{1,0:T(8,128)S(1)} %shard_map.79), channel_id=1, source_target_pairs={{0,5},{4,1},{1,4},{5,0},{2,7},{6,3},{3,6},{7,2},{8,13},{12,9},{9,1... | collective-permute-start | bytes 122888 | tf_op jit(solution)/shard_map/ppermute | solution.py:201
  35.0 1.7 %collective-permute-start.15 = (f32[16,640]{1,0:T(8,128)S(1)}, f32[16,640]{1,0:T(8,128)S(1)}, u32[]{:S(2)}, u32[]{:S(2)}) collective-permute-start(f32[16,640]{1,0:T(8,128)S(1)} %shard_map.79), channel_id=1, source_target_pairs={{0,4},{4,0},{1,5},{5,1},{2,6},{6,2},{3,7},{7,3},{8,12},{12,8},{9,1... | collective-permute-start | bytes 122888 | tf_op jit(solution)/shard_map/ppermute | solution.py:201

commit v6 on v5

--- a/solution.py
+++ b/solution.py
@@ -114,6 +114,26 @@
         out_ref[:, index * size : (index + 1) * size] = total(first + index).astype(out_ref.dtype)
 
 
+def one_backward_kernel(columns_ref, counts_ref, values_ref, source_ref, *refs):
+    others, (out_ref, pieces, sums) = refs[:-3], refs[-3:]
+    size = sums.shape[2]
+    split_into(pieces, source_ref)
+    sums[...] = jnp.zeros_like(sums)
+
+    def product(block, row, column):
+        return jnp.dot(pieces[row], block, preferred_element_type=f32)
+
+    products(
+        columns_ref, counts_ref, values_ref, 0, product, sums, lambda row, column: column
+    )
+    for index in range(sums.shape[0]):
+        place = slice(index * size, (index + 1) * size)
+        total = sums[index]
+        for other_ref in others:
+            total = other_ref[:, place] + total
+        out_ref[:, place] = total.astype(out_ref.dtype)
+
+
 def merge_kernel(ratio, mask, start_ref, once_ref, forward_ref, *refs):
     terms = [term_ref[...] for term_ref in refs[:-1]]
     out_ref = refs[-1]
@@ -124,24 +144,28 @@
         dimension_numbers=(((1,), (1,)), ((), ())),
         preferred_element_type=f32,
     )
-    gram = dot(jnp.concatenate([start, once, *terms], axis=0), jnp.concatenate([start, once], axis=0))
-    rows = [gram[place * vectors : (place + 1) * vectors] for place in range(2 + len(terms))]
-    cross = [row[:, vectors:] for row in rows[2:]]
-    turned = [dot(once, term) for term in terms]
+    wide = [term.astype(f32) for term in terms]
+    whole = xor_sum(wide[0], wide[1:])
+    high = whole.astype(jnp.bfloat16)
+    low = (whole - high.astype(f32)).astype(jnp.bfloat16)
+    gram = dot(
+        jnp.concatenate([start, once, high, low], axis=0), jnp.concatenate([start, once], axis=0)
+    )
+    rows = [gram[place * vectors : (place + 1) * vectors] for place in range(4)]
+    cross = rows[2][:, vectors:] + rows[3][:, vectors:]
+    turned = dot(once, high) + dot(once, low)
     row, column = lax.axis_index("row"), lax.axis_index("col")
     part = (row % ratio) ^ mask
     due = row // ratio == column
     backward = jnp.zeros((vectors, width), f32)
     for place in range(ratio):
-        here = [term[:, place * width : (place + 1) * width].astype(f32) for term in terms]
-        backward = jnp.where(due & (part == place), xor_sum(here[0], here[1:]), backward)
+        here = whole[:, place * width : (place + 1) * width]
+        backward = jnp.where(due & (part == place), here, backward)
     out_ref[:, :width] = forward_ref[...] + backward
     out_ref[:, width:] = jnp.zeros((vectors, out_ref.shape[1] - width), f32)
     out_ref[:, width : width + 2 * vectors] = rows[0]
     out_ref[:, width + 2 * vectors : width + 4 * vectors] = rows[1]
-    out_ref[:, width + 4 * vectors : width + 5 * vectors] = xor_sum(cross[0], cross[1:]) + xor_sum(
-        turned[0], turned[1:]
-    )
+    out_ref[:, width + 4 * vectors : width + 5 * vectors] = cross + turned
 
 
 def last_kernel(norm_scale, total_ref, twice_ref, basis_ref, projected_ref):
@@ -223,7 +247,7 @@
         for step in range(col_count):
             if step or crossed:
                 sums[step] = send(value, [((a, c), (a, c ^ step)) for a, c in chips], mask)
-        order = [step ^ 1 for step in range(col_count)]
+        order = list(range(col_count))
         return xor_sum(sums[order[0]], [sums[step] for step in order[1:]])
 
     def over_planes(value):
@@ -231,15 +255,14 @@
             terms = {0: value}
             for step in range(1, col_count):
                 terms[step] = send(value, [((a, c), (a ^ step, c)) for a, c in chips])
-            return [terms[step] for step in reversed(range(col_count))]
+            return [terms[step] for step in range(col_count)]
         rest, terms = lax.psum(value, "row") * (1.0 / ratio), []
         for _ in range(3):
             terms.append(rest.astype(jnp.bfloat16))
             rest = rest - terms[-1].astype(f32)
         return terms
 
-    def whole_slab(part):
-        parts = of_chip(part)
+    def whole_slab(parts):
         slab = []
         for place in range(ratio):
             piece = parts[0]
@@ -277,6 +300,25 @@
             ratio * bytes_accessed,
         )(*tiles[0], *tiles[1], *tiles[2], source)
 
+    def backward_by_tile(parts):
+        total = []
+        for step, part in enumerate(parts):
+            out_dtype = slab_shape.dtype if step == ratio - 1 else f32
+            total = [
+                call(
+                    one_backward_kernel,
+                    jax.ShapeDtypeStruct((vectors, col_width), out_dtype),
+                    [table] * 2 + [vmem] * (2 + len(total)),
+                    [
+                        pltpu.VMEM((row_blocks, vectors, block_size), part.dtype),
+                        pltpu.VMEM((col_blocks, vectors, block_size), f32),
+                    ],
+                    flops,
+                    bytes_accessed,
+                )(*[arrays[step] for arrays in tiles], part, *total)
+            ]
+        return total[0]
+
     start_rows = send(start_block, gather_pairs)
     forward = forward_of(start_block)
     start_rows, forward = lax.optimization_barrier((start_rows, forward))
@@ -284,9 +326,10 @@
     backward = send(backward, gather_pairs)
     applied_once = col_sum(forward + backward).astype(jnp.bfloat16)
 
-    once = whole_slab(applied_once)
+    once_parts = of_chip(applied_once)
+    once = whole_slab(once_parts)
     once_columns = send(once, spread_pairs)
-    terms = over_planes(backward_of(once, slab_shape, None))
+    terms = over_planes(backward_by_tile(once_parts))
     forward = forward_of(once_columns)
     message = call(
         functools.partial(merge_kernel, ratio, opposite if crossed else 0),

time: 37.5 us -> 37.4 us (level)
  waiting for transfers between devices: 12.1 us -> 11.7 us
    pallas_call x0 -> x2, Pallas kernels: none -> 0.65 us  [backward_by_tile(): call(one_backward_kernel, jax.ShapeDtypeStruct((vectors, col_width), out_...]
    pallas_call x2 -> x1, Pallas kernels: 0.86 us -> 0.43 us  [backward_of(): call(functools.partial(backward_kernel, ratio, mask), out_shape, [table]...]
  transfers between devices with their start and end apart: 18 -> 18, of which waited for: 11 -> 11; matrix products, arithmetic and copies ran while one was open for 0% -> 0% of each run, Pallas kernels for 3% -> 4%
where the time goes in v6:
time: 37.4 us; the launch traced here: 37.2 us
  starting transfers between devices  21 us (56%)
  waiting for transfers between devices  11.7 us (31%)
  Pallas kernels  2.89 us (8%)
  local copies, waits for them, and re-layouts  0.78 us (2%)
  between operations  0.71 us (2%)
    ppermute x18, starting transfers between devices, send(): lax.ppermute(value, both, [(device(*source, member), device(*target, memb...  21 us
    ppermute x18, waiting for transfers between devices, send(): lax.ppermute(value, both, [(device(*source, member), device(*target, memb...  11.7 us
    pallas_call x2, Pallas kernels, forward_of(): call(forward_kernel, part_shape, [table] * 2 + [vmem] * 2, [pieces, pltpu...  0.8 us
    unnamed x12, local copies, waits for them, and re-layouts  0.78 us
  transfers between devices with their start and end apart: 18, of which 11 were waited for; matrix products, arithmetic and copies ran while one was open for 0% of the time, Pallas kernels for 4%

profile of v6, /device:TPU:0, one launch (start us, length us, event | category | flops | bytes accessed | tf_op | source)
XLA Modules:
  0.0 37.2 jit_solution(9998896345852408487)
XLA Ops:
  0.6 0.5 %collective-permute-start.3 = (bf16[12,128,128]{2,1,0:T(8,128)(2,1)}, bf16[12,128,128]{2,1,0:T(8,128)(2,1)S(1)}, u32[]{:S(2)}, u32[]{:S(2)}) collective-permute-start(bf16[12,128,128]{2,1,0:T(8,128)(2,1)} %bitcast.3), channel_id=1, source_target_pairs={{0,4},{4,0},{1,5},{5,1},{2,6},{6,2},{3,7},{7,3},{8,12},{12,8},{9,1... | collective-permute-start | bytes 1179656 | tf_op jit(solution)/shard_map/ppermute | solution.py:225
  1.2 3.6 %collective-permute-start = (bf16[16,1024]{1,0:T(8,128)(2,1)}, bf16[16,1024]{1,0:T(8,128)(2,1)S(1)}, u32[]{:S(2)}, u32[]{:S(2)}) collective-permute-start(bf16[16,1024]{1,0:T(8,128)(2,1)} %start_ref.1), channel_id=1, source_target_pairs={{24,4},{28,0},{16,5},{20,1},{8,6},{12,2},{0,7},{4,3},{25,13},{29,9... | collective-permute-start | bytes 98312 | tf_op jit(solution)/shard_map/ppermute | solution.py:225
  4.8 0.4 %collective-permute-start.2 = (s32[1,4]{1,0:T(1,128)}, s32[1,4]{1,0:T(1,128)S(1)}, u32[]{:S(2)}, u32[]{:S(2)}) collective-permute-start(s32[1,4]{1,0:T(1,128)} %bitcast.9), channel_id=1, source_target_pairs={{0,4},{4,0},{1,5},{5,1},{2,6},{6,2},{3,7},{7,3},{8,12},{12,8},{9,1... | collective-permute-start | bytes 56 | tf_op jit(solution)/shard_map/ppermute | solution.py:225
  5.2 1.0 %collective-permute-done.2.counts_ref.refs_3_ = s32[1,4]{1,0:T(1,128)S(1)} collective-permute-done((s32[1,4]{1,0:T(1,128)}, s32[1,4]{1,0:T(1,128)S(1)}, u32[]{:S(2)}, u32[]{:S(2)}) %collective-permute-start.2) | collective-permute-done | bytes 48 | tf_op jit(solution)/shard_map/ppermute | solution.py:225
  6.2 0.8 %copy-done.2 = bf16[16,1024]{1,0:T(8,128)(2,1)S(1)} copy-done((bf16[16,1024]{1,0:T(8,128)(2,1)S(1)}, bf16[16,1024]{1,0:T(8,128)(2,1)}, u32[]{:S(2)}) %copy-start.2) | copy-done | bytes 32792
  7.4 0.6 %collective-permute-done.refs_6_ = bf16[16,1024]{1,0:T(8,128)(2,1)S(1)} collective-permute-done((bf16[16,1024]{1,0:T(8,128)(2,1)}, bf16[16,1024]{1,0:T(8,128)(2,1)S(1)}, u32[]{:S(2)}, u32[]{:S(2)}) %collective-permute-start) | collective-permute-done | bytes 32800 | tf_op jit(solution)/shard_map/ppermute | solution.py:225
  8.0 0.4 %shard_map.76 = f32[16,512]{1,0:T(8,128)S(1)} custom-call(s32[1,12]{1,0:T(1,128)S(1)} %bitcast.7, s32[1,12]{1,0:T(1,128)S(1)} %collective-permute-done.1.columns_ref.refs_1_, s32[1,4]{1,0:T(1,128)S(1)} %bitcast.10, s32[1,4]{1,0:T(1,128)S(1)} %collective-permute-done.2.counts_ref.refs_3_, bf16[12,128,128]{2,1,0:T(8,128)(2,1)S(1)} %bitcast.4, ...), custom_call_target="tpu_custom_call" | custom-call | flops 12582912 | bytes 786432 | tf_op jit(solution)/shard_map/pallas_call | solution.py:294
  8.4 3.2 %collective-permute-start.4 = (f32[16,512]{1,0:T(8,128)S(1)}, f32[16,512]{1,0:T(8,128)S(1)}, u32[]{:S(2)}, u32[]{:S(2)}) collective-permute-start(f32[16,512]{1,0:T(8,128)S(1)} %shard_map.76), channel_id=1, source_target_pairs={{24,4},{28,0},{16,5},{20,1},{8,6},{12,2},{0,7},{4,3},{25,13},{29,9... | collective-permute-start | bytes 98312 | tf_op jit(solution)/shard_map/ppermute | solution.py:225
  11.6 2.2 %collective-permute-done.4 = f32[16,512]{1,0:T(8,128)S(1)} collective-permute-done((f32[16,512]{1,0:T(8,128)S(1)}, f32[16,512]{1,0:T(8,128)S(1)}, u32[]{:S(2)}, u32[]{:S(2)}) %collective-permute-start.4) | collective-permute-done | bytes 32800 | tf_op jit(solution)/shard_map/ppermute | solution.py:225
  13.8 2.0 %collective-permute-start.8 = (f32[16,512]{1,0:T(8,128)S(1)}, f32[16,512]{1,0:T(8,128)S(1)}, u32[]{:S(2)}, u32[]{:S(2)}) collective-permute-start(f32[16,512]{1,0:T(8,128)S(1)} %add.25), channel_id=1, source_target_pairs={{0,7},{4,3},{1,6},{5,2},{2,5},{6,1},{3,4},{7,0},{8,15},{12,11},{9,... | collective-permute-start | bytes 98312 | tf_op jit(solution)/shard_map/ppermute | solution.py:225
  15.9 1.4 %collective-permute-start.7 = (f32[16,512]{1,0:T(8,128)S(1)}, f32[16,512]{1,0:T(8,128)S(1)}, u32[]{:S(2)}, u32[]{:S(2)}) collective-permute-start(f32[16,512]{1,0:T(8,128)S(1)} %add.25), channel_id=1, source_target_pairs={{0,6},{4,2},{1,7},{5,3},{2,4},{6,0},{3,5},{7,1},{8,14},{12,10},{9,... | collective-permute-start | bytes 98312 | tf_op jit(solution)/shard_map/ppermute | solution.py:225
  17.4 0.8 %collective-permute-done.8 = f32[16,512]{1,0:T(8,128)S(1)} collective-permute-done((f32[16,512]{1,0:T(8,128)S(1)}, f32[16,512]{1,0:T(8,128)S(1)}, u32[]{:S(2)}, u32[]{:S(2)}) %collective-permute-start.8) | collective-permute-done | bytes 32800 | tf_op jit(solution)/shard_map/ppermute | solution.py:225
  18.1 1.1 %collective-permute-done.7 = f32[16,512]{1,0:T(8,128)S(1)} collective-permute-done((f32[16,512]{1,0:T(8,128)S(1)}, f32[16,512]{1,0:T(8,128)S(1)}, u32[]{:S(2)}, u32[]{:S(2)}) %collective-permute-start.7) | collective-permute-done | bytes 32800 | tf_op jit(solution)/shard_map/ppermute | solution.py:225
  19.2 1.5 %collective-permute-done.6 = f32[16,512]{1,0:T(8,128)S(1)} collective-permute-done((f32[16,512]{1,0:T(8,128)S(1)}, f32[16,512]{1,0:T(8,128)S(1)}, u32[]{:S(2)}, u32[]{:S(2)}) %collective-permute-start.6) | collective-permute-done | bytes 32800 | tf_op jit(solution)/shard_map/ppermute | solution.py:225
  21.3 0.7 %collective-permute-done.9.source_ref = bf16[16,512]{1,0:T(8,128)(2,1)S(1)} collective-permute-done((bf16[16,512]{1,0:T(8,128)(2,1)S(1)}, bf16[16,512]{1,0:T(8,128)(2,1)S(1)}, u32[]{:S(2)}, u32[]{:S(2)}) %collective-permute-start.9) | collective-permute-done | bytes 16416 | tf_op jit(solution)/shard_map/ppermute | solution.py:225
  22.0 2.2 %collective-permute-start.10 = (bf16[16,1024]{1,0:T(8,128)(2,1)S(1)}, bf16[16,1024]{1,0:T(8,128)(2,1)S(1)}, u32[]{:S(2)}, u32[]{:S(2)}) collective-permute-start(bf16[16,1024]{1,0:T(8,128)(2,1)S(1)} %pad_maximum_fusion), channel_id=1, source_target_pairs={{0,28},{4,24},{1,20},{5,16},{2,12},{6,8},{3,4},{7,0},{9,29},{13,25... | collective-permute-start | bytes 98312 | tf_op jit(solution)/shard_map/ppermute | solution.py:225
  24.6 1.1 %collective-permute-start.13 = (bf16[16,1024]{1,0:T(8,128)(2,1)S(1)}, bf16[16,1024]{1,0:T(8,128)(2,1)S(1)}, u32[]{:S(2)}, u32[]{:S(2)}) collective-permute-start(bf16[16,1024]{1,0:T(8,128)(2,1)S(1)} %shard_map.79.refs_0_), channel_id=1, source_target_pairs={{0,28},{4,24},{1,29},{5,25},{2,30},{6,26},{3,31},{7,27},{8,20},{12... | collective-permute-start | bytes 98312 | tf_op jit(solution)/shard_map/ppermute | solution.py:225
  25.7 2.8 %collective-permute-start.11 = (bf16[16,1024]{1,0:T(8,128)(2,1)S(1)}, bf16[16,1024]{1,0:T(8,128)(2,1)S(1)}, u32[]{:S(2)}, u32[]{:S(2)}) collective-permute-start(bf16[16,1024]{1,0:T(8,128)(2,1)S(1)} %shard_map.79.refs_0_), channel_id=1, source_target_pairs={{0,12},{4,8},{1,13},{5,9},{2,14},{6,10},{3,15},{7,11},{8,4},{12,0}... | collective-permute-start | bytes 98312 | tf_op jit(solution)/shard_map/ppermute | solution.py:225
  28.9 0.9 %collective-permute-done.13.refs_3_ = bf16[16,1024]{1,0:T(8,128)(2,1)S(1)} collective-permute-done((bf16[16,1024]{1,0:T(8,128)(2,1)S(1)}, bf16[16,1024]{1,0:T(8,128)(2,1)S(1)}, u32[]{:S(2)}, u32[]{:S(2)}) %collective-permute-start.13) | collective-permute-done | bytes 32800 | tf_op jit(solution)/shard_map/ppermute | solution.py:225
  29.8 1.7 %collective-permute-done.12.refs_2_ = bf16[16,1024]{1,0:T(8,128)(2,1)S(1)} collective-permute-done((bf16[16,1024]{1,0:T(8,128)(2,1)S(1)}, bf16[16,1024]{1,0:T(8,128)(2,1)S(1)}, u32[]{:S(2)}, u32[]{:S(2)}) %collective-permute-start.12) | collective-permute-done | bytes 32800 | tf_op jit(solution)/shard_map/ppermute | solution.py:225
  32.5 2.3 %collective-permute-start.15 = (f32[16,640]{1,0:T(8,128)S(1)}, f32[16,640]{1,0:T(8,128)S(1)}, u32[]{:S(2)}, u32[]{:S(2)}) collective-permute-start(f32[16,640]{1,0:T(8,128)S(1)} %shard_map.80), channel_id=1, source_target_pairs={{0,5},{4,1},{1,4},{5,0},{2,7},{6,3},{3,6},{7,2},{8,13},{12,9},{9,1... | collective-permute-start | bytes 122888 | tf_op jit(solution)/shard_map/ppermute | solution.py:225
  34.8 0.4 %collective-permute-start.14 = (f32[16,640]{1,0:T(8,128)S(1)}, f32[16,640]{1,0:T(8,128)S(1)}, u32[]{:S(2)}, u32[]{:S(2)}) collective-permute-start(f32[16,640]{1,0:T(8,128)S(1)} %shard_map.80), channel_id=1, source_target_pairs={{0,4},{4,0},{1,5},{5,1},{2,6},{6,2},{3,7},{7,3},{8,12},{12,8},{9,1... | collective-permute-start | bytes 122888 | tf_op jit(solution)/shard_map/ppermute | solution.py:225
  35.2 1.2 %collective-permute-done.17 = f32[16,640]{1,0:T(8,128)S(1)} collective-permute-done((f32[16,640]{1,0:T(8,128)S(1)}, f32[16,640]{1,0:T(8,128)S(1)}, u32[]{:S(2)}, u32[]{:S(2)}) %collective-permute-start.17) | collective-permute-done | bytes 40992 | tf_op jit(solution)/shard_map/ppermute | solution.py:225
  36.5 0.7 %shard_map.81 = (bf16[16,512]{1,0:T(8,128)(2,1)}, f32[32,32]{1,0:T(8,128)}, f32[32,32]{1,0:T(8,128)}) custom-call(f32[16,640]{1,0:T(8,128)S(1)} %add_add_fusion.total_ref), custom_call_target="tpu_custom_call" | custom-call | tf_op jit(solution)/shard_map/pallas_call | solution.py:344
  (36 shorter events, 2.9 us)
Async XLA Ops:
  0.6 7.3 %copy-start = (bf16[1,1,12,128,128]{4,3,2,1,0:T(8,128)(2,1)S(1)}, bf16[1,1,12,128,128]{4,3,2,1,0:T(8,128)(2,1)}, u32[]{:S(2)}) copy-start(bf16[1,1,12,128,128]{4,3,2,1,0:T(8,128)(2,1)} %param.5) | copy-start | bytes 1179652
  0.6 5.5 %collective-permute-start.3 = (bf16[12,128,128]{2,1,0:T(8,128)(2,1)}, bf16[12,128,128]{2,1,0:T(8,128)(2,1)S(1)}, u32[]{:S(2)}, u32[]{:S(2)}) collective-permute-start(bf16[12,128,128]{2,1,0:T(8,128)(2,1)} %bitcast.3), channel_id=1, source_target_pairs={{0,4},{4,0},{1,5},{5,1},{2,6},{6,2},{3,7},{7,3},{8,12},{12,8},{9,1... | collective-permute-start | bytes 1179656 | tf_op jit(solution)/shard_map/ppermute | solution.py:225
  1.2 6.8 %collective-permute-start = (bf16[16,1024]{1,0:T(8,128)(2,1)}, bf16[16,1024]{1,0:T(8,128)(2,1)S(1)}, u32[]{:S(2)}, u32[]{:S(2)}) collective-permute-start(bf16[16,1024]{1,0:T(8,128)(2,1)} %start_ref.1), channel_id=1, source_target_pairs={{24,4},{28,0},{16,5},{20,1},{8,6},{12,2},{0,7},{4,3},{25,13},{29,9... | collective-permute-start | bytes 98312 | tf_op jit(solution)/shard_map/ppermute | solution.py:225
  4.7 1.5 %collective-permute-start.1 = (s32[1,12]{1,0:T(1,128)}, s32[1,12]{1,0:T(1,128)S(1)}, u32[]{:S(2)}, u32[]{:S(2)}) collective-permute-start(s32[1,12]{1,0:T(1,128)} %bitcast.6), channel_id=1, source_target_pairs={{0,4},{4,0},{1,5},{5,1},{2,6},{6,2},{3,7},{7,3},{8,12},{12,8},{9,1... | collective-permute-start | bytes 152 | tf_op jit(solution)/shard_map/ppermute | solution.py:225
  4.8 1.4 %collective-permute-start.2 = (s32[1,4]{1,0:T(1,128)}, s32[1,4]{1,0:T(1,128)S(1)}, u32[]{:S(2)}, u32[]{:S(2)}) collective-permute-start(s32[1,4]{1,0:T(1,128)} %bitcast.9), channel_id=1, source_target_pairs={{0,4},{4,0},{1,5},{5,1},{2,6},{6,2},{3,7},{7,3},{8,12},{12,8},{9,1... | collective-permute-start | bytes 56 | tf_op jit(solution)/shard_map/ppermute | solution.py:225
  6.2 0.8 %copy-start.2 = (bf16[16,1024]{1,0:T(8,128)(2,1)S(1)}, bf16[16,1024]{1,0:T(8,128)(2,1)}, u32[]{:S(2)}) copy-start(bf16[16,1024]{1,0:T(8,128)(2,1)} %start_ref.1) | copy-start | bytes 98308
  6.9 1.0 %copy-start.4 = (s32[1,1,12]{2,1,0:T(1,128)S(1)}, s32[1,1,12]{2,1,0:T(1,128)}, u32[]{:S(2)}) copy-start(s32[1,1,12]{2,1,0:T(1,128)} %param.6) | copy-start | bytes 148
  7.0 1.0 %copy-start.5 = (s32[1,1,4]{2,1,0:T(1,128)S(1)}, s32[1,1,4]{2,1,0:T(1,128)}, u32[]{:S(2)}) copy-start(s32[1,1,4]{2,1,0:T(1,128)} %param.7) | copy-start | bytes 52
  8.4 5.4 %collective-permute-start.4 = (f32[16,512]{1,0:T(8,128)S(1)}, f32[16,512]{1,0:T(8,128)S(1)}, u32[]{:S(2)}, u32[]{:S(2)}) collective-permute-start(f32[16,512]{1,0:T(8,128)S(1)} %shard_map.76), channel_id=1, source_target_pairs={{24,4},{28,0},{16,5},{20,1},{8,6},{12,2},{0,7},{4,3},{25,13},{29,9... | collective-permute-start | bytes 98312 | tf_op jit(solution)/shard_map/ppermute | solution.py:225
  13.8 4.3 %collective-permute-start.8 = (f32[16,512]{1,0:T(8,128)S(1)}, f32[16,512]{1,0:T(8,128)S(1)}, u32[]{:S(2)}, u32[]{:S(2)}) collective-permute-start(f32[16,512]{1,0:T(8,128)S(1)} %add.25), channel_id=1, source_target_pairs={{0,7},{4,3},{1,6},{5,2},{2,5},{6,1},{3,4},{7,0},{8,15},{12,11},{9,... | collective-permute-start | bytes 98312 | tf_op jit(solution)/shard_map/ppermute | solution.py:225
  15.9 3.3 %collective-permute-start.7 = (f32[16,512]{1,0:T(8,128)S(1)}, f32[16,512]{1,0:T(8,128)S(1)}, u32[]{:S(2)}, u32[]{:S(2)}) collective-permute-start(f32[16,512]{1,0:T(8,128)S(1)} %add.25), channel_id=1, source_target_pairs={{0,6},{4,2},{1,7},{5,3},{2,4},{6,0},{3,5},{7,1},{8,14},{12,10},{9,... | collective-permute-start | bytes 98312 | tf_op jit(solution)/shard_map/ppermute | solution.py:225
  17.3 3.5 %collective-permute-start.6 = (f32[16,512]{1,0:T(8,128)S(1)}, f32[16,512]{1,0:T(8,128)S(1)}, u32[]{:S(2)}, u32[]{:S(2)}) collective-permute-start(f32[16,512]{1,0:T(8,128)S(1)} %add.25), channel_id=1, source_target_pairs={{0,5},{4,1},{1,4},{5,0},{2,7},{6,3},{3,6},{7,2},{8,13},{12,9},{9,1... | collective-permute-start | bytes 98312 | tf_op jit(solution)/shard_map/ppermute | solution.py:225
  17.3 3.5 %collective-permute-start.5 = (f32[16,512]{1,0:T(8,128)S(1)}, f32[16,512]{1,0:T(8,128)S(1)}, u32[]{:S(2)}, u32[]{:S(2)}) collective-permute-start(f32[16,512]{1,0:T(8,128)S(1)} %add.25), channel_id=1, source_target_pairs={{0,4},{4,0},{1,5},{5,1},{2,6},{6,2},{3,7},{7,3},{8,12},{12,8},{9,1... | collective-permute-start | bytes 98312 | tf_op jit(solution)/shard_map/ppermute | solution.py:225
  20.8 1.3 %copy-start.1 = (bf16[16,512]{1,0:T(8,128)(2,1)}, bf16[16,512]{1,0:T(8,128)(2,1)S(1)}, u32[]{:S(2)}) copy-start(bf16[16,512]{1,0:T(8,128)(2,1)S(1)} %add_convert_fusion.source_ref) | copy-start | bytes 49156
  20.8 1.2 %collective-permute-start.9 = (bf16[16,512]{1,0:T(8,128)(2,1)S(1)}, bf16[16,512]{1,0:T(8,128)(2,1)S(1)}, u32[]{:S(2)}, u32[]{:S(2)}) collective-permute-start(bf16[16,512]{1,0:T(8,128)(2,1)S(1)} %add_convert_fusion.source_ref), channel_id=1, source_target_pairs={{0,4},{4,0},{1,5},{5,1},{2,6},{6,2},{3,7},{7,3},{8,12},{12,8},{9,1... | collective-permute-start | bytes 49160 | tf_op jit(solution)/shard_map/ppermute | solution.py:225
  22.0 6.5 %collective-permute-start.10 = (bf16[16,1024]{1,0:T(8,128)(2,1)S(1)}, bf16[16,1024]{1,0:T(8,128)(2,1)S(1)}, u32[]{:S(2)}, u32[]{:S(2)}) collective-permute-start(bf16[16,1024]{1,0:T(8,128)(2,1)S(1)} %pad_maximum_fusion), channel_id=1, source_target_pairs={{0,28},{4,24},{1,20},{5,16},{2,12},{6,8},{3,4},{7,0},{9,29},{13,25... | collective-permute-start | bytes 98312 | tf_op jit(solution)/shard_map/ppermute | solution.py:225
  24.6 6.9 %copy-start.3 = (bf16[16,1024]{1,0:T(8,128)(2,1)S(1)}, bf16[16,1024]{1,0:T(8,128)(2,1)}, u32[]{:S(2)}) copy-start(bf16[16,1024]{1,0:T(8,128)(2,1)} %start_ref.1) | copy-start | bytes 98308
  24.6 5.2 %collective-permute-start.13 = (bf16[16,1024]{1,0:T(8,128)(2,1)S(1)}, bf16[16,1024]{1,0:T(8,128)(2,1)S(1)}, u32[]{:S(2)}, u32[]{:S(2)}) collective-permute-start(bf16[16,1024]{1,0:T(8,128)(2,1)S(1)} %shard_map.79.refs_0_), channel_id=1, source_target_pairs={{0,28},{4,24},{1,29},{5,25},{2,30},{6,26},{3,31},{7,27},{8,20},{12... | collective-permute-start | bytes 98312 | tf_op jit(solution)/shard_map/ppermute | solution.py:225
  25.7 5.8 %collective-permute-start.12 = (bf16[16,1024]{1,0:T(8,128)(2,1)S(1)}, bf16[16,1024]{1,0:T(8,128)(2,1)S(1)}, u32[]{:S(2)}, u32[]{:S(2)}) collective-permute-start(bf16[16,1024]{1,0:T(8,128)(2,1)S(1)} %shard_map.79.refs_0_), channel_id=1, source_target_pairs={{0,20},{4,16},{1,21},{5,17},{2,22},{6,18},{3,23},{7,19},{8,28},{12... | collective-permute-start | bytes 98312 | tf_op jit(solution)/shard_map/ppermute | solution.py:225
  25.7 5.8 %collective-permute-start.11 = (bf16[16,1024]{1,0:T(8,128)(2,1)S(1)}, bf16[16,1024]{1,0:T(8,128)(2,1)S(1)}, u32[]{:S(2)}, u32[]{:S(2)}) collective-permute-start(bf16[16,1024]{1,0:T(8,128)(2,1)S(1)} %shard_map.79.refs_0_), channel_id=1, source_target_pairs={{0,12},{4,8},{1,13},{5,9},{2,14},{6,10},{3,15},{7,11},{8,4},{12,0}... | collective-permute-start | bytes 98312 | tf_op jit(solution)/shard_map/ppermute | solution.py:225
  31.8 4.6 %collective-permute-start.17 = (f32[16,640]{1,0:T(8,128)S(1)}, f32[16,640]{1,0:T(8,128)S(1)}, u32[]{:S(2)}, u32[]{:S(2)}) collective-permute-start(f32[16,640]{1,0:T(8,128)S(1)} %shard_map.80), channel_id=1, source_target_pairs={{0,7},{4,3},{1,6},{5,2},{2,5},{6,1},{3,4},{7,0},{8,15},{12,11},{9,... | collective-permute-start | bytes 122888 | tf_op jit(solution)/shard_map/ppermute | solution.py:225
  32.2 4.2 %collective-permute-start.16 = (f32[16,640]{1,0:T(8,128)S(1)}, f32[16,640]{1,0:T(8,128)S(1)}, u32[]{:S(2)}, u32[]{:S(2)}) collective-permute-start(f32[16,640]{1,0:T(8,128)S(1)} %shard_map.80), channel_id=1, source_target_pairs={{0,6},{4,2},{1,7},{5,3},{2,4},{6,0},{3,5},{7,1},{8,14},{12,10},{9,... | collective-permute-start | bytes 122888 | tf_op jit(solution)/shard_map/ppermute | solution.py:225
  32.5 4.0 %collective-permute-start.15 = (f32[16,640]{1,0:T(8,128)S(1)}, f32[16,640]{1,0:T(8,128)S(1)}, u32[]{:S(2)}, u32[]{:S(2)}) collective-permute-start(f32[16,640]{1,0:T(8,128)S(1)} %shard_map.80), channel_id=1, source_target_pairs={{0,5},{4,1},{1,4},{5,0},{2,7},{6,3},{3,6},{7,2},{8,13},{12,9},{9,1... | collective-permute-start | bytes 122888 | tf_op jit(solution)/shard_map/ppermute | solution.py:225
  34.8 1.7 %collective-permute-start.14 = (f32[16,640]{1,0:T(8,128)S(1)}, f32[16,640]{1,0:T(8,128)S(1)}, u32[]{:S(2)}, u32[]{:S(2)}) collective-permute-start(f32[16,640]{1,0:T(8,128)S(1)} %shard_map.80), channel_id=1, source_target_pairs={{0,4},{4,0},{1,5},{5,1},{2,6},{6,2},{3,7},{7,3},{8,12},{12,8},{9,1... | collective-permute-start | bytes 122888 | tf_op jit(solution)/shard_map/ppermute | solution.py:225

commit v7 on v6

--- a/solution.py
+++ b/solution.py
@@ -187,7 +187,7 @@
     pairs = []
     for column in range(col_count):
         planes = sorted(range(col_count), key=lambda a: -abs(a - column))
-        places = sorted(range(col_count), key=lambda c: bin(c ^ column).count("1"))
+        places = sorted(range(col_count), key=lambda c: (bin(c ^ column).count("1"), c ^ column))
         pairs += [((plane, column), (column, place)) for plane, place in zip(planes, places)]
     return pairs
 

time: 37.4 us -> 37.1 us (level)
  no operation moved by 1% of the time
where the time goes in v7:
time: 37.1 us; the launch traced here: 36.8 us
  starting transfers between devices  20.7 us (56%)
  waiting for transfers between devices  11.7 us (32%)
  Pallas kernels  2.88 us (8%)
  local copies, waits for them, and re-layouts  0.78 us (2%)
  between operations  0.71 us (2%)
    ppermute x18, starting transfers between devices, send(): lax.ppermute(value, both, [(device(*source, member), device(*target, memb...  20.7 us
    ppermute x18, waiting for transfers between devices, send(): lax.ppermute(value, both, [(device(*source, member), device(*target, memb...  11.7 us
    pallas_call x2, Pallas kernels, forward_of(): call(forward_kernel, part_shape, [table] * 2 + [vmem] * 2, [pieces, pltpu...  0.79 us
    unnamed x12, local copies, waits for them, and re-layouts  0.78 us
  transfers between devices with their start and end apart: 18, of which 11 were waited for; matrix products, arithmetic and copies ran while one was open for 0% of the time, Pallas kernels for 4%

profile of v7, /device:TPU:0, one launch (start us, length us, event | category | flops | bytes accessed | tf_op | source)
XLA Modules:
  0.0 36.8 jit_solution(16516442725962835222)
XLA Ops:
  0.6 0.5 %collective-permute-start.3 = (bf16[12,128,128]{2,1,0:T(8,128)(2,1)}, bf16[12,128,128]{2,1,0:T(8,128)(2,1)S(1)}, u32[]{:S(2)}, u32[]{:S(2)}) collective-permute-start(bf16[12,128,128]{2,1,0:T(8,128)(2,1)} %bitcast.3), channel_id=1, source_target_pairs={{0,4},{4,0},{1,5},{5,1},{2,6},{6,2},{3,7},{7,3},{8,12},{12,8},{9,1... | collective-permute-start | bytes 1179656 | tf_op jit(solution)/shard_map/ppermute | solution.py:225
  1.2 3.6 %collective-permute-start = (bf16[16,1024]{1,0:T(8,128)(2,1)}, bf16[16,1024]{1,0:T(8,128)(2,1)S(1)}, u32[]{:S(2)}, u32[]{:S(2)}) collective-permute-start(bf16[16,1024]{1,0:T(8,128)(2,1)} %start_ref.1), channel_id=1, source_target_pairs={{24,4},{28,0},{16,5},{20,1},{8,6},{12,2},{0,7},{4,3},{25,13},{29,9... | collective-permute-start | bytes 98312 | tf_op jit(solution)/shard_map/ppermute | solution.py:225
  4.8 0.4 %collective-permute-start.2 = (s32[1,4]{1,0:T(1,128)}, s32[1,4]{1,0:T(1,128)S(1)}, u32[]{:S(2)}, u32[]{:S(2)}) collective-permute-start(s32[1,4]{1,0:T(1,128)} %bitcast.9), channel_id=1, source_target_pairs={{0,4},{4,0},{1,5},{5,1},{2,6},{6,2},{3,7},{7,3},{8,12},{12,8},{9,1... | collective-permute-start | bytes 56 | tf_op jit(solution)/shard_map/ppermute | solution.py:225
  5.2 1.0 %collective-permute-done.2.counts_ref.refs_3_ = s32[1,4]{1,0:T(1,128)S(1)} collective-permute-done((s32[1,4]{1,0:T(1,128)}, s32[1,4]{1,0:T(1,128)S(1)}, u32[]{:S(2)}, u32[]{:S(2)}) %collective-permute-start.2) | collective-permute-done | bytes 48 | tf_op jit(solution)/shard_map/ppermute | solution.py:225
  6.2 0.8 %copy-done.2 = bf16[16,1024]{1,0:T(8,128)(2,1)S(1)} copy-done((bf16[16,1024]{1,0:T(8,128)(2,1)S(1)}, bf16[16,1024]{1,0:T(8,128)(2,1)}, u32[]{:S(2)}) %copy-start.2) | copy-done | bytes 32792
  7.3 0.6 %collective-permute-done.refs_6_ = bf16[16,1024]{1,0:T(8,128)(2,1)S(1)} collective-permute-done((bf16[16,1024]{1,0:T(8,128)(2,1)}, bf16[16,1024]{1,0:T(8,128)(2,1)S(1)}, u32[]{:S(2)}, u32[]{:S(2)}) %collective-permute-start) | collective-permute-done | bytes 32800 | tf_op jit(solution)/shard_map/ppermute | solution.py:225
  8.4 3.2 %collective-permute-start.4 = (f32[16,512]{1,0:T(8,128)S(1)}, f32[16,512]{1,0:T(8,128)S(1)}, u32[]{:S(2)}, u32[]{:S(2)}) collective-permute-start(f32[16,512]{1,0:T(8,128)S(1)} %shard_map.76), channel_id=1, source_target_pairs={{24,4},{28,0},{16,5},{20,1},{8,6},{12,2},{0,7},{4,3},{25,13},{29,9... | collective-permute-start | bytes 98312 | tf_op jit(solution)/shard_map/ppermute | solution.py:225
  11.6 2.2 %collective-permute-done.4 = f32[16,512]{1,0:T(8,128)S(1)} collective-permute-done((f32[16,512]{1,0:T(8,128)S(1)}, f32[16,512]{1,0:T(8,128)S(1)}, u32[]{:S(2)}, u32[]{:S(2)}) %collective-permute-start.4) | collective-permute-done | bytes 32800 | tf_op jit(solution)/shard_map/ppermute | solution.py:225
  13.8 2.1 %collective-permute-start.8 = (f32[16,512]{1,0:T(8,128)S(1)}, f32[16,512]{1,0:T(8,128)S(1)}, u32[]{:S(2)}, u32[]{:S(2)}) collective-permute-start(f32[16,512]{1,0:T(8,128)S(1)} %add.25), channel_id=1, source_target_pairs={{0,7},{4,3},{1,6},{5,2},{2,5},{6,1},{3,4},{7,0},{8,15},{12,11},{9,... | collective-permute-start | bytes 98312 | tf_op jit(solution)/shard_map/ppermute | solution.py:225
  15.9 1.4 %collective-permute-start.7 = (f32[16,512]{1,0:T(8,128)S(1)}, f32[16,512]{1,0:T(8,128)S(1)}, u32[]{:S(2)}, u32[]{:S(2)}) collective-permute-start(f32[16,512]{1,0:T(8,128)S(1)} %add.25), channel_id=1, source_target_pairs={{0,6},{4,2},{1,7},{5,3},{2,4},{6,0},{3,5},{7,1},{8,14},{12,10},{9,... | collective-permute-start | bytes 98312 | tf_op jit(solution)/shard_map/ppermute | solution.py:225
  17.4 0.8 %collective-permute-done.8 = f32[16,512]{1,0:T(8,128)S(1)} collective-permute-done((f32[16,512]{1,0:T(8,128)S(1)}, f32[16,512]{1,0:T(8,128)S(1)}, u32[]{:S(2)}, u32[]{:S(2)}) %collective-permute-start.8) | collective-permute-done | bytes 32800 | tf_op jit(solution)/shard_map/ppermute | solution.py:225
  18.1 1.1 %collective-permute-done.7 = f32[16,512]{1,0:T(8,128)S(1)} collective-permute-done((f32[16,512]{1,0:T(8,128)S(1)}, f32[16,512]{1,0:T(8,128)S(1)}, u32[]{:S(2)}, u32[]{:S(2)}) %collective-permute-start.7) | collective-permute-done | bytes 32800 | tf_op jit(solution)/shard_map/ppermute | solution.py:225
  19.2 1.5 %collective-permute-done.6 = f32[16,512]{1,0:T(8,128)S(1)} collective-permute-done((f32[16,512]{1,0:T(8,128)S(1)}, f32[16,512]{1,0:T(8,128)S(1)}, u32[]{:S(2)}, u32[]{:S(2)}) %collective-permute-start.6) | collective-permute-done | bytes 32800 | tf_op jit(solution)/shard_map/ppermute | solution.py:225
  21.3 0.7 %collective-permute-done.9.source_ref = bf16[16,512]{1,0:T(8,128)(2,1)S(1)} collective-permute-done((bf16[16,512]{1,0:T(8,128)(2,1)S(1)}, bf16[16,512]{1,0:T(8,128)(2,1)S(1)}, u32[]{:S(2)}, u32[]{:S(2)}) %collective-permute-start.9) | collective-permute-done | bytes 16416 | tf_op jit(solution)/shard_map/ppermute | solution.py:225
  22.0 1.7 %collective-permute-start.10 = (bf16[16,1024]{1,0:T(8,128)(2,1)S(1)}, bf16[16,1024]{1,0:T(8,128)(2,1)S(1)}, u32[]{:S(2)}, u32[]{:S(2)}) collective-permute-start(bf16[16,1024]{1,0:T(8,128)(2,1)S(1)} %pad_maximum_fusion), channel_id=1, source_target_pairs={{0,28},{4,24},{1,20},{5,16},{2,12},{6,8},{3,4},{7,0},{9,29},{13,25... | collective-permute-start | bytes 98312 | tf_op jit(solution)/shard_map/ppermute | solution.py:225
  24.1 1.8 %collective-permute-start.13 = (bf16[16,1024]{1,0:T(8,128)(2,1)S(1)}, bf16[16,1024]{1,0:T(8,128)(2,1)S(1)}, u32[]{:S(2)}, u32[]{:S(2)}) collective-permute-start(bf16[16,1024]{1,0:T(8,128)(2,1)S(1)} %shard_map.79.refs_0_), channel_id=1, source_target_pairs={{0,28},{4,24},{1,29},{5,25},{2,30},{6,26},{3,31},{7,27},{8,20},{12... | collective-permute-start | bytes 98312 | tf_op jit(solution)/shard_map/ppermute | solution.py:225
  26.0 2.2 %collective-permute-start.11 = (bf16[16,1024]{1,0:T(8,128)(2,1)S(1)}, bf16[16,1024]{1,0:T(8,128)(2,1)S(1)}, u32[]{:S(2)}, u32[]{:S(2)}) collective-permute-start(bf16[16,1024]{1,0:T(8,128)(2,1)S(1)} %shard_map.79.refs_0_), channel_id=1, source_target_pairs={{0,12},{4,8},{1,13},{5,9},{2,14},{6,10},{3,15},{7,11},{8,4},{12,0}... | collective-permute-start | bytes 98312 | tf_op jit(solution)/shard_map/ppermute | solution.py:225
  28.6 0.7 %collective-permute-done.13.refs_3_ = bf16[16,1024]{1,0:T(8,128)(2,1)S(1)} collective-permute-done((bf16[16,1024]{1,0:T(8,128)(2,1)S(1)}, bf16[16,1024]{1,0:T(8,128)(2,1)S(1)}, u32[]{:S(2)}, u32[]{:S(2)}) %collective-permute-start.13) | collective-permute-done | bytes 32800 | tf_op jit(solution)/shard_map/ppermute | solution.py:225
  29.3 1.8 %collective-permute-done.12.refs_2_ = bf16[16,1024]{1,0:T(8,128)(2,1)S(1)} collective-permute-done((bf16[16,1024]{1,0:T(8,128)(2,1)S(1)}, bf16[16,1024]{1,0:T(8,128)(2,1)S(1)}, u32[]{:S(2)}, u32[]{:S(2)}) %collective-permute-start.12) | collective-permute-done | bytes 32800 | tf_op jit(solution)/shard_map/ppermute | solution.py:225
  31.5 0.6 %collective-permute-start.17 = (f32[16,640]{1,0:T(8,128)S(1)}, f32[16,640]{1,0:T(8,128)S(1)}, u32[]{:S(2)}, u32[]{:S(2)}) collective-permute-start(f32[16,640]{1,0:T(8,128)S(1)} %shard_map.80), channel_id=1, source_target_pairs={{0,7},{4,3},{1,6},{5,2},{2,5},{6,1},{3,4},{7,0},{8,15},{12,11},{9,... | collective-permute-start | bytes 122888 | tf_op jit(solution)/shard_map/ppermute | solution.py:225
  32.0 0.6 %collective-permute-start.16 = (f32[16,640]{1,0:T(8,128)S(1)}, f32[16,640]{1,0:T(8,128)S(1)}, u32[]{:S(2)}, u32[]{:S(2)}) collective-permute-start(f32[16,640]{1,0:T(8,128)S(1)} %shard_map.80), channel_id=1, source_target_pairs={{0,6},{4,2},{1,7},{5,3},{2,4},{6,0},{3,5},{7,1},{8,14},{12,10},{9,... | collective-permute-start | bytes 122888 | tf_op jit(solution)/shard_map/ppermute | solution.py:225
  32.6 1.8 %collective-permute-start.15 = (f32[16,640]{1,0:T(8,128)S(1)}, f32[16,640]{1,0:T(8,128)S(1)}, u32[]{:S(2)}, u32[]{:S(2)}) collective-permute-start(f32[16,640]{1,0:T(8,128)S(1)} %shard_map.80), channel_id=1, source_target_pairs={{0,5},{4,1},{1,4},{5,0},{2,7},{6,3},{3,6},{7,2},{8,13},{12,9},{9,1... | collective-permute-start | bytes 122888 | tf_op jit(solution)/shard_map/ppermute | solution.py:225
  34.8 1.2 %collective-permute-done.17 = f32[16,640]{1,0:T(8,128)S(1)} collective-permute-done((f32[16,640]{1,0:T(8,128)S(1)}, f32[16,640]{1,0:T(8,128)S(1)}, u32[]{:S(2)}, u32[]{:S(2)}) %collective-permute-start.17) | collective-permute-done | bytes 40992 | tf_op jit(solution)/shard_map/ppermute | solution.py:225
  36.1 0.7 %shard_map.81 = (bf16[16,512]{1,0:T(8,128)(2,1)}, f32[32,32]{1,0:T(8,128)}, f32[32,32]{1,0:T(8,128)}) custom-call(f32[16,640]{1,0:T(8,128)S(1)} %add_add_fusion.total_ref), custom_call_target="tpu_custom_call" | custom-call | tf_op jit(solution)/shard_map/pallas_call | solution.py:344
  (36 shorter events, 3.1 us)
Async XLA Ops:
  0.6 7.3 %copy-start = (bf16[1,1,12,128,128]{4,3,2,1,0:T(8,128)(2,1)S(1)}, bf16[1,1,12,128,128]{4,3,2,1,0:T(8,128)(2,1)}, u32[]{:S(2)}) copy-start(bf16[1,1,12,128,128]{4,3,2,1,0:T(8,128)(2,1)} %param.5) | copy-start | bytes 1179652
  0.6 5.5 %collective-permute-start.3 = (bf16[12,128,128]{2,1,0:T(8,128)(2,1)}, bf16[12,128,128]{2,1,0:T(8,128)(2,1)S(1)}, u32[]{:S(2)}, u32[]{:S(2)}) collective-permute-start(bf16[12,128,128]{2,1,0:T(8,128)(2,1)} %bitcast.3), channel_id=1, source_target_pairs={{0,4},{4,0},{1,5},{5,1},{2,6},{6,2},{3,7},{7,3},{8,12},{12,8},{9,1... | collective-permute-start | bytes 1179656 | tf_op jit(solution)/shard_map/ppermute | solution.py:225
  1.2 6.8 %collective-permute-start = (bf16[16,1024]{1,0:T(8,128)(2,1)}, bf16[16,1024]{1,0:T(8,128)(2,1)S(1)}, u32[]{:S(2)}, u32[]{:S(2)}) collective-permute-start(bf16[16,1024]{1,0:T(8,128)(2,1)} %start_ref.1), channel_id=1, source_target_pairs={{24,4},{28,0},{16,5},{20,1},{8,6},{12,2},{0,7},{4,3},{25,13},{29,9... | collective-permute-start | bytes 98312 | tf_op jit(solution)/shard_map/ppermute | solution.py:225
  4.7 1.5 %collective-permute-start.1 = (s32[1,12]{1,0:T(1,128)}, s32[1,12]{1,0:T(1,128)S(1)}, u32[]{:S(2)}, u32[]{:S(2)}) collective-permute-start(s32[1,12]{1,0:T(1,128)} %bitcast.6), channel_id=1, source_target_pairs={{0,4},{4,0},{1,5},{5,1},{2,6},{6,2},{3,7},{7,3},{8,12},{12,8},{9,1... | collective-permute-start | bytes 152 | tf_op jit(solution)/shard_map/ppermute | solution.py:225
  4.8 1.4 %collective-permute-start.2 = (s32[1,4]{1,0:T(1,128)}, s32[1,4]{1,0:T(1,128)S(1)}, u32[]{:S(2)}, u32[]{:S(2)}) collective-permute-start(s32[1,4]{1,0:T(1,128)} %bitcast.9), channel_id=1, source_target_pairs={{0,4},{4,0},{1,5},{5,1},{2,6},{6,2},{3,7},{7,3},{8,12},{12,8},{9,1... | collective-permute-start | bytes 56 | tf_op jit(solution)/shard_map/ppermute | solution.py:225
  6.2 0.8 %copy-start.2 = (bf16[16,1024]{1,0:T(8,128)(2,1)S(1)}, bf16[16,1024]{1,0:T(8,128)(2,1)}, u32[]{:S(2)}) copy-start(bf16[16,1024]{1,0:T(8,128)(2,1)} %start_ref.1) | copy-start | bytes 98308
  6.9 1.0 %copy-start.4 = (s32[1,1,12]{2,1,0:T(1,128)S(1)}, s32[1,1,12]{2,1,0:T(1,128)}, u32[]{:S(2)}) copy-start(s32[1,1,12]{2,1,0:T(1,128)} %param.6) | copy-start | bytes 148
  7.0 1.0 %copy-start.5 = (s32[1,1,4]{2,1,0:T(1,128)S(1)}, s32[1,1,4]{2,1,0:T(1,128)}, u32[]{:S(2)}) copy-start(s32[1,1,4]{2,1,0:T(1,128)} %param.7) | copy-start | bytes 52
  8.4 5.4 %collective-permute-start.4 = (f32[16,512]{1,0:T(8,128)S(1)}, f32[16,512]{1,0:T(8,128)S(1)}, u32[]{:S(2)}, u32[]{:S(2)}) collective-permute-start(f32[16,512]{1,0:T(8,128)S(1)} %shard_map.76), channel_id=1, source_target_pairs={{24,4},{28,0},{16,5},{20,1},{8,6},{12,2},{0,7},{4,3},{25,13},{29,9... | collective-permute-start | bytes 98312 | tf_op jit(solution)/shard_map/ppermute | solution.py:225
  13.8 4.3 %collective-permute-start.8 = (f32[16,512]{1,0:T(8,128)S(1)}, f32[16,512]{1,0:T(8,128)S(1)}, u32[]{:S(2)}, u32[]{:S(2)}) collective-permute-start(f32[16,512]{1,0:T(8,128)S(1)} %add.25), channel_id=1, source_target_pairs={{0,7},{4,3},{1,6},{5,2},{2,5},{6,1},{3,4},{7,0},{8,15},{12,11},{9,... | collective-permute-start | bytes 98312 | tf_op jit(solution)/shard_map/ppermute | solution.py:225
  15.9 3.3 %collective-permute-start.7 = (f32[16,512]{1,0:T(8,128)S(1)}, f32[16,512]{1,0:T(8,128)S(1)}, u32[]{:S(2)}, u32[]{:S(2)}) collective-permute-start(f32[16,512]{1,0:T(8,128)S(1)} %add.25), channel_id=1, source_target_pairs={{0,6},{4,2},{1,7},{5,3},{2,4},{6,0},{3,5},{7,1},{8,14},{12,10},{9,... | collective-permute-start | bytes 98312 | tf_op jit(solution)/shard_map/ppermute | solution.py:225
  17.3 3.5 %collective-permute-start.6 = (f32[16,512]{1,0:T(8,128)S(1)}, f32[16,512]{1,0:T(8,128)S(1)}, u32[]{:S(2)}, u32[]{:S(2)}) collective-permute-start(f32[16,512]{1,0:T(8,128)S(1)} %add.25), channel_id=1, source_target_pairs={{0,5},{4,1},{1,4},{5,0},{2,7},{6,3},{3,6},{7,2},{8,13},{12,9},{9,1... | collective-permute-start | bytes 98312 | tf_op jit(solution)/shard_map/ppermute | solution.py:225
  17.3 3.5 %collective-permute-start.5 = (f32[16,512]{1,0:T(8,128)S(1)}, f32[16,512]{1,0:T(8,128)S(1)}, u32[]{:S(2)}, u32[]{:S(2)}) collective-permute-start(f32[16,512]{1,0:T(8,128)S(1)} %add.25), channel_id=1, source_target_pairs={{0,4},{4,0},{1,5},{5,1},{2,6},{6,2},{3,7},{7,3},{8,12},{12,8},{9,1... | collective-permute-start | bytes 98312 | tf_op jit(solution)/shard_map/ppermute | solution.py:225
  20.8 1.3 %copy-start.1 = (bf16[16,512]{1,0:T(8,128)(2,1)}, bf16[16,512]{1,0:T(8,128)(2,1)S(1)}, u32[]{:S(2)}) copy-start(bf16[16,512]{1,0:T(8,128)(2,1)S(1)} %add_convert_fusion.source_ref) | copy-start | bytes 49156
  20.8 1.2 %collective-permute-start.9 = (bf16[16,512]{1,0:T(8,128)(2,1)S(1)}, bf16[16,512]{1,0:T(8,128)(2,1)S(1)}, u32[]{:S(2)}, u32[]{:S(2)}) collective-permute-start(bf16[16,512]{1,0:T(8,128)(2,1)S(1)} %add_convert_fusion.source_ref), channel_id=1, source_target_pairs={{0,4},{4,0},{1,5},{5,1},{2,6},{6,2},{3,7},{7,3},{8,12},{12,8},{9,1... | collective-permute-start | bytes 49160 | tf_op jit(solution)/shard_map/ppermute | solution.py:225
  22.0 6.2 %collective-permute-start.10 = (bf16[16,1024]{1,0:T(8,128)(2,1)S(1)}, bf16[16,1024]{1,0:T(8,128)(2,1)S(1)}, u32[]{:S(2)}, u32[]{:S(2)}) collective-permute-start(bf16[16,1024]{1,0:T(8,128)(2,1)S(1)} %pad_maximum_fusion), channel_id=1, source_target_pairs={{0,28},{4,24},{1,20},{5,16},{2,12},{6,8},{3,4},{7,0},{9,29},{13,25... | collective-permute-start | bytes 98312 | tf_op jit(solution)/shard_map/ppermute | solution.py:225
  24.1 7.0 %copy-start.3 = (bf16[16,1024]{1,0:T(8,128)(2,1)S(1)}, bf16[16,1024]{1,0:T(8,128)(2,1)}, u32[]{:S(2)}) copy-start(bf16[16,1024]{1,0:T(8,128)(2,1)} %start_ref.1) | copy-start | bytes 98308
  24.1 5.2 %collective-permute-start.13 = (bf16[16,1024]{1,0:T(8,128)(2,1)S(1)}, bf16[16,1024]{1,0:T(8,128)(2,1)S(1)}, u32[]{:S(2)}, u32[]{:S(2)}) collective-permute-start(bf16[16,1024]{1,0:T(8,128)(2,1)S(1)} %shard_map.79.refs_0_), channel_id=1, source_target_pairs={{0,28},{4,24},{1,29},{5,25},{2,30},{6,26},{3,31},{7,27},{8,20},{12... | collective-permute-start | bytes 98312 | tf_op jit(solution)/shard_map/ppermute | solution.py:225
  25.9 5.2 %collective-permute-start.12 = (bf16[16,1024]{1,0:T(8,128)(2,1)S(1)}, bf16[16,1024]{1,0:T(8,128)(2,1)S(1)}, u32[]{:S(2)}, u32[]{:S(2)}) collective-permute-start(bf16[16,1024]{1,0:T(8,128)(2,1)S(1)} %shard_map.79.refs_0_), channel_id=1, source_target_pairs={{0,20},{4,16},{1,21},{5,17},{2,22},{6,18},{3,23},{7,19},{8,28},{12... | collective-permute-start | bytes 98312 | tf_op jit(solution)/shard_map/ppermute | solution.py:225
  26.0 5.1 %collective-permute-start.11 = (bf16[16,1024]{1,0:T(8,128)(2,1)S(1)}, bf16[16,1024]{1,0:T(8,128)(2,1)S(1)}, u32[]{:S(2)}, u32[]{:S(2)}) collective-permute-start(bf16[16,1024]{1,0:T(8,128)(2,1)S(1)} %shard_map.79.refs_0_), channel_id=1, source_target_pairs={{0,12},{4,8},{1,13},{5,9},{2,14},{6,10},{3,15},{7,11},{8,4},{12,0}... | collective-permute-start | bytes 98312 | tf_op jit(solution)/shard_map/ppermute | solution.py:225
  31.5 4.6 %collective-permute-start.17 = (f32[16,640]{1,0:T(8,128)S(1)}, f32[16,640]{1,0:T(8,128)S(1)}, u32[]{:S(2)}, u32[]{:S(2)}) collective-permute-start(f32[16,640]{1,0:T(8,128)S(1)} %shard_map.80), channel_id=1, source_target_pairs={{0,7},{4,3},{1,6},{5,2},{2,5},{6,1},{3,4},{7,0},{8,15},{12,11},{9,... | collective-permute-start | bytes 122888 | tf_op jit(solution)/shard_map/ppermute | solution.py:225
  32.0 4.0 %collective-permute-start.16 = (f32[16,640]{1,0:T(8,128)S(1)}, f32[16,640]{1,0:T(8,128)S(1)}, u32[]{:S(2)}, u32[]{:S(2)}) collective-permute-start(f32[16,640]{1,0:T(8,128)S(1)} %shard_map.80), channel_id=1, source_target_pairs={{0,6},{4,2},{1,7},{5,3},{2,4},{6,0},{3,5},{7,1},{8,14},{12,10},{9,... | collective-permute-start | bytes 122888 | tf_op jit(solution)/shard_map/ppermute | solution.py:225
  32.6 3.5 %collective-permute-start.15 = (f32[16,640]{1,0:T(8,128)S(1)}, f32[16,640]{1,0:T(8,128)S(1)}, u32[]{:S(2)}, u32[]{:S(2)}) collective-permute-start(f32[16,640]{1,0:T(8,128)S(1)} %shard_map.80), channel_id=1, source_target_pairs={{0,5},{4,1},{1,4},{5,0},{2,7},{6,3},{3,6},{7,2},{8,13},{12,9},{9,1... | collective-permute-start | bytes 122888 | tf_op jit(solution)/shard_map/ppermute | solution.py:225
  34.4 1.7 %collective-permute-start.14 = (f32[16,640]{1,0:T(8,128)S(1)}, f32[16,640]{1,0:T(8,128)S(1)}, u32[]{:S(2)}, u32[]{:S(2)}) collective-permute-start(f32[16,640]{1,0:T(8,128)S(1)} %shard_map.80), channel_id=1, source_target_pairs={{0,4},{4,0},{1,5},{5,1},{2,6},{6,2},{3,7},{7,3},{8,12},{12,8},{9,1... | collective-permute-start | bytes 122888 | tf_op jit(solution)/shard_map/ppermute | solution.py:225

commit v8 on v7

--- a/solution.py
+++ b/solution.py
@@ -255,7 +255,7 @@
             terms = {0: value}
             for step in range(1, col_count):
                 terms[step] = send(value, [((a, c), (a ^ step, c)) for a, c in chips])
-            return [terms[step] for step in range(col_count)]
+            return [terms[step] for step in sorted(terms, key=lambda step: (step & 1, step))]
         rest, terms = lax.psum(value, "row") * (1.0 / ratio), []
         for _ in range(3):
             terms.append(rest.astype(jnp.bfloat16))

time: 37.1 us -> 37.3 us (level)
  transfers between devices with their start and end apart: 18 -> 18, of which waited for: 11 -> 12; matrix products, arithmetic and copies ran while one was open for 0% -> 0% of each run, Pallas kernels for 4% -> 4%
where the time goes in v8:
time: 37.3 us; the launch traced here: 37.1 us
  starting transfers between devices  20.8 us (56%)
  waiting for transfers between devices  11.8 us (32%)
  Pallas kernels  2.89 us (8%)
  local copies, waits for them, and re-layouts  0.78 us (2%)
  between operations  0.71 us (2%)
    ppermute x18, starting transfers between devices, send(): lax.ppermute(value, both, [(device(*source, member), device(*target, memb...  20.8 us
    ppermute x18, waiting for transfers between devices, send(): lax.ppermute(value, both, [(device(*source, member), device(*target, memb...  11.8 us
    pallas_call x2, Pallas kernels, forward_of(): call(forward_kernel, part_shape, [table] * 2 + [vmem] * 2, [pieces, pltpu...  0.8 us
    unnamed x12, local copies, waits for them, and re-layouts  0.78 us
  transfers between devices with their start and end apart: 18, of which 12 were waited for; matrix products, arithmetic and copies ran while one was open for 0% of the time, Pallas kernels for 4%

profile of v8, /device:TPU:0, one launch (start us, length us, event | category | flops | bytes accessed | tf_op | source)
XLA Modules:
  0.0 37.1 jit_solution(14751989663154825464)
XLA Ops:
  0.6 0.5 %collective-permute-start.3 = (bf16[12,128,128]{2,1,0:T(8,128)(2,1)}, bf16[12,128,128]{2,1,0:T(8,128)(2,1)S(1)}, u32[]{:S(2)}, u32[]{:S(2)}) collective-permute-start(bf16[12,128,128]{2,1,0:T(8,128)(2,1)} %bitcast.3), channel_id=1, source_target_pairs={{0,4},{4,0},{1,5},{5,1},{2,6},{6,2},{3,7},{7,3},{8,12},{12,8},{9,1... | collective-permute-start | bytes 1179656 | tf_op jit(solution)/shard_map/ppermute | solution.py:225
  1.2 3.6 %collective-permute-start = (bf16[16,1024]{1,0:T(8,128)(2,1)}, bf16[16,1024]{1,0:T(8,128)(2,1)S(1)}, u32[]{:S(2)}, u32[]{:S(2)}) collective-permute-start(bf16[16,1024]{1,0:T(8,128)(2,1)} %start_ref.1), channel_id=1, source_target_pairs={{24,4},{28,0},{16,5},{20,1},{8,6},{12,2},{0,7},{4,3},{25,13},{29,9... | collective-permute-start | bytes 98312 | tf_op jit(solution)/shard_map/ppermute | solution.py:225
  5.2 1.0 %collective-permute-done.2.counts_ref.refs_3_ = s32[1,4]{1,0:T(1,128)S(1)} collective-permute-done((s32[1,4]{1,0:T(1,128)}, s32[1,4]{1,0:T(1,128)S(1)}, u32[]{:S(2)}, u32[]{:S(2)}) %collective-permute-start.2) | collective-permute-done | bytes 48 | tf_op jit(solution)/shard_map/ppermute | solution.py:225
  6.2 0.8 %copy-done.2 = bf16[16,1024]{1,0:T(8,128)(2,1)S(1)} copy-done((bf16[16,1024]{1,0:T(8,128)(2,1)S(1)}, bf16[16,1024]{1,0:T(8,128)(2,1)}, u32[]{:S(2)}) %copy-start.2) | copy-done | bytes 32792
  7.4 0.6 %collective-permute-done.refs_6_ = bf16[16,1024]{1,0:T(8,128)(2,1)S(1)} collective-permute-done((bf16[16,1024]{1,0:T(8,128)(2,1)}, bf16[16,1024]{1,0:T(8,128)(2,1)S(1)}, u32[]{:S(2)}, u32[]{:S(2)}) %collective-permute-start) | collective-permute-done | bytes 32800 | tf_op jit(solution)/shard_map/ppermute | solution.py:225
  8.4 3.2 %collective-permute-start.4 = (f32[16,512]{1,0:T(8,128)S(1)}, f32[16,512]{1,0:T(8,128)S(1)}, u32[]{:S(2)}, u32[]{:S(2)}) collective-permute-start(f32[16,512]{1,0:T(8,128)S(1)} %shard_map.76), channel_id=1, source_target_pairs={{24,4},{28,0},{16,5},{20,1},{8,6},{12,2},{0,7},{4,3},{25,13},{29,9... | collective-permute-start | bytes 98312 | tf_op jit(solution)/shard_map/ppermute | solution.py:225
  11.6 2.2 %collective-permute-done.4 = f32[16,512]{1,0:T(8,128)S(1)} collective-permute-done((f32[16,512]{1,0:T(8,128)S(1)}, f32[16,512]{1,0:T(8,128)S(1)}, u32[]{:S(2)}, u32[]{:S(2)}) %collective-permute-start.4) | collective-permute-done | bytes 32800 | tf_op jit(solution)/shard_map/ppermute | solution.py:225
  13.8 2.0 %collective-permute-start.8 = (f32[16,512]{1,0:T(8,128)S(1)}, f32[16,512]{1,0:T(8,128)S(1)}, u32[]{:S(2)}, u32[]{:S(2)}) collective-permute-start(f32[16,512]{1,0:T(8,128)S(1)} %add.25), channel_id=1, source_target_pairs={{0,7},{4,3},{1,6},{5,2},{2,5},{6,1},{3,4},{7,0},{8,15},{12,11},{9,... | collective-permute-start | bytes 98312 | tf_op jit(solution)/shard_map/ppermute | solution.py:225
  15.9 1.4 %collective-permute-start.7 = (f32[16,512]{1,0:T(8,128)S(1)}, f32[16,512]{1,0:T(8,128)S(1)}, u32[]{:S(2)}, u32[]{:S(2)}) collective-permute-start(f32[16,512]{1,0:T(8,128)S(1)} %add.25), channel_id=1, source_target_pairs={{0,6},{4,2},{1,7},{5,3},{2,4},{6,0},{3,5},{7,1},{8,14},{12,10},{9,... | collective-permute-start | bytes 98312 | tf_op jit(solution)/shard_map/ppermute | solution.py:225
  17.4 0.8 %collective-permute-done.8 = f32[16,512]{1,0:T(8,128)S(1)} collective-permute-done((f32[16,512]{1,0:T(8,128)S(1)}, f32[16,512]{1,0:T(8,128)S(1)}, u32[]{:S(2)}, u32[]{:S(2)}) %collective-permute-start.8) | collective-permute-done | bytes 32800 | tf_op jit(solution)/shard_map/ppermute | solution.py:225
  18.1 1.1 %collective-permute-done.7 = f32[16,512]{1,0:T(8,128)S(1)} collective-permute-done((f32[16,512]{1,0:T(8,128)S(1)}, f32[16,512]{1,0:T(8,128)S(1)}, u32[]{:S(2)}, u32[]{:S(2)}) %collective-permute-start.7) | collective-permute-done | bytes 32800 | tf_op jit(solution)/shard_map/ppermute | solution.py:225
  19.2 1.5 %collective-permute-done.6 = f32[16,512]{1,0:T(8,128)S(1)} collective-permute-done((f32[16,512]{1,0:T(8,128)S(1)}, f32[16,512]{1,0:T(8,128)S(1)}, u32[]{:S(2)}, u32[]{:S(2)}) %collective-permute-start.6) | collective-permute-done | bytes 32800 | tf_op jit(solution)/shard_map/ppermute | solution.py:225
  21.3 0.7 %collective-permute-done.9.source_ref = bf16[16,512]{1,0:T(8,128)(2,1)S(1)} collective-permute-done((bf16[16,512]{1,0:T(8,128)(2,1)S(1)}, bf16[16,512]{1,0:T(8,128)(2,1)S(1)}, u32[]{:S(2)}, u32[]{:S(2)}) %collective-permute-start.9) | collective-permute-done | bytes 16416 | tf_op jit(solution)/shard_map/ppermute | solution.py:225
  22.0 1.9 %collective-permute-start.10 = (bf16[16,1024]{1,0:T(8,128)(2,1)S(1)}, bf16[16,1024]{1,0:T(8,128)(2,1)S(1)}, u32[]{:S(2)}, u32[]{:S(2)}) collective-permute-start(bf16[16,1024]{1,0:T(8,128)(2,1)S(1)} %pad_maximum_fusion), channel_id=1, source_target_pairs={{0,28},{4,24},{1,20},{5,16},{2,12},{6,8},{3,4},{7,0},{9,29},{13,25... | collective-permute-start | bytes 98312 | tf_op jit(solution)/shard_map/ppermute | solution.py:225
  24.3 1.7 %collective-permute-start.13 = (bf16[16,1024]{1,0:T(8,128)(2,1)S(1)}, bf16[16,1024]{1,0:T(8,128)(2,1)S(1)}, u32[]{:S(2)}, u32[]{:S(2)}) collective-permute-start(bf16[16,1024]{1,0:T(8,128)(2,1)S(1)} %shard_map.79.refs_0_), channel_id=1, source_target_pairs={{0,28},{4,24},{1,29},{5,25},{2,30},{6,26},{3,31},{7,27},{8,20},{12... | collective-permute-start | bytes 98312 | tf_op jit(solution)/shard_map/ppermute | solution.py:225
  25.9 0.6 %collective-permute-start.12 = (bf16[16,1024]{1,0:T(8,128)(2,1)S(1)}, bf16[16,1024]{1,0:T(8,128)(2,1)S(1)}, u32[]{:S(2)}, u32[]{:S(2)}) collective-permute-start(bf16[16,1024]{1,0:T(8,128)(2,1)S(1)} %shard_map.79.refs_0_), channel_id=1, source_target_pairs={{0,12},{4,8},{1,13},{5,9},{2,14},{6,10},{3,15},{7,11},{8,4},{12,0}... | collective-permute-start | bytes 98312 | tf_op jit(solution)/shard_map/ppermute | solution.py:225
  26.5 1.9 %collective-permute-start.11 = (bf16[16,1024]{1,0:T(8,128)(2,1)S(1)}, bf16[16,1024]{1,0:T(8,128)(2,1)S(1)}, u32[]{:S(2)}, u32[]{:S(2)}) collective-permute-start(bf16[16,1024]{1,0:T(8,128)(2,1)S(1)} %shard_map.79.refs_0_), channel_id=1, source_target_pairs={{0,20},{4,16},{1,21},{5,17},{2,22},{6,18},{3,23},{7,19},{8,28},{12... | collective-permute-start | bytes 98312 | tf_op jit(solution)/shard_map/ppermute | solution.py:225
  28.8 0.8 %collective-permute-done.13.refs_3_ = bf16[16,1024]{1,0:T(8,128)(2,1)S(1)} collective-permute-done((bf16[16,1024]{1,0:T(8,128)(2,1)S(1)}, bf16[16,1024]{1,0:T(8,128)(2,1)S(1)}, u32[]{:S(2)}, u32[]{:S(2)}) %collective-permute-start.13) | collective-permute-done | bytes 32800 | tf_op jit(solution)/shard_map/ppermute | solution.py:225
  29.8 1.0 %collective-permute-done.11.refs_1_ = bf16[16,1024]{1,0:T(8,128)(2,1)S(1)} collective-permute-done((bf16[16,1024]{1,0:T(8,128)(2,1)S(1)}, bf16[16,1024]{1,0:T(8,128)(2,1)S(1)}, u32[]{:S(2)}, u32[]{:S(2)}) %collective-permute-start.11) | collective-permute-done | bytes 32800 | tf_op jit(solution)/shard_map/ppermute | solution.py:225
  31.1 0.8 %collective-permute-start.17 = (f32[16,640]{1,0:T(8,128)S(1)}, f32[16,640]{1,0:T(8,128)S(1)}, u32[]{:S(2)}, u32[]{:S(2)}) collective-permute-start(f32[16,640]{1,0:T(8,128)S(1)} %shard_map.80), channel_id=1, source_target_pairs={{0,7},{4,3},{1,6},{5,2},{2,5},{6,1},{3,4},{7,0},{8,15},{12,11},{9,... | collective-permute-start | bytes 122888 | tf_op jit(solution)/shard_map/ppermute | solution.py:225
  31.9 2.2 %collective-permute-start.15 = (f32[16,640]{1,0:T(8,128)S(1)}, f32[16,640]{1,0:T(8,128)S(1)}, u32[]{:S(2)}, u32[]{:S(2)}) collective-permute-start(f32[16,640]{1,0:T(8,128)S(1)} %shard_map.80), channel_id=1, source_target_pairs={{0,5},{4,1},{1,4},{5,0},{2,7},{6,3},{3,6},{7,2},{8,13},{12,9},{9,1... | collective-permute-start | bytes 122888 | tf_op jit(solution)/shard_map/ppermute | solution.py:225
  34.4 1.3 %collective-permute-done.17 = f32[16,640]{1,0:T(8,128)S(1)} collective-permute-done((f32[16,640]{1,0:T(8,128)S(1)}, f32[16,640]{1,0:T(8,128)S(1)}, u32[]{:S(2)}, u32[]{:S(2)}) %collective-permute-start.17) | collective-permute-done | bytes 40992 | tf_op jit(solution)/shard_map/ppermute | solution.py:225
  35.7 0.7 %collective-permute-done.16 = f32[16,640]{1,0:T(8,128)S(1)} collective-permute-done((f32[16,640]{1,0:T(8,128)S(1)}, f32[16,640]{1,0:T(8,128)S(1)}, u32[]{:S(2)}, u32[]{:S(2)}) %collective-permute-start.16) | collective-permute-done | bytes 40992 | tf_op jit(solution)/shard_map/ppermute | solution.py:225
  36.4 0.7 %shard_map.81 = (bf16[16,512]{1,0:T(8,128)(2,1)}, f32[32,32]{1,0:T(8,128)}, f32[32,32]{1,0:T(8,128)}) custom-call(f32[16,640]{1,0:T(8,128)S(1)} %add_add_fusion.total_ref), custom_call_target="tpu_custom_call" | custom-call | tf_op jit(solution)/shard_map/pallas_call | solution.py:344
  (36 shorter events, 3.7 us)
Async XLA Ops:
  0.6 7.3 %copy-start = (bf16[1,1,12,128,128]{4,3,2,1,0:T(8,128)(2,1)S(1)}, bf16[1,1,12,128,128]{4,3,2,1,0:T(8,128)(2,1)}, u32[]{:S(2)}) copy-start(bf16[1,1,12,128,128]{4,3,2,1,0:T(8,128)(2,1)} %param.5) | copy-start | bytes 1179652
  0.6 5.5 %collective-permute-start.3 = (bf16[12,128,128]{2,1,0:T(8,128)(2,1)}, bf16[12,128,128]{2,1,0:T(8,128)(2,1)S(1)}, u32[]{:S(2)}, u32[]{:S(2)}) collective-permute-start(bf16[12,128,128]{2,1,0:T(8,128)(2,1)} %bitcast.3), channel_id=1, source_target_pairs={{0,4},{4,0},{1,5},{5,1},{2,6},{6,2},{3,7},{7,3},{8,12},{12,8},{9,1... | collective-permute-start | bytes 1179656 | tf_op jit(solution)/shard_map/ppermute | solution.py:225
  1.2 6.8 %collective-permute-start = (bf16[16,1024]{1,0:T(8,128)(2,1)}, bf16[16,1024]{1,0:T(8,128)(2,1)S(1)}, u32[]{:S(2)}, u32[]{:S(2)}) collective-permute-start(bf16[16,1024]{1,0:T(8,128)(2,1)} %start_ref.1), channel_id=1, source_target_pairs={{24,4},{28,0},{16,5},{20,1},{8,6},{12,2},{0,7},{4,3},{25,13},{29,9... | collective-permute-start | bytes 98312 | tf_op jit(solution)/shard_map/ppermute | solution.py:225
  4.7 1.5 %collective-permute-start.1 = (s32[1,12]{1,0:T(1,128)}, s32[1,12]{1,0:T(1,128)S(1)}, u32[]{:S(2)}, u32[]{:S(2)}) collective-permute-start(s32[1,12]{1,0:T(1,128)} %bitcast.6), channel_id=1, source_target_pairs={{0,4},{4,0},{1,5},{5,1},{2,6},{6,2},{3,7},{7,3},{8,12},{12,8},{9,1... | collective-permute-start | bytes 152 | tf_op jit(solution)/shard_map/ppermute | solution.py:225
  4.8 1.4 %collective-permute-start.2 = (s32[1,4]{1,0:T(1,128)}, s32[1,4]{1,0:T(1,128)S(1)}, u32[]{:S(2)}, u32[]{:S(2)}) collective-permute-start(s32[1,4]{1,0:T(1,128)} %bitcast.9), channel_id=1, source_target_pairs={{0,4},{4,0},{1,5},{5,1},{2,6},{6,2},{3,7},{7,3},{8,12},{12,8},{9,1... | collective-permute-start | bytes 56 | tf_op jit(solution)/shard_map/ppermute | solution.py:225
  6.2 0.8 %copy-start.2 = (bf16[16,1024]{1,0:T(8,128)(2,1)S(1)}, bf16[16,1024]{1,0:T(8,128)(2,1)}, u32[]{:S(2)}) copy-start(bf16[16,1024]{1,0:T(8,128)(2,1)} %start_ref.1) | copy-start | bytes 98308
  6.9 1.0 %copy-start.4 = (s32[1,1,12]{2,1,0:T(1,128)S(1)}, s32[1,1,12]{2,1,0:T(1,128)}, u32[]{:S(2)}) copy-start(s32[1,1,12]{2,1,0:T(1,128)} %param.6) | copy-start | bytes 148
  7.0 1.0 %copy-start.5 = (s32[1,1,4]{2,1,0:T(1,128)S(1)}, s32[1,1,4]{2,1,0:T(1,128)}, u32[]{:S(2)}) copy-start(s32[1,1,4]{2,1,0:T(1,128)} %param.7) | copy-start | bytes 52
  8.4 5.4 %collective-permute-start.4 = (f32[16,512]{1,0:T(8,128)S(1)}, f32[16,512]{1,0:T(8,128)S(1)}, u32[]{:S(2)}, u32[]{:S(2)}) collective-permute-start(f32[16,512]{1,0:T(8,128)S(1)} %shard_map.76), channel_id=1, source_target_pairs={{24,4},{28,0},{16,5},{20,1},{8,6},{12,2},{0,7},{4,3},{25,13},{29,9... | collective-permute-start | bytes 98312 | tf_op jit(solution)/shard_map/ppermute | solution.py:225
  13.8 4.3 %collective-permute-start.8 = (f32[16,512]{1,0:T(8,128)S(1)}, f32[16,512]{1,0:T(8,128)S(1)}, u32[]{:S(2)}, u32[]{:S(2)}) collective-permute-start(f32[16,512]{1,0:T(8,128)S(1)} %add.25), channel_id=1, source_target_pairs={{0,7},{4,3},{1,6},{5,2},{2,5},{6,1},{3,4},{7,0},{8,15},{12,11},{9,... | collective-permute-start | bytes 98312 | tf_op jit(solution)/shard_map/ppermute | solution.py:225
  15.9 3.3 %collective-permute-start.7 = (f32[16,512]{1,0:T(8,128)S(1)}, f32[16,512]{1,0:T(8,128)S(1)}, u32[]{:S(2)}, u32[]{:S(2)}) collective-permute-start(f32[16,512]{1,0:T(8,128)S(1)} %add.25), channel_id=1, source_target_pairs={{0,6},{4,2},{1,7},{5,3},{2,4},{6,0},{3,5},{7,1},{8,14},{12,10},{9,... | collective-permute-start | bytes 98312 | tf_op jit(solution)/shard_map/ppermute | solution.py:225
  17.3 3.4 %collective-permute-start.6 = (f32[16,512]{1,0:T(8,128)S(1)}, f32[16,512]{1,0:T(8,128)S(1)}, u32[]{:S(2)}, u32[]{:S(2)}) collective-permute-start(f32[16,512]{1,0:T(8,128)S(1)} %add.25), channel_id=1, source_target_pairs={{0,5},{4,1},{1,4},{5,0},{2,7},{6,3},{3,6},{7,2},{8,13},{12,9},{9,1... | collective-permute-start | bytes 98312 | tf_op jit(solution)/shard_map/ppermute | solution.py:225
  17.3 3.4 %collective-permute-start.5 = (f32[16,512]{1,0:T(8,128)S(1)}, f32[16,512]{1,0:T(8,128)S(1)}, u32[]{:S(2)}, u32[]{:S(2)}) collective-permute-start(f32[16,512]{1,0:T(8,128)S(1)} %add.25), channel_id=1, source_target_pairs={{0,4},{4,0},{1,5},{5,1},{2,6},{6,2},{3,7},{7,3},{8,12},{12,8},{9,1... | collective-permute-start | bytes 98312 | tf_op jit(solution)/shard_map/ppermute | solution.py:225
  20.8 1.3 %copy-start.1 = (bf16[16,512]{1,0:T(8,128)(2,1)}, bf16[16,512]{1,0:T(8,128)(2,1)S(1)}, u32[]{:S(2)}) copy-start(bf16[16,512]{1,0:T(8,128)(2,1)S(1)} %add_convert_fusion.source_ref) | copy-start | bytes 49156
  20.8 1.2 %collective-permute-start.9 = (bf16[16,512]{1,0:T(8,128)(2,1)S(1)}, bf16[16,512]{1,0:T(8,128)(2,1)S(1)}, u32[]{:S(2)}, u32[]{:S(2)}) collective-permute-start(bf16[16,512]{1,0:T(8,128)(2,1)S(1)} %add_convert_fusion.source_ref), channel_id=1, source_target_pairs={{0,4},{4,0},{1,5},{5,1},{2,6},{6,2},{3,7},{7,3},{8,12},{12,8},{9,1... | collective-permute-start | bytes 49160 | tf_op jit(solution)/shard_map/ppermute | solution.py:225
  22.0 6.4 %collective-permute-start.10 = (bf16[16,1024]{1,0:T(8,128)(2,1)S(1)}, bf16[16,1024]{1,0:T(8,128)(2,1)S(1)}, u32[]{:S(2)}, u32[]{:S(2)}) collective-permute-start(bf16[16,1024]{1,0:T(8,128)(2,1)S(1)} %pad_maximum_fusion), channel_id=1, source_target_pairs={{0,28},{4,24},{1,20},{5,16},{2,12},{6,8},{3,4},{7,0},{9,29},{13,25... | collective-permute-start | bytes 98312 | tf_op jit(solution)/shard_map/ppermute | solution.py:225
  24.3 6.5 %copy-start.3 = (bf16[16,1024]{1,0:T(8,128)(2,1)S(1)}, bf16[16,1024]{1,0:T(8,128)(2,1)}, u32[]{:S(2)}) copy-start(bf16[16,1024]{1,0:T(8,128)(2,1)} %start_ref.1) | copy-start | bytes 98308
  24.3 5.3 %collective-permute-start.13 = (bf16[16,1024]{1,0:T(8,128)(2,1)S(1)}, bf16[16,1024]{1,0:T(8,128)(2,1)S(1)}, u32[]{:S(2)}, u32[]{:S(2)}) collective-permute-start(bf16[16,1024]{1,0:T(8,128)(2,1)S(1)} %shard_map.79.refs_0_), channel_id=1, source_target_pairs={{0,28},{4,24},{1,29},{5,25},{2,30},{6,26},{3,31},{7,27},{8,20},{12... | collective-permute-start | bytes 98312 | tf_op jit(solution)/shard_map/ppermute | solution.py:225
  25.9 3.9 %collective-permute-start.12 = (bf16[16,1024]{1,0:T(8,128)(2,1)S(1)}, bf16[16,1024]{1,0:T(8,128)(2,1)S(1)}, u32[]{:S(2)}, u32[]{:S(2)}) collective-permute-start(bf16[16,1024]{1,0:T(8,128)(2,1)S(1)} %shard_map.79.refs_0_), channel_id=1, source_target_pairs={{0,12},{4,8},{1,13},{5,9},{2,14},{6,10},{3,15},{7,11},{8,4},{12,0}... | collective-permute-start | bytes 98312 | tf_op jit(solution)/shard_map/ppermute | solution.py:225
  26.5 4.2 %collective-permute-start.11 = (bf16[16,1024]{1,0:T(8,128)(2,1)S(1)}, bf16[16,1024]{1,0:T(8,128)(2,1)S(1)}, u32[]{:S(2)}, u32[]{:S(2)}) collective-permute-start(bf16[16,1024]{1,0:T(8,128)(2,1)S(1)} %shard_map.79.refs_0_), channel_id=1, source_target_pairs={{0,20},{4,16},{1,21},{5,17},{2,22},{6,18},{3,23},{7,19},{8,28},{12... | collective-permute-start | bytes 98312 | tf_op jit(solution)/shard_map/ppermute | solution.py:225
  31.1 4.6 %collective-permute-start.17 = (f32[16,640]{1,0:T(8,128)S(1)}, f32[16,640]{1,0:T(8,128)S(1)}, u32[]{:S(2)}, u32[]{:S(2)}) collective-permute-start(f32[16,640]{1,0:T(8,128)S(1)} %shard_map.80), channel_id=1, source_target_pairs={{0,7},{4,3},{1,6},{5,2},{2,5},{6,1},{3,4},{7,0},{8,15},{12,11},{9,... | collective-permute-start | bytes 122888 | tf_op jit(solution)/shard_map/ppermute | solution.py:225
  31.9 4.5 %collective-permute-start.16 = (f32[16,640]{1,0:T(8,128)S(1)}, f32[16,640]{1,0:T(8,128)S(1)}, u32[]{:S(2)}, u32[]{:S(2)}) collective-permute-start(f32[16,640]{1,0:T(8,128)S(1)} %shard_map.80), channel_id=1, source_target_pairs={{0,6},{4,2},{1,7},{5,3},{2,4},{6,0},{3,5},{7,1},{8,14},{12,10},{9,... | collective-permute-start | bytes 122888 | tf_op jit(solution)/shard_map/ppermute | solution.py:225
  31.9 4.4 %collective-permute-start.15 = (f32[16,640]{1,0:T(8,128)S(1)}, f32[16,640]{1,0:T(8,128)S(1)}, u32[]{:S(2)}, u32[]{:S(2)}) collective-permute-start(f32[16,640]{1,0:T(8,128)S(1)} %shard_map.80), channel_id=1, source_target_pairs={{0,5},{4,1},{1,4},{5,0},{2,7},{6,3},{3,6},{7,2},{8,13},{12,9},{9,1... | collective-permute-start | bytes 122888 | tf_op jit(solution)/shard_map/ppermute | solution.py:225
  34.1 2.3 %collective-permute-start.14 = (f32[16,640]{1,0:T(8,128)S(1)}, f32[16,640]{1,0:T(8,128)S(1)}, u32[]{:S(2)}, u32[]{:S(2)}) collective-permute-start(f32[16,640]{1,0:T(8,128)S(1)} %shard_map.80), channel_id=1, source_target_pairs={{0,4},{4,0},{1,5},{5,1},{2,6},{6,2},{3,7},{7,3},{8,12},{12,8},{9,1... | collective-permute-start | bytes 122888 | tf_op jit(solution)/shard_map/ppermute | solution.py:225
